TPU v7x, 256 devices: a whole 4x4x8 slice. The times are simulated.
256 devices in a mesh: dp: 2 (over y_hi), fsdp: 16 (over x, y_lo, core), tensor: 8 (over z).
Axes of the slice: x: 4, y: 4 (y_hi: 2, y_lo: 2; y = y_hi * 2 + y_lo), z: 8, core: 2. Of those that a mesh axis runs over, the one named last changes fastest.
Arguments:
- activations: bfloat16 [4096, 8192], P(('dp', 'fsdp'), 'tensor'), may hold values from -6 to 6
- cotangent: bfloat16 [4096, 8192], P(('dp', 'fsdp'), 'tensor'), may hold values from -6 to 6
- up_tiles: bfloat16 [1024, 128, 128], P(('fsdp', 'tensor')), may hold values from -0.1875 to 0.1875
- down_tiles: bfloat16 [1024, 128, 128], P(('fsdp', 'tensor')), may hold values from -0.125 to 0.125
- up_rows: int32 [128, 8], P(None, 'tensor'), may hold values from 0 to 63, as said below
- up_cols: int32 [128, 8], P(None, 'tensor'), may hold values from 0 to 15, as said below
- down_rows: int32 [128, 8], P(None, 'tensor'), may hold values from 0 to 15, as said below
- down_cols: int32 [128, 8], P(None, 'tensor'), may hold values from 0 to 63, as said below
Outputs:
- output: bfloat16 [4096, 8192], P(('dp', 'fsdp'), 'tensor')
- input_grad: bfloat16 [4096, 8192], P(('dp', 'fsdp'), 'tensor')
- up_grad: float32 [1024, 128, 128], P(('fsdp', 'tensor'))
- down_grad: float32 [1024, 128, 128], P(('fsdp', 'tensor'))
Inputs may be any that keep to these rules, and one draw needn't show every extreme that they name: `up_rows`: within a column, the up tiles of one hidden-unit block name distinct feature blocks. `up_cols`: every value occurs exactly 8 times in each column. `down_rows`: every value occurs exactly 8 times in each column. `down_cols`: within a column, the down tiles of one hidden-unit block name distinct feature blocks.
All inputs are finite; a program needn't handle non-finite values.
Results may differ from a plain program's by a relative error of at most 0.018.
Values may be sent and summed in bfloat16 or wider, within the bound.
No kernel may reach another device: no remote copies, remote signals or barrier semaphores. Data moves between devices by JAX's collectives and lax.ppermute only.
A program may use at most 128 MiB of HBM per device.

v0:
```python
import functools

import jax
import jax.numpy as jnp
from jax import lax
from jax.experimental import pallas as pl
from jax.experimental.pallas import tpu as pltpu
from jax.sharding import PartitionSpec as P

BF = jnp.bfloat16
F32 = jnp.float32
inv_root_two = 0.7071067811865476
inv_root_tau = 0.3989422804014327

B = 128
H = 16
K = 8
NT = 128
COST = 10_000_000
UNROLL = 2
VMEM_LIMIT = 56 * 1024 * 1024

SMEM_SPEC = pl.BlockSpec(memory_space=pltpu.SMEM)
VMEM_SPEC = pl.BlockSpec(memory_space=pltpu.VMEM)
ANY_SPEC = pl.BlockSpec(memory_space=pl.ANY)


def gelu_parts(values):
    normal_cdf = 0.5 * (1.0 + lax.erf(values * inv_root_two))
    density = inv_root_tau * jnp.exp(-0.5 * values * values)
    return (values * normal_cdf, normal_cdf + values * density)


def dot(a, b, dims):
    return lax.dot_general(a, b, ((dims[:1], dims[1:]), ((), ())), preferred_element_type=F32)


def plan_kernel(cols_ref, rows_ref, up_ref, down_ref, count):
    for near, order in ((cols_ref, up_ref), (rows_ref, down_ref)):
        for h in range(H):
            count[h] = 0

        def step(j, carry):
            h = near[j]
            c = count[h]
            order[h * K + c] = j
            count[h] = c + 1
            return carry

        lax.fori_loop(0, NT, step, 0)


def plan(cols, rows):
    shape = jax.ShapeDtypeStruct((NT,), jnp.int32)
    return pl.pallas_call(
        plan_kernel,
        out_shape=(shape, shape),
        in_specs=[SMEM_SPEC] * 2,
        out_specs=(SMEM_SPEC, SMEM_SPEC),
        scratch_shapes=[pltpu.SMEM((H,), jnp.int32)],
        name="plan",
    )(cols, rows)


def block(ref, f):
    return ref[f >> 3, :, pl.ds(pl.multiple_of((f & 7) * B, B), B)]


class Wide:
    def __init__(self, arrays, places):
        self.arrays, self.places = arrays, places


def wide_copies(places, refs, pos, buf, sems, first):
    copies = []
    for n, (which, index, shift, lines) in enumerate(places):
        slot = shift if isinstance(shift, int) else (pos[0] + shift[0]) & 7
        src = refs[which].at[index] if index is not None else refs[which]
        dst = buf.at[slot] if lines is None else buf.at[slot, pl.ds(*lines)]
        copies.append(pltpu.make_async_copy(src, dst, sems.at[first + n]))
    return copies


def tile_copies(places, refs, pos, buf, sems, first):
    copies = []
    for n, (which, index, (dx, dy, dc)) in enumerate(places):
        slot = ((pos[1] - dx) & 3) * 4 + (pos[2] ^ dy) * 2 + (pos[3] ^ dc)
        src = refs[which].at[index] if index is not None else refs[which]
        copies.append(
            pltpu.make_async_copy(src, buf.at[pl.ds(slot * 8, 8)], sems.at[first + n])
        )
    return copies


WIDE = pltpu.VMEM((8, B, 8 * B), BF)
TILES = pltpu.VMEM((NT, B, B), BF)
WIDE_ACC = pltpu.VMEM((8, B, 8 * B), F32)


def call(kernel, out_shape, smem, hbm, vmem, scratch, out_specs=None, name=None):
    n_out = len(out_shape)
    return pl.pallas_call(
        kernel,
        out_shape=tuple(out_shape),
        in_specs=[SMEM_SPEC] * len(smem) + [ANY_SPEC] * len(hbm) + [VMEM_SPEC] * len(vmem),
        out_specs=out_specs or (VMEM_SPEC,) * n_out,
        scratch_shapes=scratch,
        compiler_params=pltpu.CompilerParams(vmem_limit_bytes=VMEM_LIMIT),
        cost_estimate=pl.CostEstimate(flops=COST, bytes_accessed=COST // 100, transcendentals=0),
        name=name,
    )(*smem, *hbm, *vmem)


def start(copies):
    for c in copies:
        c.start()


def finish(copies):
    for c in copies:
        c.wait()


def far_blocks(buf, rows, order, h):
    return jnp.concatenate([block(buf, rows[order[h * K + k]]) for k in range(K)], axis=1)


def add_far(acc, far, js, term):
    for k, j in enumerate(js):
        f = far[j]
        at = (f >> 3, slice(None), pl.ds(pl.multiple_of((f & 7) * B, B), B))
        acc[at] += term[:, k * B : (k + 1) * B]


def forward(up_order, rows, down_order, cols, pos, x, up, down):
    def kernel(up_order, rows, down_order, cols, pos, *refs):
        nx, nu, nd = len(x.arrays), len(up.arrays), len(down.arrays)
        x_refs, u_refs, d_refs = refs[:nx], refs[nx : nx + nu], refs[nx + nu : nx + nu + nd]
        hidden, slope, out, xbuf, ubuf, dbuf, acc, sems = refs[nx + nu + nd :]
        first = wide_copies(x.places, x_refs, pos, xbuf, sems, 0)
        first += tile_copies(up.places, u_refs, pos, ubuf, sems, len(first))
        later = tile_copies(down.places, d_refs, pos, dbuf, sems, len(first))
        start(first)
        start(later)
        acc[...] = jnp.zeros_like(acc)
        finish(first)

        def step(h, carry):
            lhs = far_blocks(xbuf, rows, up_order, h)
            rhs = jnp.concatenate([ubuf[up_order[h * K + k]] for k in range(K)], axis=0)
            act, der = gelu_parts(dot(lhs, rhs, (1, 0)))
            hidden[h] = act.astype(BF)
            slope[h] = der
            return carry

        lax.fori_loop(0, H, step, 0, unroll=UNROLL)
        finish(later)

        def spread_step(h, carry):
            js = [down_order[h * K + k] for k in range(K)]
            rhs = jnp.concatenate([dbuf[j] for j in js], axis=1)
            add_far(acc, cols, js, dot(hidden[h], rhs, (1, 0)))
            return carry

        lax.fori_loop(0, H, spread_step, 0, unroll=UNROLL)
        out[...] = acc[...].astype(BF)

    n = len(x.places) + len(up.places) + len(down.places)
    return call(
        kernel,
        (
            jax.ShapeDtypeStruct((H, B, B), BF),
            jax.ShapeDtypeStruct((H, B, B), F32),
            jax.ShapeDtypeStruct((8, B, 8 * B), BF),
        ),
        (up_order, rows, down_order, cols, pos),
        (*x.arrays, *up.arrays, *down.arrays),
        (),
        [WIDE, TILES, TILES, WIDE_ACC, pltpu.SemaphoreType.DMA((n,))],
        name="forward",
    )


def grad_shapes(x_first):
    n, m = (4, 2) if x_first else (2, 4)
    piece = jax.ShapeDtypeStruct((n // 2, m, 8, B, B), BF)
    return [piece] * 2 + [jax.ShapeDtypeStruct((n, m, 8, B, B), BF)]


def grad_scratch(x_first):
    n, m = (4, 2) if x_first else (2, 4)
    return pltpu.VMEM((2, n, m, 8, B, B), BF)


def grad_place(j, pos, x_first):
    dc, dx, dy = ((j >> 3) & 1) ^ pos[3], ((j >> 5) - pos[1]) & 3, ((j >> 4) & 1) ^ pos[2]
    return (dc, (dx + 3) & 3, dy, j & 7) if x_first else (dc, dy, dx, j & 7)


def grad_copies(grads, outs, sems, first):
    n = outs[0].shape[0]
    return [
        pltpu.make_async_copy(grads.at[1, pl.ds(0, n)], outs[0], sems.at[first]),
        pltpu.make_async_copy(grads.at[1, pl.ds(n, n)], outs[1], sems.at[first + 1]),
        pltpu.make_async_copy(grads.at[0], outs[2], sems.at[first + 2]),
    ]


def backward(down_order, cols, up_order, rows, pos, hidden, slope, cot, w, x):
    up_shapes, down_shapes = grad_shapes(False), grad_shapes(True)

    def kernel(down_order, cols, up_order, rows, pos, *refs):
        nc, nw, nx = len(cot.arrays), len(w.arrays), len(x.arrays)
        c_refs, w_refs, x_refs = refs[:nc], refs[nc : nc + nw], refs[nc + nw : nc + nw + nx]
        hidden, slope, pre = refs[nc + nw + nx : nc + nw + nx + 3]
        ups, downs = refs[nc + nw + nx + 3 : -6][:3], refs[nc + nw + nx + 3 : -6][3:]
        cbuf, wbuf, xbuf, up_terms, down_terms, sems = refs[-6:]
        first = wide_copies(cot.places, c_refs, pos, cbuf, sems, 0)
        first += tile_copies(w.places, w_refs, pos, wbuf, sems, len(first))
        later = wide_copies(x.places, x_refs, pos, xbuf, sems, len(first))
        n = len(first) + len(later)
        start(first)
        start(later)
        finish(first)

        def step(h, carry):
            lhs = far_blocks(cbuf, cols, down_order, h)
            rhs = jnp.concatenate([wbuf[down_order[h * K + k]] for k in range(K)], axis=1)
            pre[h] = (dot(lhs, rhs, (1, 1)) * slope[h]).astype(BF)
            return carry

        lax.fori_loop(0, H, step, 0, unroll=UNROLL)
        finish(later)

        def up_term(h, carry):
            lhs = far_blocks(xbuf, rows, up_order, h)
            out = dot(lhs, pre[h], (0, 0)).astype(BF)
            for k in range(K):
                at = grad_place(up_order[h * K + k], pos, False)
                up_terms[at] = out[k * B : (k + 1) * B]
            return carry

        lax.fori_loop(0, H, up_term, 0, unroll=UNROLL)
        up_copies = grad_copies(up_terms, ups, sems, n)
        start(up_copies)

        def down_term(h, carry):
            out = dot(hidden[h], far_blocks(cbuf, cols, down_order, h), (0, 0)).astype(BF)
            for k in range(K):
                at = grad_place(down_order[h * K + k], pos, True)
                down_terms[at] = out[:, k * B : (k + 1) * B]
            return carry

        lax.fori_loop(0, H, down_term, 0, unroll=UNROLL)
        down_copies = grad_copies(down_terms, downs, sems, n + 3)
        start(down_copies)
        finish(up_copies)
        finish(down_copies)

    n = len(cot.places) + len(w.places) + len(x.places) + 6
    out = call(
        kernel,
        [jax.ShapeDtypeStruct((H, B, B), BF)] + up_shapes + down_shapes,
        (down_order, cols, up_order, rows, pos),
        (*cot.arrays, *w.arrays, *x.arrays),
        (hidden, slope),
        [
            WIDE,
            TILES,
            WIDE,
            grad_scratch(False),
            grad_scratch(True),
            pltpu.SemaphoreType.DMA((n,)),
        ],
        out_specs=(VMEM_SPEC,) + (ANY_SPEC,) * 6,
        name="backward",
    )
    return out[0], out[1:4], out[4:]


RING = (0, 1, 2, 3, 6, 7)


def input_part(order, far, pos, act, w):
    def kernel(order, far, pos, *refs):
        nw = len(w.arrays)
        act, up, down, rest, wbuf, acc, sems = refs[nw:]
        copies = tile_copies(w.places, refs[:nw], pos, wbuf, sems, 0)
        start(copies)
        acc[...] = jnp.zeros_like(acc)
        finish(copies)

        def step(h, carry):
            js = [order[h * K + k] for k in range(K)]
            rhs = jnp.concatenate([wbuf[j] for j in js], axis=0)
            add_far(acc, far, js, dot(act[h], rhs, (1, 1)))
            return carry

        lax.fori_loop(0, H, step, 0, unroll=UNROLL)
        up[...] = acc[(pos[0] + 4) & 7].astype(BF)
        down[...] = acc[(pos[0] + 5) & 7].astype(BF)
        for n, r in enumerate(RING):
            rest[n] = acc[(pos[0] + r) & 7].astype(BF)

    one = jax.ShapeDtypeStruct((B, 8 * B), BF)
    return call(
        kernel,
        [one, one, jax.ShapeDtypeStruct((6, B, 8 * B), BF)],
        (order, far, pos),
        w.arrays,
        (act,),
        [TILES, WIDE_ACC, pltpu.SemaphoreType.DMA((len(w.places),))],
        name="input_part",
    )


def core_swap(a):
    return lax.ppermute(a, "fsdp", [(i, i ^ 1) for i in range(16)])


def y_swap(a):
    return lax.ppermute(a, "fsdp", [(i, i ^ 2) for i in range(16)])


def x_shift(a, d):
    return lax.ppermute(a, "fsdp", [(i, (i + 4 * d) % 16) for i in range(16)])


def dp_swap(a):
    return lax.ppermute(a, "dp", [(0, 1), (1, 0)])


def z_up(a):
    return lax.ppermute(a, "tensor", [(i, (i + 1) % 8) for i in range(8)])


def z_down(a):
    return lax.ppermute(a, "tensor", [(i, (i + 7) % 8) for i in range(8)])


def gather_up(tiles, *early):
    both = after(jnp.stack([tiles, y_swap(tiles)]), *early)
    mine = [both] + [x_shift(both, d) for d in (1, 3, 2)]
    arrays = mine + [core_swap(a) for a in mine]
    places = []
    for n in range(8):
        for dy in range(2):
            places.append((n, dy, ((0, 1, 3, 2)[n % 4], dy, n // 4)))
    return Wide(tuple(arrays), places)


def gather_down(tiles, early):
    x1, x3, x2 = (x_shift(tiles, d) for d in (1, 3, 2))
    mine = [jnp.stack([tiles, after(x1, early)]), jnp.stack([x3, after(x2, early)])]
    mine += [y_swap(a) for a in mine]
    arrays = mine + [core_swap(a) for a in mine]
    places = []
    for n in range(8):
        for i in range(2):
            places.append((n, i, ((0, 1, 3, 2)[n % 2 * 2 + i], n // 2 % 2, n // 4)))
    return Wide(tuple(arrays), places)


def add(a, b):
    return a.astype(F32) + b.astype(F32)


def scatter_features(partial):
    return lax.psum_scatter(partial, "tensor", scatter_dimension=0, tiled=True)[0]


def after(value, *others):
    return lax.optimization_barrier((value, *others))[0]


def body(activations, cotangent, up_tiles, down_tiles, up_rows, up_cols, down_rows, down_cols):
    f = lax.axis_index("fsdp")
    pos = jnp.stack([lax.axis_index("tensor"), f >> 2, (f >> 1) & 1, f & 1]).astype(jnp.int32)
    rows, cols = up_rows[:, 0], down_cols[:, 0]
    up_order, down_order = plan(up_cols[:, 0], down_rows[:, 0])
    pair = lax.all_gather(jnp.stack([activations, cotangent]), "tensor", axis=0, tiled=False)
    x = Wide((pair,), [(0, (z, 0), z, None) for z in range(8)])
    cot = Wide((pair,), [(0, (z, 1), z, None) for z in range(8)])
    up = gather_up(up_tiles, up_order, down_order, pos)
    down = gather_down(down_tiles, up.arrays[0])

    hidden, slope, partial_out = forward(up_order, rows, down_order, cols, pos, x, up, down)
    output = scatter_features(partial_out)
    pre_grad, (up0, up1, up_keep), (down12, down30, down_keep) = backward(
        down_order, cols, up_order, rows, pos, hidden, slope, cot, down, x
    )
    u1, u0 = core_swap(up1), core_swap(up0)
    near = add(up_keep[1], u1[0]).astype(BF)
    u_y = y_swap(near)
    d12, d30 = core_swap(down12), core_swap(down30)
    t1, t2 = add(down_keep[0], d12[0]).astype(BF), add(down_keep[1], d12[1]).astype(BF)
    d_x1 = x_shift(t1, 1)
    t3 = add(down_keep[2], d30[0]).astype(BF)
    d_x3 = x_shift(t3, 3)
    pre_grad_b = after(pre_grad, near, t1, t3)
    part4, part5, rest = input_part(up_order, rows, pos, pre_grad_b, up)

    part = {r: rest[n] for n, r in enumerate(RING)}
    z1, w1 = z_up(part4), z_down(part5)
    d_x2 = x_shift(after(t2, d_x1), 2)
    z2, w2 = add(part[3], z1).astype(BF), add(part[6], w1).astype(BF)
    z2, w2 = z_up(after(z2, output, d_x1, d_x3)), z_down(after(w2, output, d_x1, d_x3))
    total = (add(up_keep[0], u0[0]) + u_y.astype(F32)).astype(BF)
    u_x1, u_x3 = x_shift(total[1], 1), x_shift(total[3], 3)
    z3, w3 = add(part[2], z2).astype(BF), add(part[7], w2).astype(BF)
    z3, w3 = z_up(after(z3, total, d_x2)), z_down(after(w3, total, d_x2))
    own = add(down_keep[3], d30[1]) + add(d_x1, d_x3) + d_x2.astype(F32)
    d_y = y_swap(own[1].astype(BF))
    u_x2 = x_shift(after(total[2], u_x1), 2)
    down_mine = (own[0] + d_y.astype(F32)).astype(BF)
    z4 = add(part[1], z3).astype(BF)
    z4 = z_up(after(z4, u_x3))
    d_dp = dp_swap(down_mine)
    up_mine = (total[0].astype(F32) + add(u_x1, u_x3) + u_x2.astype(F32)).astype(BF)
    u_dp = dp_swap(up_mine)
    input_grad = (part[0].astype(F32) + add(z4, w3)).astype(BF)
    return (output, input_grad, add(up_mine, u_dp), add(down_mine, d_dp))


def solution(mesh):
    in_specs = (
        P(("dp", "fsdp"), "tensor"),
        P(("dp", "fsdp"), "tensor"),
        P(("fsdp", "tensor"), None, None),
        P(("fsdp", "tensor"), None, None),
        P(None, "tensor"),
        P(None, "tensor"),
        P(None, "tensor"),
        P(None, "tensor"),
    )
    out_specs = (
        P(("dp", "fsdp"), "tensor"),
        P(("dp", "fsdp"), "tensor"),
        P(("fsdp", "tensor"), None, None),
        P(("fsdp", "tensor"), None, None),
    )
    return jax.shard_map(body, mesh=mesh, in_specs=in_specs, out_specs=out_specs, check_vma=False)
```

profile of v0, /device:TPU:8, one launch (start us, length us, event | category | flops | bytes accessed | tf_op | source)
XLA Modules:
  0.0 175.1 jit_solution(3583619735450831088)
XLA Ops:
  7.2 1.9 %pad_maximum_fusion = bf16[2,128,1024]{2,1,0:T(8,128)(2,1)} fusion(bf16[1,128,1024]{2,1,0:T(8,128)(2,1)} %bitcast.74, bf16[1,128,1024]{2,1,0:T(8,128)(2,1)} %bitcast.75), kind=kLoop, calls=%fused_computation.16 | loop fusion | flops 262144 | bytes 1048576 | tf_op jit(solution)/shard_map/stack | solution.py:381
  9.2 2.3 %collective-permute-start = (bf16[8,128,128]{2,1,0:T(8,128)(2,1)}, bf16[8,128,128]{2,1,0:T(8,128)(2,1)S(1)}, u32[]{:S(2)}, u32[]{:S(2)}) collective-permute-start(bf16[8,128,128]{2,1,0:T(8,128)(2,1)} %param.10), channel_id=1, source_target_pairs={{0,16},{8,24},{16,0},{24,8},{32,48},{40,56},{48,32},{56,40},{64,80... | collective-permute-start | bytes 786440 | tf_op jit(solution)/shard_map/ppermute | solution.py:322
  15.4 4.6 %plan.1 = (s32[128]{0:T(128)}, s32[128]{0:T(128)}) custom-call(s32[128]{0:T(128)} %bitcast.88, s32[128]{0:T(128)} %bitcast.89), custom_call_target="tpu_custom_call" | custom-call | tf_op jit(solution)/shard_map/plan/pallas_call | solution.py:55
  22.1 2.9 %collective-permute-done.9 = bf16[8,128,128]{2,1,0:T(8,128)(2,1)S(1)} collective-permute-done((bf16[8,128,128]{2,1,0:T(8,128)(2,1)}, bf16[8,128,128]{2,1,0:T(8,128)(2,1)S(1)}, u32[]{:S(2)}, u32[]{:S(2)}) %collective-permute-start.9) | collective-permute-done | bytes 262176 | tf_op jit(solution)/shard_map/ppermute | solution.py:326
  27.6 2.2 %collective-permute-start.3 = (bf16[2,8,128,128]{3,2,1,0:T(8,128)(2,1)S(1)}, bf16[2,8,128,128]{3,2,1,0:T(8,128)(2,1)S(1)}, u32[]{:S(2)}, u32[]{:S(2)}) collective-permute-start(bf16[2,8,128,128]{3,2,1,0:T(8,128)(2,1)S(1)} %pad_maximum_fusion.1.refs_1_.refs_0_), channel_id=1, source_target_pairs={{0,64},{8,72},{16,80},{24,88},{32,96},{40,104},{48,112},{56,120},{... | collective-permute-start | bytes 1572872 | tf_op jit(solution)/shard_map/ppermute | solution.py:326
  29.9 10.1 %collective-permute-done.12.refs_12_.refs_4_ = bf16[2,8,128,128]{3,2,1,0:T(8,128)(2,1)S(1)} collective-permute-done((bf16[2,8,128,128]{3,2,1,0:T(8,128)(2,1)S(1)}, bf16[2,8,128,128]{3,2,1,0:T(8,128)(2,1)S(1)}, u32[]{:S(2)}, u32[]{:S(2)}) %collective-permute-start.12) | collective-permute-done | bytes 524320 | tf_op jit(solution)/shard_map/ppermute | solution.py:322
  39.9 2.6 %collective-permute-start.2 = (bf16[2,8,128,128]{3,2,1,0:T(8,128)(2,1)S(1)}, bf16[2,8,128,128]{3,2,1,0:T(8,128)(2,1)S(1)}, u32[]{:S(2)}, u32[]{:S(2)}) collective-permute-start(bf16[2,8,128,128]{3,2,1,0:T(8,128)(2,1)S(1)} %pad_maximum_fusion.1.refs_1_.refs_0_), channel_id=1, source_target_pairs={{0,96},{8,104},{16,112},{24,120},{32,0},{40,8},{48,16},{56,24},{64... | collective-permute-start | bytes 1572872 | tf_op jit(solution)/shard_map/ppermute | solution.py:326
  42.6 8.1 %collective-permute-done.11.refs_11_.refs_3_ = bf16[2,8,128,128]{3,2,1,0:T(8,128)(2,1)S(1)} collective-permute-done((bf16[2,8,128,128]{3,2,1,0:T(8,128)(2,1)S(1)}, bf16[2,8,128,128]{3,2,1,0:T(8,128)(2,1)S(1)}, u32[]{:S(2)}, u32[]{:S(2)}) %collective-permute-start.11) | collective-permute-done | bytes 524320 | tf_op jit(solution)/shard_map/ppermute | solution.py:322
  51.3 3.3 %collective-permute-done.2.refs_3_.refs_2_ = bf16[2,8,128,128]{3,2,1,0:T(8,128)(2,1)S(1)} collective-permute-done((bf16[2,8,128,128]{3,2,1,0:T(8,128)(2,1)S(1)}, bf16[2,8,128,128]{3,2,1,0:T(8,128)(2,1)S(1)}, u32[]{:S(2)}, u32[]{:S(2)}) %collective-permute-start.2) | collective-permute-done | bytes 524320 | tf_op jit(solution)/shard_map/ppermute | solution.py:326
  54.6 2.0 %collective-permute-done.1.refs_2_.refs_1_ = bf16[2,8,128,128]{3,2,1,0:T(8,128)(2,1)S(1)} collective-permute-done((bf16[2,8,128,128]{3,2,1,0:T(8,128)(2,1)S(1)}, bf16[2,8,128,128]{3,2,1,0:T(8,128)(2,1)S(1)}, u32[]{:S(2)}, u32[]{:S(2)}) %collective-permute-start.1) | collective-permute-done | bytes 524320 | tf_op jit(solution)/shard_map/ppermute | solution.py:326
  59.9 8.2 %all-gather.3.cloned.1.call-done = bf16[16,128,1024]{2,1,0:T(8,128)(2,1)} async-done(((bf16[2,128,1024]{2,1,0:T(8,128)(2,1)}), bf16[16,128,1024]{2,1,0:T(8,128)(2,1)}) %all-gather.3.cloned.1.call-update) | async-done | bytes 4194320 | tf_op jit(solution)/shard_map/all_gather | solution.py:381
  68.1 11.2 %forward.1 = (bf16[16,128,128]{2,1,0:T(8,128)(2,1)}, f32[16,128,128]{2,1,0:T(8,128)}, bf16[8,128,1024]{2,1,0:T(8,128)(2,1)}) custom-call(s32[128]{0:T(128)} %get-tuple-element.30.up_order.order, s32[128]{0:T(128)} %bitcast.82, s32[128]{0:T(128)} %get-tuple-element.31.down_order, s32[128]{0:T(128)} %bitcast.85, s32[4]{0:T(128)} %pad_add_fusion.pos, ...), custom_call_target="tpu_custom_call" | custom-call | flops 10000000 | bytes 100000 | tf_op jit(solution)/shard_map/forward/pallas_call | solution.py:102
  79.4 15.4 %backward.1 = (bf16[16,128,128]{2,1,0:T(8,128)(2,1)}, bf16[1,4,8,128,128]{4,3,2,1,0:T(8,128)(2,1)}, bf16[1,4,8,128,128]{4,3,2,1,0:T(8,128)(2,1)}, bf16[2,4,8,128...) custom-call(s32[128]{0:T(128)} %get-tuple-element.31.down_order, ...), custom_call_target="tpu_custom_call" | custom-call | flops 10000000 | bytes 100000 | tf_op jit(solution)/shard_map/backward/pallas_call | solution.py:102
  97.7 2.6 %fusion.1 = bf16[4,8,128,128]{3,2,1,0:T(8,128)(2,1)} fusion(bf16[1,4,8,128,128]{4,3,2,1,0:T(8,128)(2,1)S(1)} %collective-permute-done.17, bf16[2,4,8,128,128]{4,3,2,1,0:T(8,128)(2,1)} %get-tuple-element.39), kind=kLoop, calls=%fused_computation.3 | loop fusion | flops 2097152 | bytes 3145728 | tf_op jit(solution)/shard_map/convert_element_type | solution.py:393
  106.9 8.0 %input_part.1 = (bf16[128,1024]{1,0:T(8,128)(2,1)}, bf16[128,1024]{1,0:T(8,128)(2,1)}, bf16[6,128,1024]{2,1,0:T(8,128)(2,1)}) custom-call(s32[128]{0:T(128)} %get-tuple-element.30.up_order.order, s32[128]{0:T(128)} %bitcast.84, s32[4]{0:T(128)} %pad_add_fusion.pos, bf16[2,8,128,128]{3,2,1,0:T(8,128)(2,1)} %copy-done.2, bf16[2,8,128,128]{3,2,1,0:T(8,128)(2,1)} %copy-done.12, ...), custom_call_target="tpu_custom_call" | custom-call | flops 10000000 | bytes 100000 | tf_op jit(solution)/shard_map/input_part/pallas_call | solution.py:102
  115.0 9.8 %collective-permute-done.20 = bf16[128,1024]{1,0:T(8,128)(2,1)S(1)} collective-permute-done((bf16[128,1024]{1,0:T(8,128)(2,1)}, bf16[128,1024]{1,0:T(8,128)(2,1)S(1)}, u32[]{:S(2)}, u32[]{:S(2)}) %collective-permute-start.20) | collective-permute-done | bytes 262176 | tf_op jit(solution)/shard_map/ppermute | solution.py:334
  126.1 2.4 %collective-permute-start.26 = (bf16[2,8,128,128]{3,2,1,0:T(8,128)(2,1)}, bf16[2,8,128,128]{3,2,1,0:T(8,128)(2,1)}, u32[]{:S(2)}, u32[]{:S(2)}) collective-permute-start(bf16[2,8,128,128]{3,2,1,0:T(8,128)(2,1)} %get-tuple-element.49), channel_id=1, source_target_pairs={{0,64},{8,72},{16,80},{24,88},{32,96},{40,104},{48,112},{56,120},{... | collective-permute-start | bytes 1572872 | tf_op jit(solution)/shard_map/ppermute | solution.py:326
  129.9 2.3 %fusion = bf16[4,8,128,128]{3,2,1,0:T(8,128)(2,1)S(1)} fusion(bf16[4,8,128,128]{3,2,1,0:T(8,128)(2,1)} %collective-permute-done.25, bf16[1,4,8,128,128]{4,3,2,1,0:T(8,128)(2,1)} %collective-permute-done.24, bf16[2,4,8,128,128]{4,3,2,1,0:T(8,128)(2,1)} %get-tuple-element.39), kind=kLoop, calls=%fused_computation.1 | loop fusion | flops 3145728 | bytes 4194304 | tf_op jit(solution)/shard_map/convert_element_type | solution.py:408
  133.3 3.3 %collective-permute-done.23 = bf16[128,1024]{1,0:T(8,128)(2,1)S(1)} collective-permute-done((bf16[128,1024]{1,0:T(8,128)(2,1)S(1)}, bf16[128,1024]{1,0:T(8,128)(2,1)S(1)}, u32[]{:S(2)}, u32[]{:S(2)}) %collective-permute-start.23) | collective-permute-done | bytes 262176 | tf_op jit(solution)/shard_map/ppermute | solution.py:334
  136.7 6.2 %collective-permute-done.26 = bf16[2,8,128,128]{3,2,1,0:T(8,128)(2,1)} collective-permute-done((bf16[2,8,128,128]{3,2,1,0:T(8,128)(2,1)}, bf16[2,8,128,128]{3,2,1,0:T(8,128)(2,1)}, u32[]{:S(2)}, u32[]{:S(2)}) %collective-permute-start.26) | collective-permute-done | bytes 524320 | tf_op jit(solution)/shard_map/ppermute | solution.py:326
  147.2 2.1 %collective-permute-start.34 = (bf16[8,128,128]{2,1,0:T(8,128)(2,1)S(1)}, bf16[8,128,128]{2,1,0:T(8,128)(2,1)S(1)}, u32[]{:S(2)}, u32[]{:S(2)}) collective-permute-start(bf16[8,128,128]{2,1,0:T(8,128)(2,1)S(1)} %get-tuple-element.55), channel_id=1, source_target_pairs={{0,64},{8,72},{16,80},{24,88},{32,96},{40,104},{48,112},{56,120},{... | collective-permute-start | bytes 786440 | tf_op jit(solution)/shard_map/ppermute | solution.py:326
  153.0 2.3 %collective-permute-start.37 = (bf16[8,128,128]{2,1,0:T(8,128)(2,1)S(1)}, bf16[8,128,128]{2,1,0:T(8,128)(2,1)S(1)}, u32[]{:S(2)}, u32[]{:S(2)}) collective-permute-start(bf16[8,128,128]{2,1,0:T(8,128)(2,1)S(1)} %fusion.7), channel_id=1, source_target_pairs={{0,128},{128,0},{1,129},{129,1},{2,130},{130,2},{3,131},{131,3},{4... | collective-permute-start | bytes 786440 | tf_op jit(solution)/shard_map/ppermute | solution.py:330
  156.3 2.3 %collective-permute-start.35 = (bf16[8,128,128]{2,1,0:T(8,128)(2,1)S(1)}, bf16[8,128,128]{2,1,0:T(8,128)(2,1)S(1)}, u32[]{:S(2)}, u32[]{:S(2)}) collective-permute-start(bf16[8,128,128]{2,1,0:T(8,128)(2,1)S(1)} %fusion.9), channel_id=1, source_target_pairs={{0,128},{128,0},{1,129},{129,1},{2,130},{130,2},{3,131},{131,3},{4... | collective-permute-start | bytes 786440 | tf_op jit(solution)/shard_map/ppermute | solution.py:330
  164.1 2.5 %collective-permute-done.35 = bf16[8,128,128]{2,1,0:T(8,128)(2,1)S(1)} collective-permute-done((bf16[8,128,128]{2,1,0:T(8,128)(2,1)S(1)}, bf16[8,128,128]{2,1,0:T(8,128)(2,1)S(1)}, u32[]{:S(2)}, u32[]{:S(2)}) %collective-permute-start.35) | collective-permute-done | bytes 262176 | tf_op jit(solution)/shard_map/ppermute | solution.py:330
  (116 shorter events, 42.2 us)
Async XLA Ops:
  7.2 60.9 %all-gather.3.cloned.1.call-start = ((), (), s32[]{:S(2)}) async-start(), calls=%async_computation.2 | async-start | bytes 4718592 | tf_op jit(solution)/shard_map/all_gather | solution.py:381
  9.2 119.3 %reduce-scatter.2.cloned.1.call-start = ((), (), s32[]{:S(2)}) async-start(), calls=%async_computation.1 | async-start | bytes 2359296 | tf_op jit(solution)/shard_map/reduce_scatter | solution.py:369
  9.2 10.8 %collective-permute-start = (bf16[8,128,128]{2,1,0:T(8,128)(2,1)}, bf16[8,128,128]{2,1,0:T(8,128)(2,1)S(1)}, u32[]{:S(2)}, u32[]{:S(2)}) collective-permute-start(bf16[8,128,128]{2,1,0:T(8,128)(2,1)} %param.10), channel_id=1, source_target_pairs={{0,16},{8,24},{16,0},{24,8},{32,48},{40,56},{48,32},{56,40},{64,80... | collective-permute-start | bytes 786440 | tf_op jit(solution)/shard_map/ppermute | solution.py:322
  11.5 10.6 %collective-permute-start.10 = (bf16[8,128,128]{2,1,0:T(8,128)(2,1)}, bf16[8,128,128]{2,1,0:T(8,128)(2,1)S(1)}, u32[]{:S(2)}, u32[]{:S(2)}) collective-permute-start(bf16[8,128,128]{2,1,0:T(8,128)(2,1)} %param.11), channel_id=1, source_target_pairs={{0,64},{8,72},{16,80},{24,88},{32,96},{40,104},{48,112},{56,120},{... | collective-permute-start | bytes 786440 | tf_op jit(solution)/shard_map/ppermute | solution.py:326
  12.8 12.2 %collective-permute-start.9 = (bf16[8,128,128]{2,1,0:T(8,128)(2,1)}, bf16[8,128,128]{2,1,0:T(8,128)(2,1)S(1)}, u32[]{:S(2)}, u32[]{:S(2)}) collective-permute-start(bf16[8,128,128]{2,1,0:T(8,128)(2,1)} %param.11), channel_id=1, source_target_pairs={{0,96},{8,104},{16,112},{24,120},{32,0},{40,8},{48,16},{56,24},{64... | collective-permute-start | bytes 786440 | tf_op jit(solution)/shard_map/ppermute | solution.py:326
  13.9 12.9 %collective-permute-start.8 = (bf16[8,128,128]{2,1,0:T(8,128)(2,1)}, bf16[8,128,128]{2,1,0:T(8,128)(2,1)S(1)}, u32[]{:S(2)}, u32[]{:S(2)}) collective-permute-start(bf16[8,128,128]{2,1,0:T(8,128)(2,1)} %param.11), channel_id=1, source_target_pairs={{0,32},{8,40},{16,48},{24,56},{32,64},{40,72},{48,80},{56,88},{64,... | collective-permute-start | bytes 786440 | tf_op jit(solution)/shard_map/ppermute | solution.py:326
  25.1 14.8 %collective-permute-start.12 = (bf16[2,8,128,128]{3,2,1,0:T(8,128)(2,1)S(1)}, bf16[2,8,128,128]{3,2,1,0:T(8,128)(2,1)S(1)}, u32[]{:S(2)}, u32[]{:S(2)}) collective-permute-start(bf16[2,8,128,128]{3,2,1,0:T(8,128)(2,1)S(1)} %pad_maximum_fusion.3.refs_10_.refs_2_), channel_id=1, source_target_pairs={{0,16},{8,24},{16,0},{24,8},{32,48},{40,56},{48,32},{56,40},{64,80... | collective-permute-start | bytes 1572872 | tf_op jit(solution)/shard_map/ppermute | solution.py:322
  26.9 15.7 %collective-permute-start.13 = (bf16[2,8,128,128]{3,2,1,0:T(8,128)(2,1)S(1)}, bf16[2,8,128,128]{3,2,1,0:T(8,128)(2,1)S(1)}, u32[]{:S(2)}, u32[]{:S(2)}) collective-permute-start(bf16[2,8,128,128]{3,2,1,0:T(8,128)(2,1)S(1)} %pad_maximum_fusion.2.refs_9_.refs_1_), channel_id=1, source_target_pairs={{0,8},{8,0},{16,24},{24,16},{32,40},{40,32},{48,56},{56,48},{64,72... | collective-permute-start | bytes 1572872 | tf_op jit(solution)/shard_map/ppermute | solution.py:318
  27.1 23.6 %collective-permute-start.11 = (bf16[2,8,128,128]{3,2,1,0:T(8,128)(2,1)S(1)}, bf16[2,8,128,128]{3,2,1,0:T(8,128)(2,1)S(1)}, u32[]{:S(2)}, u32[]{:S(2)}) collective-permute-start(bf16[2,8,128,128]{3,2,1,0:T(8,128)(2,1)S(1)} %pad_maximum_fusion.2.refs_9_.refs_1_), channel_id=1, source_target_pairs={{0,16},{8,24},{16,0},{24,8},{32,48},{40,56},{48,32},{56,40},{64,80... | collective-permute-start | bytes 1572872 | tf_op jit(solution)/shard_map/ppermute | solution.py:322
  27.6 23.2 %collective-permute-start.4 = (bf16[2,8,128,128]{3,2,1,0:T(8,128)(2,1)S(1)}, bf16[2,8,128,128]{3,2,1,0:T(8,128)(2,1)}, u32[]{:S(2)}, u32[]{:S(2)}) collective-permute-start(bf16[2,8,128,128]{3,2,1,0:T(8,128)(2,1)S(1)} %pad_maximum_fusion.1.refs_1_.refs_0_), channel_id=1, source_target_pairs={{0,8},{8,0},{16,24},{24,16},{32,40},{40,32},{48,56},{56,48},{64,72... | collective-permute-start | bytes 1572872 | tf_op jit(solution)/shard_map/ppermute | solution.py:318
  27.6 23.6 %collective-permute-start.3 = (bf16[2,8,128,128]{3,2,1,0:T(8,128)(2,1)S(1)}, bf16[2,8,128,128]{3,2,1,0:T(8,128)(2,1)S(1)}, u32[]{:S(2)}, u32[]{:S(2)}) collective-permute-start(bf16[2,8,128,128]{3,2,1,0:T(8,128)(2,1)S(1)} %pad_maximum_fusion.1.refs_1_.refs_0_), channel_id=1, source_target_pairs={{0,64},{8,72},{16,80},{24,88},{32,96},{40,104},{48,112},{56,120},{... | collective-permute-start | bytes 1572872 | tf_op jit(solution)/shard_map/ppermute | solution.py:326
  39.9 14.7 %collective-permute-start.2 = (bf16[2,8,128,128]{3,2,1,0:T(8,128)(2,1)S(1)}, bf16[2,8,128,128]{3,2,1,0:T(8,128)(2,1)S(1)}, u32[]{:S(2)}, u32[]{:S(2)}) collective-permute-start(bf16[2,8,128,128]{3,2,1,0:T(8,128)(2,1)S(1)} %pad_maximum_fusion.1.refs_1_.refs_0_), channel_id=1, source_target_pairs={{0,96},{8,104},{16,112},{24,120},{32,0},{40,8},{48,16},{56,24},{64... | collective-permute-start | bytes 1572872 | tf_op jit(solution)/shard_map/ppermute | solution.py:326
  42.6 14.0 %collective-permute-start.1 = (bf16[2,8,128,128]{3,2,1,0:T(8,128)(2,1)S(1)}, bf16[2,8,128,128]{3,2,1,0:T(8,128)(2,1)S(1)}, u32[]{:S(2)}, u32[]{:S(2)}) collective-permute-start(bf16[2,8,128,128]{3,2,1,0:T(8,128)(2,1)S(1)} %pad_maximum_fusion.1.refs_1_.refs_0_), channel_id=1, source_target_pairs={{0,32},{8,40},{16,48},{24,56},{32,64},{40,72},{48,80},{56,88},{64,... | collective-permute-start | bytes 1572872 | tf_op jit(solution)/shard_map/ppermute | solution.py:326
  95.5 34.4 %collective-permute-start.24 = (bf16[1,4,8,128,128]{4,3,2,1,0:T(8,128)(2,1)}, bf16[1,4,8,128,128]{4,3,2,1,0:T(8,128)(2,1)}, u32[]{:S(2)}, u32[]{:S(2)}) collective-permute-start(bf16[1,4,8,128,128]{4,3,2,1,0:T(8,128)(2,1)} %get-tuple-element.48), channel_id=1, source_target_pairs={{0,8},{8,0},{16,24},{24,16},{32,40},{40,32},{48,56},{56,48},{64,72... | collective-permute-start | bytes 3145736 | tf_op jit(solution)/shard_map/ppermute | solution.py:318
  100.4 29.5 %collective-permute-start.25 = (bf16[4,8,128,128]{3,2,1,0:T(8,128)(2,1)}, bf16[4,8,128,128]{3,2,1,0:T(8,128)(2,1)}, u32[]{:S(2)}, u32[]{:S(2)}) collective-permute-start(bf16[4,8,128,128]{3,2,1,0:T(8,128)(2,1)} %fusion.1), channel_id=1, source_target_pairs={{0,16},{8,24},{16,0},{24,8},{32,48},{40,56},{48,32},{56,40},{64,80... | collective-permute-start | bytes 3145736 | tf_op jit(solution)/shard_map/ppermute | solution.py:322
  103.6 22.4 %collective-permute-start.21 = (bf16[2,8,128,128]{3,2,1,0:T(8,128)(2,1)S(1)}, bf16[2,8,128,128]{3,2,1,0:T(8,128)(2,1)}, u32[]{:S(2)}, u32[]{:S(2)}) collective-permute-start(bf16[2,8,128,128]{3,2,1,0:T(8,128)(2,1)S(1)} %get-tuple-element.57), channel_id=1, source_target_pairs={{0,32},{8,40},{16,48},{24,56},{32,64},{40,72},{48,80},{56,88},{64,... | collective-permute-start | bytes 1572872 | tf_op jit(solution)/shard_map/ppermute | solution.py:326
  105.1 23.3 %collective-permute-start.22 = (bf16[2,8,128,128]{3,2,1,0:T(8,128)(2,1)S(1)}, bf16[2,8,128,128]{3,2,1,0:T(8,128)(2,1)}, u32[]{:S(2)}, u32[]{:S(2)}) collective-permute-start(bf16[2,8,128,128]{3,2,1,0:T(8,128)(2,1)S(1)} %get-tuple-element.58), channel_id=1, source_target_pairs={{0,96},{8,104},{16,112},{24,120},{32,0},{40,8},{48,16},{56,24},{64... | collective-permute-start | bytes 1572872 | tf_op jit(solution)/shard_map/ppermute | solution.py:326
  114.9 9.9 %collective-permute-start.20 = (bf16[128,1024]{1,0:T(8,128)(2,1)}, bf16[128,1024]{1,0:T(8,128)(2,1)S(1)}, u32[]{:S(2)}, u32[]{:S(2)}) collective-permute-start(bf16[128,1024]{1,0:T(8,128)(2,1)} %get-tuple-element.46), channel_id=1, source_target_pairs={{0,1},{1,2},{2,3},{3,4},{4,5},{5,6},{6,7},{7,0},{8,9},{9,10},{10,1... | collective-permute-start | bytes 786440 | tf_op jit(solution)/shard_map/ppermute | solution.py:334
  124.8 24.5 %collective-permute-start.30 = (bf16[128,1024]{1,0:T(8,128)(2,1)}, bf16[128,1024]{1,0:T(8,128)(2,1)}, u32[]{:S(2)}, u32[]{:S(2)}) collective-permute-start(bf16[128,1024]{1,0:T(8,128)(2,1)} %get-tuple-element.52), channel_id=1, source_target_pairs={{0,7},{1,0},{2,1},{3,2},{4,3},{5,4},{6,5},{7,6},{8,15},{9,8},{10,9... | collective-permute-start | bytes 786440 | tf_op jit(solution)/shard_map/ppermute | solution.py:338
  126.1 16.8 %collective-permute-start.26 = (bf16[2,8,128,128]{3,2,1,0:T(8,128)(2,1)}, bf16[2,8,128,128]{3,2,1,0:T(8,128)(2,1)}, u32[]{:S(2)}, u32[]{:S(2)}) collective-permute-start(bf16[2,8,128,128]{3,2,1,0:T(8,128)(2,1)} %get-tuple-element.49), channel_id=1, source_target_pairs={{0,64},{8,72},{16,80},{24,88},{32,96},{40,104},{48,112},{56,120},{... | collective-permute-start | bytes 1572872 | tf_op jit(solution)/shard_map/ppermute | solution.py:326
  132.4 14.8 %collective-permute-start.33 = (bf16[8,128,128]{2,1,0:T(8,128)(2,1)S(1)}, bf16[8,128,128]{2,1,0:T(8,128)(2,1)S(1)}, u32[]{:S(2)}, u32[]{:S(2)}) collective-permute-start(bf16[8,128,128]{2,1,0:T(8,128)(2,1)S(1)} %get-tuple-element.61), channel_id=1, source_target_pairs={{0,32},{8,40},{16,48},{24,56},{32,64},{40,72},{48,80},{56,88},{64,... | collective-permute-start | bytes 786440 | tf_op jit(solution)/shard_map/ppermute | solution.py:326
  147.2 8.9 %collective-permute-start.34 = (bf16[8,128,128]{2,1,0:T(8,128)(2,1)S(1)}, bf16[8,128,128]{2,1,0:T(8,128)(2,1)S(1)}, u32[]{:S(2)}, u32[]{:S(2)}) collective-permute-start(bf16[8,128,128]{2,1,0:T(8,128)(2,1)S(1)} %get-tuple-element.55), channel_id=1, source_target_pairs={{0,64},{8,72},{16,80},{24,88},{32,96},{40,104},{48,112},{56,120},{... | collective-permute-start | bytes 786440 | tf_op jit(solution)/shard_map/ppermute | solution.py:326
  153.0 10.3 %collective-permute-start.37 = (bf16[8,128,128]{2,1,0:T(8,128)(2,1)S(1)}, bf16[8,128,128]{2,1,0:T(8,128)(2,1)S(1)}, u32[]{:S(2)}, u32[]{:S(2)}) collective-permute-start(bf16[8,128,128]{2,1,0:T(8,128)(2,1)S(1)} %fusion.7), channel_id=1, source_target_pairs={{0,128},{128,0},{1,129},{129,1},{2,130},{130,2},{3,131},{131,3},{4... | collective-permute-start | bytes 786440 | tf_op jit(solution)/shard_map/ppermute | solution.py:330
  156.3 10.3 %collective-permute-start.35 = (bf16[8,128,128]{2,1,0:T(8,128)(2,1)S(1)}, bf16[8,128,128]{2,1,0:T(8,128)(2,1)S(1)}, u32[]{:S(2)}, u32[]{:S(2)}) collective-permute-start(bf16[8,128,128]{2,1,0:T(8,128)(2,1)S(1)} %fusion.9), channel_id=1, source_target_pairs={{0,128},{128,0},{1,129},{129,1},{2,130},{130,2},{3,131},{131,3},{4... | collective-permute-start | bytes 786440 | tf_op jit(solution)/shard_map/ppermute | solution.py:330
  (33 other events, 380.9 us)
Sparse Core Ops, SparseCore 0:
  10.4 57.6 all-gather.2
  79.5 41.2 reduce-scatter.1
where the time goes:
time: 176 us; the launch traced here: 175 us
  waiting for transfers between devices  64.9 us (37%)
  Pallas kernels  39.2 us (22%)
  starting transfers between devices  36.6 us (21%)
  other arithmetic  16.8 us (10%)
  between operations  14.3 us (8%)
  local copies, waits for them, and re-layouts  3.35 us (2%)
    pallas_call x3, Pallas kernels, call(): pl.pallas_call(kernel, out_shape=tuple(out_shape), in_specs=[SMEM_SPEC] *...  34.6 us
    ppermute x5, waiting for transfers between devices, y_swap(): return lax.ppermute(a, 'fsdp', [(i, i ^ 2) for i in range(16)])  19 us
    ppermute x12, starting transfers between devices, x_shift(): return lax.ppermute(a, 'fsdp', [(i, (i + 4 * d) % 16) for i in range(16)])  16.8 us
    ppermute x12, waiting for transfers between devices, x_shift(): return lax.ppermute(a, 'fsdp', [(i, (i + 4 * d) % 16) for i in range(16)])  16.3 us
    ppermute x4, waiting for transfers between devices, z_up(): return lax.ppermute(a, 'tensor', [(i, (i + 1) % 8) for i in range(8)])  14.3 us
    all_gather x1, waiting for transfers between devices, body(): lax.all_gather(jnp.stack([activations, cotangent]), 'tensor', axis=0, til...  8.23 us
    ppermute x5, starting transfers between devices, y_swap(): return lax.ppermute(a, 'fsdp', [(i, i ^ 2) for i in range(16)])  5.66 us
    ppermute x4, starting transfers between devices, z_up(): return lax.ppermute(a, 'tensor', [(i, (i + 1) % 8) for i in range(8)])  5.08 us
  transfers between devices with their start and end apart: 40, of which 17 were waited for; matrix products, arithmetic and copies ran while one was open for 8% of the time, Pallas kernels for 16%

commit v1 on v0

--- a/solution.py
+++ b/solution.py
@@ -401,22 +401,25 @@
     part4, part5, rest = input_part(up_order, rows, pos, pre_grad_b, up)
 
     part = {r: rest[n] for n, r in enumerate(RING)}
+    part4, part5, _ = lax.optimization_barrier((part4, part5, (d_x1, d_x3)))
     z1, w1 = z_up(part4), z_down(part5)
     d_x2 = x_shift(after(t2, d_x1), 2)
-    z2, w2 = add(part[3], z1).astype(BF), add(part[6], w1).astype(BF)
-    z2, w2 = z_up(after(z2, output, d_x1, d_x3)), z_down(after(w2, output, d_x1, d_x3))
     total = (add(up_keep[0], u0[0]) + u_y.astype(F32)).astype(BF)
     u_x1, u_x3 = x_shift(total[1], 1), x_shift(total[3], 3)
-    z3, w3 = add(part[2], z2).astype(BF), add(part[7], w2).astype(BF)
-    z3, w3 = z_up(after(z3, total, d_x2)), z_down(after(w3, total, d_x2))
+    z1, w1, _ = lax.optimization_barrier((z1, w1, total))
+    z2, w2 = add(part[3], z1).astype(BF), add(part[6], w1).astype(BF)
+    z2, w2, _ = lax.optimization_barrier((z2, w2, (output, d_x2)))
+    z2, w2 = z_up(z2), z_down(w2)
     own = add(down_keep[3], d30[1]) + add(d_x1, d_x3) + d_x2.astype(F32)
     d_y = y_swap(own[1].astype(BF))
     u_x2 = x_shift(after(total[2], u_x1), 2)
+    z3, w3 = add(part[2], z2).astype(BF), add(part[7], w2).astype(BF)
+    z3, w3, _ = lax.optimization_barrier((z3, w3, (u_x1, u_x3)))
+    z3, w3 = z_up(z3), z_down(w3)
     down_mine = (own[0] + d_y.astype(F32)).astype(BF)
-    z4 = add(part[1], z3).astype(BF)
-    z4 = z_up(after(z4, u_x3))
     d_dp = dp_swap(down_mine)
     up_mine = (total[0].astype(F32) + add(u_x1, u_x3) + u_x2.astype(F32)).astype(BF)
+    z4 = z_up(after(add(part[1], z3).astype(BF), w3, d_y, u_x2))
     u_dp = dp_swap(up_mine)
     input_grad = (part[0].astype(F32) + add(z4, w3)).astype(BF)
     return (output, input_grad, add(up_mine, u_dp), add(down_mine, d_dp))

time: 176 us -> 171 us (0.972)
  waiting for transfers between devices: 64.9 us -> 57.6 us
  starting transfers between devices: 36.6 us -> 38.8 us
    ppermute x4, waiting for transfers between devices: 14.3 us -> 4.15 us  [z_up(): return lax.ppermute(a, 'tensor', [(i, (i + 1) % 8) for i in range(8)])]
    ppermute x3, starting transfers between devices: 2.37 us -> 7.89 us  [z_down(): return lax.ppermute(a, 'tensor', [(i, (i + 7) % 8) for i in range(8)])]
    ppermute x5, waiting for transfers between devices: 19 us -> 22.5 us  [y_swap(): return lax.ppermute(a, 'fsdp', [(i, i ^ 2) for i in range(16)])]
    ppermute x12, waiting for transfers between devices: 16.3 us -> 13.2 us  [x_shift(): return lax.ppermute(a, 'fsdp', [(i, (i + 4 * d) % 16) for i in range(16)])]
    ppermute x3, waiting for transfers between devices: 0.01 us -> 2.77 us  [z_down(): return lax.ppermute(a, 'tensor', [(i, (i + 7) % 8) for i in range(8)])]
    ppermute x4, starting transfers between devices: 5.08 us -> 2.36 us  [z_up(): return lax.ppermute(a, 'tensor', [(i, (i + 1) % 8) for i in range(8)])]
  transfers between devices with their start and end apart: 40 -> 40, of which waited for: 17 -> 18; matrix products, arithmetic and copies ran while one was open for 8% -> 9% of each run, Pallas kernels for 16% -> 16%
where the time goes in v1:
time: 171 us
  waiting for transfers between devices  57.6 us (34%)
  Pallas kernels  39.3 us (23%)
  starting transfers between devices  38.8 us (23%)
  other arithmetic  16.3 us (10%)
  between operations  14.3 us (8%)
  local copies, waits for them, and re-layouts  4.23 us (2%)
    pallas_call x3, Pallas kernels, call(): pl.pallas_call(kernel, out_shape=tuple(out_shape), in_specs=[SMEM_SPEC] *...  34.7 us
    ppermute x5, waiting for transfers between devices, y_swap(): return lax.ppermute(a, 'fsdp', [(i, i ^ 2) for i in range(16)])  22.5 us
    ppermute x12, starting transfers between devices, x_shift(): return lax.ppermute(a, 'fsdp', [(i, (i + 4 * d) % 16) for i in range(16)])  16.9 us
    ppermute x12, waiting for transfers between devices, x_shift(): return lax.ppermute(a, 'fsdp', [(i, (i + 4 * d) % 16) for i in range(16)])  13.2 us
    all_gather x1, waiting for transfers between devices, body(): lax.all_gather(jnp.stack([activations, cotangent]), 'tensor', axis=0, til...  8.22 us
    ppermute x3, starting transfers between devices, z_down(): return lax.ppermute(a, 'tensor', [(i, (i + 7) % 8) for i in range(8)])  7.89 us
    ppermute x5, starting transfers between devices, y_swap(): return lax.ppermute(a, 'fsdp', [(i, i ^ 2) for i in range(16)])  5.43 us
    pallas_call x1, Pallas kernels, plan(): pl.pallas_call(plan_kernel, out_shape=(shape, shape), in_specs=[SMEM_SPEC...  4.58 us
  transfers between devices with their start and end apart: 40, of which 18 were waited for; matrix products, arithmetic and copies ran while one was open for 9% of the time, Pallas kernels for 16%

profile of v1, /device:TPU:8, one launch (start us, length us, event | category | flops | bytes accessed | tf_op | source)
XLA Modules:
  0.0 170.6 jit_solution(2271308534598415912)
XLA Ops:
  9.2 2.3 %collective-permute-start = (bf16[8,128,128]{2,1,0:T(8,128)(2,1)}, bf16[8,128,128]{2,1,0:T(8,128)(2,1)S(1)}, u32[]{:S(2)}, u32[]{:S(2)}) collective-permute-start(bf16[8,128,128]{2,1,0:T(8,128)(2,1)} %param.10), channel_id=1, source_target_pairs={{0,16},{8,24},{16,0},{24,8},{32,48},{40,56},{48,32},{56,40},{64,80... | collective-permute-start | bytes 786440 | tf_op jit(solution)/shard_map/ppermute | solution.py:322
  15.4 4.6 %plan.1 = (s32[128]{0:T(128)}, s32[128]{0:T(128)}) custom-call(s32[128]{0:T(128)} %bitcast.88, s32[128]{0:T(128)} %bitcast.89), custom_call_target="tpu_custom_call" | custom-call | tf_op jit(solution)/shard_map/plan/pallas_call | solution.py:55
  22.1 2.9 %collective-permute-done.9 = bf16[8,128,128]{2,1,0:T(8,128)(2,1)S(1)} collective-permute-done((bf16[8,128,128]{2,1,0:T(8,128)(2,1)}, bf16[8,128,128]{2,1,0:T(8,128)(2,1)S(1)}, u32[]{:S(2)}, u32[]{:S(2)}) %collective-permute-start.9) | collective-permute-done | bytes 262176 | tf_op jit(solution)/shard_map/ppermute | solution.py:326
  27.6 2.2 %collective-permute-start.3 = (bf16[2,8,128,128]{3,2,1,0:T(8,128)(2,1)S(1)}, bf16[2,8,128,128]{3,2,1,0:T(8,128)(2,1)S(1)}, u32[]{:S(2)}, u32[]{:S(2)}) collective-permute-start(bf16[2,8,128,128]{3,2,1,0:T(8,128)(2,1)S(1)} %pad_maximum_fusion.1.refs_1_.refs_0_), channel_id=1, source_target_pairs={{0,64},{8,72},{16,80},{24,88},{32,96},{40,104},{48,112},{56,120},{... | collective-permute-start | bytes 1572872 | tf_op jit(solution)/shard_map/ppermute | solution.py:326
  29.9 10.1 %collective-permute-done.12.refs_12_.refs_4_ = bf16[2,8,128,128]{3,2,1,0:T(8,128)(2,1)S(1)} collective-permute-done((bf16[2,8,128,128]{3,2,1,0:T(8,128)(2,1)S(1)}, bf16[2,8,128,128]{3,2,1,0:T(8,128)(2,1)S(1)}, u32[]{:S(2)}, u32[]{:S(2)}) %collective-permute-start.12) | collective-permute-done | bytes 524320 | tf_op jit(solution)/shard_map/ppermute | solution.py:322
  39.9 2.6 %collective-permute-start.2 = (bf16[2,8,128,128]{3,2,1,0:T(8,128)(2,1)S(1)}, bf16[2,8,128,128]{3,2,1,0:T(8,128)(2,1)S(1)}, u32[]{:S(2)}, u32[]{:S(2)}) collective-permute-start(bf16[2,8,128,128]{3,2,1,0:T(8,128)(2,1)S(1)} %pad_maximum_fusion.1.refs_1_.refs_0_), channel_id=1, source_target_pairs={{0,96},{8,104},{16,112},{24,120},{32,0},{40,8},{48,16},{56,24},{64... | collective-permute-start | bytes 1572872 | tf_op jit(solution)/shard_map/ppermute | solution.py:326
  42.6 8.1 %collective-permute-done.11.refs_11_.refs_3_ = bf16[2,8,128,128]{3,2,1,0:T(8,128)(2,1)S(1)} collective-permute-done((bf16[2,8,128,128]{3,2,1,0:T(8,128)(2,1)S(1)}, bf16[2,8,128,128]{3,2,1,0:T(8,128)(2,1)S(1)}, u32[]{:S(2)}, u32[]{:S(2)}) %collective-permute-start.11) | collective-permute-done | bytes 524320 | tf_op jit(solution)/shard_map/ppermute | solution.py:322
  51.3 3.3 %collective-permute-done.2.refs_3_.refs_2_ = bf16[2,8,128,128]{3,2,1,0:T(8,128)(2,1)S(1)} collective-permute-done((bf16[2,8,128,128]{3,2,1,0:T(8,128)(2,1)S(1)}, bf16[2,8,128,128]{3,2,1,0:T(8,128)(2,1)S(1)}, u32[]{:S(2)}, u32[]{:S(2)}) %collective-permute-start.2) | collective-permute-done | bytes 524320 | tf_op jit(solution)/shard_map/ppermute | solution.py:326
  54.6 2.0 %collective-permute-done.1.refs_2_.refs_1_ = bf16[2,8,128,128]{3,2,1,0:T(8,128)(2,1)S(1)} collective-permute-done((bf16[2,8,128,128]{3,2,1,0:T(8,128)(2,1)S(1)}, bf16[2,8,128,128]{3,2,1,0:T(8,128)(2,1)S(1)}, u32[]{:S(2)}, u32[]{:S(2)}) %collective-permute-start.1) | collective-permute-done | bytes 524320 | tf_op jit(solution)/shard_map/ppermute | solution.py:326
  59.9 8.2 %all-gather.3.cloned.1.call-done = bf16[16,128,1024]{2,1,0:T(8,128)(2,1)} async-done(((bf16[2,128,1024]{2,1,0:T(8,128)(2,1)}), bf16[16,128,1024]{2,1,0:T(8,128)(2,1)}) %all-gather.3.cloned.1.call-update) | async-done | bytes 4194320 | tf_op jit(solution)/shard_map/all_gather | solution.py:381
  68.1 11.2 %forward.1 = (bf16[16,128,128]{2,1,0:T(8,128)(2,1)}, f32[16,128,128]{2,1,0:T(8,128)}, bf16[8,128,1024]{2,1,0:T(8,128)(2,1)}) custom-call(s32[128]{0:T(128)} %get-tuple-element.34.up_order.order, s32[128]{0:T(128)} %bitcast.82, s32[128]{0:T(128)} %get-tuple-element.35.down_order, s32[128]{0:T(128)} %bitcast.85, s32[4]{0:T(128)} %pad_add_fusion.pos, ...), custom_call_target="tpu_custom_call" | custom-call | flops 10000000 | bytes 100000 | tf_op jit(solution)/shard_map/forward/pallas_call | solution.py:102
  79.4 15.4 %backward.1 = (bf16[16,128,128]{2,1,0:T(8,128)(2,1)}, bf16[1,4,8,128,128]{4,3,2,1,0:T(8,128)(2,1)}, bf16[1,4,8,128,128]{4,3,2,1,0:T(8,128)(2,1)}, bf16[2,4,8,128...) custom-call(s32[128]{0:T(128)} %get-tuple-element.35.down_order, ...), custom_call_target="tpu_custom_call" | custom-call | flops 10000000 | bytes 100000 | tf_op jit(solution)/shard_map/backward/pallas_call | solution.py:102
  105.5 8.2 %input_part.1 = (bf16[128,1024]{1,0:T(8,128)(2,1)}, bf16[128,1024]{1,0:T(8,128)(2,1)}, bf16[6,128,1024]{2,1,0:T(8,128)(2,1)}) custom-call(s32[128]{0:T(128)} %get-tuple-element.34.up_order.order, s32[128]{0:T(128)} %bitcast.84, s32[4]{0:T(128)} %pad_add_fusion.pos, bf16[2,8,128,128]{3,2,1,0:T(8,128)(2,1)} %copy-done.2, bf16[2,8,128,128]{3,2,1,0:T(8,128)(2,1)} %copy-done.13, ...), custom_call_target="tpu_custom_call" | custom-call | flops 10000000 | bytes 100000 | tf_op jit(solution)/shard_map/input_part/pallas_call | solution.py:102
  113.6 4.0 %collective-permute-done.20 = bf16[2,8,128,128]{3,2,1,0:T(8,128)(2,1)S(1)} collective-permute-done((bf16[2,8,128,128]{3,2,1,0:T(8,128)(2,1)}, bf16[2,8,128,128]{3,2,1,0:T(8,128)(2,1)S(1)}, u32[]{:S(2)}, u32[]{:S(2)}) %collective-permute-start.20) | collective-permute-done | bytes 524320 | tf_op jit(solution)/shard_map/ppermute | solution.py:326
  119.4 3.2 %collective-permute-start.23 = (bf16[128,1024]{1,0:T(8,128)(2,1)}, bf16[128,1024]{1,0:T(8,128)(2,1)S(1)}, u32[]{:S(2)}, u32[]{:S(2)}) collective-permute-start(bf16[128,1024]{1,0:T(8,128)(2,1)} %get-tuple-element.53), channel_id=1, source_target_pairs={{0,7},{1,0},{2,1},{3,2},{4,3},{5,4},{6,5},{7,6},{8,15},{9,8},{10,9... | collective-permute-start | bytes 786440 | tf_op jit(solution)/shard_map/ppermute | solution.py:338
  122.7 2.1 %collective-permute-done.25 = bf16[4,8,128,128]{3,2,1,0:T(8,128)(2,1)} collective-permute-done((bf16[4,8,128,128]{3,2,1,0:T(8,128)(2,1)S(1)}, bf16[4,8,128,128]{3,2,1,0:T(8,128)(2,1)}, u32[]{:S(2)}, u32[]{:S(2)}) %collective-permute-start.25) | collective-permute-done | bytes 1048608 | tf_op jit(solution)/shard_map/ppermute | solution.py:322
  131.1 2.0 %fusion.11 = (bf16[128,1024]{1,0:T(8,128)(2,1)}, bf16[128,1024]{1,0:T(8,128)(2,1)}) fusion(bf16[128,1024]{1,0:T(8,128)(2,1)S(1)} %collective-permute-done.23, bf16[6,128,1024]{2,1,0:T(8,128)(2,1)} %get-tuple-element.49, bf16[128,1024]{1,0:T(8,128)(2,1)S(1)} %collective-permute-done.22), kind=kLoop, calls=%fused_computation.26 | loop fusion | flops 1048576 | bytes 1572864 | tf_op jit(solution)/shard_map/convert_element_type | solution.py:410
  134.1 2.4 %collective-permute-start.28 = (bf16[128,1024]{1,0:T(8,128)(2,1)}, bf16[128,1024]{1,0:T(8,128)(2,1)S(1)}, u32[]{:S(2)}, u32[]{:S(2)}) collective-permute-start(bf16[128,1024]{1,0:T(8,128)(2,1)} %get-tuple-element.59), channel_id=1, source_target_pairs={{0,7},{1,0},{2,1},{3,2},{4,3},{5,4},{6,5},{7,6},{8,15},{9,8},{10,9... | collective-permute-start | bytes 786440 | tf_op jit(solution)/shard_map/ppermute | solution.py:338
  142.7 2.2 %collective-permute-done.33 = bf16[8,128,128]{2,1,0:T(8,128)(2,1)S(1)} collective-permute-done((bf16[8,128,128]{2,1,0:T(8,128)(2,1)S(1)}, bf16[8,128,128]{2,1,0:T(8,128)(2,1)S(1)}, u32[]{:S(2)}, u32[]{:S(2)}) %collective-permute-start.33) | collective-permute-done | bytes 262176 | tf_op jit(solution)/shard_map/ppermute | solution.py:322
  145.0 3.8 %collective-permute-start.37 = (bf16[8,128,128]{2,1,0:T(8,128)(2,1)S(1)}, bf16[8,128,128]{2,1,0:T(8,128)(2,1)S(1)}, u32[]{:S(2)}, u32[]{:S(2)}) collective-permute-start(bf16[8,128,128]{2,1,0:T(8,128)(2,1)S(1)} %fusion.7), channel_id=1, source_target_pairs={{0,128},{128,0},{1,129},{129,1},{2,130},{130,2},{3,131},{131,3},{4... | collective-permute-start | bytes 786440 | tf_op jit(solution)/shard_map/ppermute | solution.py:330
  148.8 2.3 %collective-permute-start.32 = (bf16[128,1024]{1,0:T(8,128)(2,1)S(1)}, bf16[128,1024]{1,0:T(8,128)(2,1)S(1)}, u32[]{:S(2)}, u32[]{:S(2)}) collective-permute-start(bf16[128,1024]{1,0:T(8,128)(2,1)S(1)} %get-tuple-element.61), channel_id=1, source_target_pairs={{0,7},{1,0},{2,1},{3,2},{4,3},{5,4},{6,5},{7,6},{8,15},{9,8},{10,9... | collective-permute-start | bytes 786440 | tf_op jit(solution)/shard_map/ppermute | solution.py:338
  152.4 2.8 %collective-permute-done.32 = bf16[128,1024]{1,0:T(8,128)(2,1)S(1)} collective-permute-done((bf16[128,1024]{1,0:T(8,128)(2,1)S(1)}, bf16[128,1024]{1,0:T(8,128)(2,1)S(1)}, u32[]{:S(2)}, u32[]{:S(2)}) %collective-permute-start.32) | collective-permute-done | bytes 262176 | tf_op jit(solution)/shard_map/ppermute | solution.py:338
  156.2 3.9 %collective-permute-done.36 = bf16[8,128,128]{2,1,0:T(8,128)(2,1)S(1)} collective-permute-done((bf16[8,128,128]{2,1,0:T(8,128)(2,1)S(1)}, bf16[8,128,128]{2,1,0:T(8,128)(2,1)S(1)}, u32[]{:S(2)}, u32[]{:S(2)}) %collective-permute-start.36) | collective-permute-done | bytes 262176 | tf_op jit(solution)/shard_map/ppermute | solution.py:330
  160.9 2.0 %collective-permute-done.35 = bf16[128,1024]{1,0:T(8,128)(2,1)S(1)} collective-permute-done((bf16[128,1024]{1,0:T(8,128)(2,1)S(1)}, bf16[128,1024]{1,0:T(8,128)(2,1)S(1)}, u32[]{:S(2)}, u32[]{:S(2)}) %collective-permute-start.35) | collective-permute-done | bytes 262176 | tf_op jit(solution)/shard_map/ppermute | solution.py:334
  (125 shorter events, 44.6 us)
Async XLA Ops:
  7.2 60.9 %all-gather.3.cloned.1.call-start = ((), (), s32[]{:S(2)}) async-start(), calls=%async_computation.2 | async-start | bytes 4718592 | tf_op jit(solution)/shard_map/all_gather | solution.py:381
  9.2 124.0 %reduce-scatter.2.cloned.1.call-start = ((), (), s32[]{:S(2)}) async-start(), calls=%async_computation.1 | async-start | bytes 2359296 | tf_op jit(solution)/shard_map/reduce_scatter | solution.py:369
  9.2 10.8 %collective-permute-start = (bf16[8,128,128]{2,1,0:T(8,128)(2,1)}, bf16[8,128,128]{2,1,0:T(8,128)(2,1)S(1)}, u32[]{:S(2)}, u32[]{:S(2)}) collective-permute-start(bf16[8,128,128]{2,1,0:T(8,128)(2,1)} %param.10), channel_id=1, source_target_pairs={{0,16},{8,24},{16,0},{24,8},{32,48},{40,56},{48,32},{56,40},{64,80... | collective-permute-start | bytes 786440 | tf_op jit(solution)/shard_map/ppermute | solution.py:322
  11.5 10.6 %collective-permute-start.10 = (bf16[8,128,128]{2,1,0:T(8,128)(2,1)}, bf16[8,128,128]{2,1,0:T(8,128)(2,1)S(1)}, u32[]{:S(2)}, u32[]{:S(2)}) collective-permute-start(bf16[8,128,128]{2,1,0:T(8,128)(2,1)} %param.11), channel_id=1, source_target_pairs={{0,64},{8,72},{16,80},{24,88},{32,96},{40,104},{48,112},{56,120},{... | collective-permute-start | bytes 786440 | tf_op jit(solution)/shard_map/ppermute | solution.py:326
  12.8 12.2 %collective-permute-start.9 = (bf16[8,128,128]{2,1,0:T(8,128)(2,1)}, bf16[8,128,128]{2,1,0:T(8,128)(2,1)S(1)}, u32[]{:S(2)}, u32[]{:S(2)}) collective-permute-start(bf16[8,128,128]{2,1,0:T(8,128)(2,1)} %param.11), channel_id=1, source_target_pairs={{0,96},{8,104},{16,112},{24,120},{32,0},{40,8},{48,16},{56,24},{64... | collective-permute-start | bytes 786440 | tf_op jit(solution)/shard_map/ppermute | solution.py:326
  13.9 12.9 %collective-permute-start.8 = (bf16[8,128,128]{2,1,0:T(8,128)(2,1)}, bf16[8,128,128]{2,1,0:T(8,128)(2,1)S(1)}, u32[]{:S(2)}, u32[]{:S(2)}) collective-permute-start(bf16[8,128,128]{2,1,0:T(8,128)(2,1)} %param.11), channel_id=1, source_target_pairs={{0,32},{8,40},{16,48},{24,56},{32,64},{40,72},{48,80},{56,88},{64,... | collective-permute-start | bytes 786440 | tf_op jit(solution)/shard_map/ppermute | solution.py:326
  25.1 14.8 %collective-permute-start.12 = (bf16[2,8,128,128]{3,2,1,0:T(8,128)(2,1)S(1)}, bf16[2,8,128,128]{3,2,1,0:T(8,128)(2,1)S(1)}, u32[]{:S(2)}, u32[]{:S(2)}) collective-permute-start(bf16[2,8,128,128]{3,2,1,0:T(8,128)(2,1)S(1)} %pad_maximum_fusion.3.refs_10_.refs_2_), channel_id=1, source_target_pairs={{0,16},{8,24},{16,0},{24,8},{32,48},{40,56},{48,32},{56,40},{64,80... | collective-permute-start | bytes 1572872 | tf_op jit(solution)/shard_map/ppermute | solution.py:322
  26.9 15.7 %collective-permute-start.13 = (bf16[2,8,128,128]{3,2,1,0:T(8,128)(2,1)S(1)}, bf16[2,8,128,128]{3,2,1,0:T(8,128)(2,1)S(1)}, u32[]{:S(2)}, u32[]{:S(2)}) collective-permute-start(bf16[2,8,128,128]{3,2,1,0:T(8,128)(2,1)S(1)} %pad_maximum_fusion.2.refs_9_.refs_1_), channel_id=1, source_target_pairs={{0,8},{8,0},{16,24},{24,16},{32,40},{40,32},{48,56},{56,48},{64,72... | collective-permute-start | bytes 1572872 | tf_op jit(solution)/shard_map/ppermute | solution.py:318
  27.1 23.6 %collective-permute-start.11 = (bf16[2,8,128,128]{3,2,1,0:T(8,128)(2,1)S(1)}, bf16[2,8,128,128]{3,2,1,0:T(8,128)(2,1)S(1)}, u32[]{:S(2)}, u32[]{:S(2)}) collective-permute-start(bf16[2,8,128,128]{3,2,1,0:T(8,128)(2,1)S(1)} %pad_maximum_fusion.2.refs_9_.refs_1_), channel_id=1, source_target_pairs={{0,16},{8,24},{16,0},{24,8},{32,48},{40,56},{48,32},{56,40},{64,80... | collective-permute-start | bytes 1572872 | tf_op jit(solution)/shard_map/ppermute | solution.py:322
  27.6 23.2 %collective-permute-start.4 = (bf16[2,8,128,128]{3,2,1,0:T(8,128)(2,1)S(1)}, bf16[2,8,128,128]{3,2,1,0:T(8,128)(2,1)}, u32[]{:S(2)}, u32[]{:S(2)}) collective-permute-start(bf16[2,8,128,128]{3,2,1,0:T(8,128)(2,1)S(1)} %pad_maximum_fusion.1.refs_1_.refs_0_), channel_id=1, source_target_pairs={{0,8},{8,0},{16,24},{24,16},{32,40},{40,32},{48,56},{56,48},{64,72... | collective-permute-start | bytes 1572872 | tf_op jit(solution)/shard_map/ppermute | solution.py:318
  27.6 23.6 %collective-permute-start.3 = (bf16[2,8,128,128]{3,2,1,0:T(8,128)(2,1)S(1)}, bf16[2,8,128,128]{3,2,1,0:T(8,128)(2,1)S(1)}, u32[]{:S(2)}, u32[]{:S(2)}) collective-permute-start(bf16[2,8,128,128]{3,2,1,0:T(8,128)(2,1)S(1)} %pad_maximum_fusion.1.refs_1_.refs_0_), channel_id=1, source_target_pairs={{0,64},{8,72},{16,80},{24,88},{32,96},{40,104},{48,112},{56,120},{... | collective-permute-start | bytes 1572872 | tf_op jit(solution)/shard_map/ppermute | solution.py:326
  39.9 14.7 %collective-permute-start.2 = (bf16[2,8,128,128]{3,2,1,0:T(8,128)(2,1)S(1)}, bf16[2,8,128,128]{3,2,1,0:T(8,128)(2,1)S(1)}, u32[]{:S(2)}, u32[]{:S(2)}) collective-permute-start(bf16[2,8,128,128]{3,2,1,0:T(8,128)(2,1)S(1)} %pad_maximum_fusion.1.refs_1_.refs_0_), channel_id=1, source_target_pairs={{0,96},{8,104},{16,112},{24,120},{32,0},{40,8},{48,16},{56,24},{64... | collective-permute-start | bytes 1572872 | tf_op jit(solution)/shard_map/ppermute | solution.py:326
  42.6 14.0 %collective-permute-start.1 = (bf16[2,8,128,128]{3,2,1,0:T(8,128)(2,1)S(1)}, bf16[2,8,128,128]{3,2,1,0:T(8,128)(2,1)S(1)}, u32[]{:S(2)}, u32[]{:S(2)}) collective-permute-start(bf16[2,8,128,128]{3,2,1,0:T(8,128)(2,1)S(1)} %pad_maximum_fusion.1.refs_1_.refs_0_), channel_id=1, source_target_pairs={{0,32},{8,40},{16,48},{24,56},{32,64},{40,72},{48,80},{56,88},{64,... | collective-permute-start | bytes 1572872 | tf_op jit(solution)/shard_map/ppermute | solution.py:326
  95.5 27.2 %collective-permute-start.24 = (bf16[1,4,8,128,128]{4,3,2,1,0:T(8,128)(2,1)}, bf16[1,4,8,128,128]{4,3,2,1,0:T(8,128)(2,1)S(1)}, u32[]{:S(2)}, u32[]{:S(2)}) collective-permute-start(bf16[1,4,8,128,128]{4,3,2,1,0:T(8,128)(2,1)} %get-tuple-element.54), channel_id=1, source_target_pairs={{0,8},{8,0},{16,24},{24,16},{32,40},{40,32},{48,56},{56,48},{64,72... | collective-permute-start | bytes 3145736 | tf_op jit(solution)/shard_map/ppermute | solution.py:318
  99.3 25.4 %collective-permute-start.25 = (bf16[4,8,128,128]{3,2,1,0:T(8,128)(2,1)S(1)}, bf16[4,8,128,128]{3,2,1,0:T(8,128)(2,1)}, u32[]{:S(2)}, u32[]{:S(2)}) collective-permute-start(bf16[4,8,128,128]{3,2,1,0:T(8,128)(2,1)S(1)} %fusion.1), channel_id=1, source_target_pairs={{0,16},{8,24},{16,0},{24,8},{32,48},{40,56},{48,32},{56,40},{64,80... | collective-permute-start | bytes 3145736 | tf_op jit(solution)/shard_map/ppermute | solution.py:322
  102.2 15.4 %collective-permute-start.20 = (bf16[2,8,128,128]{3,2,1,0:T(8,128)(2,1)}, bf16[2,8,128,128]{3,2,1,0:T(8,128)(2,1)S(1)}, u32[]{:S(2)}, u32[]{:S(2)}) collective-permute-start(bf16[2,8,128,128]{3,2,1,0:T(8,128)(2,1)} %get-tuple-element.65), channel_id=1, source_target_pairs={{0,32},{8,40},{16,48},{24,56},{32,64},{40,72},{48,80},{56,88},{64,... | collective-permute-start | bytes 1572872 | tf_op jit(solution)/shard_map/ppermute | solution.py:326
  103.7 15.7 %collective-permute-start.21 = (bf16[2,8,128,128]{3,2,1,0:T(8,128)(2,1)S(1)}, bf16[2,8,128,128]{3,2,1,0:T(8,128)(2,1)S(1)}, u32[]{:S(2)}, u32[]{:S(2)}) collective-permute-start(bf16[2,8,128,128]{3,2,1,0:T(8,128)(2,1)S(1)} %get-tuple-element.66), channel_id=1, source_target_pairs={{0,96},{8,104},{16,112},{24,120},{32,0},{40,8},{48,16},{56,24},{64... | collective-permute-start | bytes 1572872 | tf_op jit(solution)/shard_map/ppermute | solution.py:326
  117.6 15.5 %collective-permute-start.26 = (bf16[2,8,128,128]{3,2,1,0:T(8,128)(2,1)}, bf16[2,8,128,128]{3,2,1,0:T(8,128)(2,1)}, u32[]{:S(2)}, u32[]{:S(2)}) collective-permute-start(bf16[2,8,128,128]{3,2,1,0:T(8,128)(2,1)} %get-tuple-element.57), channel_id=1, source_target_pairs={{0,64},{8,72},{16,80},{24,88},{32,96},{40,104},{48,112},{56,120},{... | collective-permute-start | bytes 1572872 | tf_op jit(solution)/shard_map/ppermute | solution.py:326
  119.4 8.8 %collective-permute-start.22 = (bf16[128,1024]{1,0:T(8,128)(2,1)}, bf16[128,1024]{1,0:T(8,128)(2,1)S(1)}, u32[]{:S(2)}, u32[]{:S(2)}) collective-permute-start(bf16[128,1024]{1,0:T(8,128)(2,1)} %get-tuple-element.52), channel_id=1, source_target_pairs={{0,1},{1,2},{2,3},{3,4},{4,5},{5,6},{6,7},{7,0},{8,9},{9,10},{10,1... | collective-permute-start | bytes 786440 | tf_op jit(solution)/shard_map/ppermute | solution.py:334
  119.4 8.8 %collective-permute-start.23 = (bf16[128,1024]{1,0:T(8,128)(2,1)}, bf16[128,1024]{1,0:T(8,128)(2,1)S(1)}, u32[]{:S(2)}, u32[]{:S(2)}) collective-permute-start(bf16[128,1024]{1,0:T(8,128)(2,1)} %get-tuple-element.53), channel_id=1, source_target_pairs={{0,7},{1,0},{2,1},{3,2},{4,3},{5,4},{6,5},{7,6},{8,15},{9,8},{10,9... | collective-permute-start | bytes 786440 | tf_op jit(solution)/shard_map/ppermute | solution.py:338
  129.1 12.1 %collective-permute-start.30 = (bf16[8,128,128]{2,1,0:T(8,128)(2,1)}, bf16[8,128,128]{2,1,0:T(8,128)(2,1)S(1)}, u32[]{:S(2)}, u32[]{:S(2)}) collective-permute-start(bf16[8,128,128]{2,1,0:T(8,128)(2,1)} %get-tuple-element.72), channel_id=1, source_target_pairs={{0,96},{8,104},{16,112},{24,120},{32,0},{40,8},{48,16},{56,24},{64... | collective-permute-start | bytes 786440 | tf_op jit(solution)/shard_map/ppermute | solution.py:326
  138.9 12.2 %collective-permute-start.34 = (bf16[8,128,128]{2,1,0:T(8,128)(2,1)S(1)}, bf16[8,128,128]{2,1,0:T(8,128)(2,1)S(1)}, u32[]{:S(2)}, u32[]{:S(2)}) collective-permute-start(bf16[8,128,128]{2,1,0:T(8,128)(2,1)S(1)} %copy-done.21), channel_id=1, source_target_pairs={{0,64},{8,72},{16,80},{24,88},{32,96},{40,104},{48,112},{56,120},{... | collective-permute-start | bytes 786440 | tf_op jit(solution)/shard_map/ppermute | solution.py:326
  141.2 11.1 %collective-permute-start.31 = (bf16[128,1024]{1,0:T(8,128)(2,1)S(1)}, bf16[128,1024]{1,0:T(8,128)(2,1)S(1)}, u32[]{:S(2)}, u32[]{:S(2)}) collective-permute-start(bf16[128,1024]{1,0:T(8,128)(2,1)S(1)} %get-tuple-element.60), channel_id=1, source_target_pairs={{0,1},{1,2},{2,3},{3,4},{4,5},{5,6},{6,7},{7,0},{8,9},{9,10},{10,1... | collective-permute-start | bytes 786440 | tf_op jit(solution)/shard_map/ppermute | solution.py:334
  145.0 10.3 %collective-permute-start.37 = (bf16[8,128,128]{2,1,0:T(8,128)(2,1)S(1)}, bf16[8,128,128]{2,1,0:T(8,128)(2,1)S(1)}, u32[]{:S(2)}, u32[]{:S(2)}) collective-permute-start(bf16[8,128,128]{2,1,0:T(8,128)(2,1)S(1)} %fusion.7), channel_id=1, source_target_pairs={{0,128},{128,0},{1,129},{129,1},{2,130},{130,2},{3,131},{131,3},{4... | collective-permute-start | bytes 786440 | tf_op jit(solution)/shard_map/ppermute | solution.py:330
  (38 other events, 412.4 us)
Sparse Core Ops, SparseCore 0:
  10.4 57.6 all-gather.2
  79.5 40.7 reduce-scatter.1

commit v2 on v1

--- a/solution.py
+++ b/solution.py
@@ -132,53 +132,11 @@
         acc[at] += term[:, k * B : (k + 1) * B]
 
 
-def forward(up_order, rows, down_order, cols, pos, x, up, down):
-    def kernel(up_order, rows, down_order, cols, pos, *refs):
-        nx, nu, nd = len(x.arrays), len(up.arrays), len(down.arrays)
-        x_refs, u_refs, d_refs = refs[:nx], refs[nx : nx + nu], refs[nx + nu : nx + nu + nd]
-        hidden, slope, out, xbuf, ubuf, dbuf, acc, sems = refs[nx + nu + nd :]
-        first = wide_copies(x.places, x_refs, pos, xbuf, sems, 0)
-        first += tile_copies(up.places, u_refs, pos, ubuf, sems, len(first))
-        later = tile_copies(down.places, d_refs, pos, dbuf, sems, len(first))
-        start(first)
-        start(later)
-        acc[...] = jnp.zeros_like(acc)
-        finish(first)
-
-        def step(h, carry):
-            lhs = far_blocks(xbuf, rows, up_order, h)
-            rhs = jnp.concatenate([ubuf[up_order[h * K + k]] for k in range(K)], axis=0)
-            act, der = gelu_parts(dot(lhs, rhs, (1, 0)))
-            hidden[h] = act.astype(BF)
-            slope[h] = der
-            return carry
-
-        lax.fori_loop(0, H, step, 0, unroll=UNROLL)
-        finish(later)
-
-        def spread_step(h, carry):
-            js = [down_order[h * K + k] for k in range(K)]
-            rhs = jnp.concatenate([dbuf[j] for j in js], axis=1)
-            add_far(acc, cols, js, dot(hidden[h], rhs, (1, 0)))
-            return carry
-
-        lax.fori_loop(0, H, spread_step, 0, unroll=UNROLL)
-        out[...] = acc[...].astype(BF)
-
-    n = len(x.places) + len(up.places) + len(down.places)
-    return call(
-        kernel,
-        (
-            jax.ShapeDtypeStruct((H, B, B), BF),
-            jax.ShapeDtypeStruct((H, B, B), F32),
-            jax.ShapeDtypeStruct((8, B, 8 * B), BF),
-        ),
-        (up_order, rows, down_order, cols, pos),
-        (*x.arrays, *up.arrays, *down.arrays),
-        (),
-        [WIDE, TILES, TILES, WIDE_ACC, pltpu.SemaphoreType.DMA((n,))],
-        name="forward",
-    )
+def add_far(acc, far, js, term):
+    for k, j in enumerate(js):
+        f = far[j]
+        at = (f >> 3, slice(None), pl.ds(pl.multiple_of((f & 7) * B, B), B))
+        acc[at] += term[:, k * B : (k + 1) * B]
 
 
 def grad_shapes(x_first):
@@ -206,38 +164,55 @@
     ]
 
 
-def backward(down_order, cols, up_order, rows, pos, hidden, slope, cot, w, x):
+RING = (0, 1, 2, 3, 6, 7)
+
+
+def tile_pass(up_order, rows, down_order, cols, pos, x, cot, up, down):
     up_shapes, down_shapes = grad_shapes(False), grad_shapes(True)
-
-    def kernel(down_order, cols, up_order, rows, pos, *refs):
-        nc, nw, nx = len(cot.arrays), len(w.arrays), len(x.arrays)
-        c_refs, w_refs, x_refs = refs[:nc], refs[nc : nc + nw], refs[nc + nw : nc + nw + nx]
-        hidden, slope, pre = refs[nc + nw + nx : nc + nw + nx + 3]
-        ups, downs = refs[nc + nw + nx + 3 : -6][:3], refs[nc + nw + nx + 3 : -6][3:]
-        cbuf, wbuf, xbuf, up_terms, down_terms, sems = refs[-6:]
-        first = wide_copies(cot.places, c_refs, pos, cbuf, sems, 0)
-        first += tile_copies(w.places, w_refs, pos, wbuf, sems, len(first))
-        later = wide_copies(x.places, x_refs, pos, xbuf, sems, len(first))
+    groups = (x.arrays, up.arrays, cot.arrays, down.arrays)
+    counts = [len(g) for g in groups]
+
+    def kernel(up_order, rows, down_order, cols, pos, *refs):
+        ins, refs = refs[: sum(counts)], refs[sum(counts) :]
+        x_refs, u_refs = ins[: counts[0]], ins[counts[0] : sum(counts[:2])]
+        c_refs, d_refs = ins[sum(counts[:2]) : sum(counts[:3])], ins[sum(counts[:3]) :]
+        ups, downs, (ring_up, ring_down, rest, out), scratch = refs[:3], refs[3:6], refs[6:10], refs[10:]
+        xbuf, ubuf, cbuf, dbuf, hidden, slope, pre, up_terms, down_terms, acc, sems = scratch
+        first = wide_copies(x.places, x_refs, pos, xbuf, sems, 0)
+        first += tile_copies(up.places, u_refs, pos, ubuf, sems, len(first))
+        later = wide_copies(cot.places, c_refs, pos, cbuf, sems, len(first))
+        later += tile_copies(down.places, d_refs, pos, dbuf, sems, len(first) + len(later))
         n = len(first) + len(later)
         start(first)
         start(later)
+        acc[...] = jnp.zeros_like(acc)
         finish(first)
 
-        def step(h, carry):
+        def forward(h, carry):
+            lhs = far_blocks(xbuf, rows, up_order, h)
+            rhs = jnp.concatenate([ubuf[up_order[h * K + k]] for k in range(K)], axis=0)
+            act, der = gelu_parts(dot(lhs, rhs, (1, 0)))
+            hidden[h] = act.astype(BF)
+            slope[h] = der
+            return carry
+
+        lax.fori_loop(0, H, forward, 0, unroll=UNROLL)
+        finish(later)
+
+        def backward(h, carry):
             lhs = far_blocks(cbuf, cols, down_order, h)
-            rhs = jnp.concatenate([wbuf[down_order[h * K + k]] for k in range(K)], axis=1)
+            rhs = jnp.concatenate([dbuf[down_order[h * K + k]] for k in range(K)], axis=1)
             pre[h] = (dot(lhs, rhs, (1, 1)) * slope[h]).astype(BF)
             return carry
 
-        lax.fori_loop(0, H, step, 0, unroll=UNROLL)
-        finish(later)
+        lax.fori_loop(0, H, backward, 0, unroll=UNROLL)
 
         def up_term(h, carry):
             lhs = far_blocks(xbuf, rows, up_order, h)
-            out = dot(lhs, pre[h], (0, 0)).astype(BF)
+            term = dot(lhs, pre[h], (0, 0)).astype(BF)
             for k in range(K):
                 at = grad_place(up_order[h * K + k], pos, False)
-                up_terms[at] = out[k * B : (k + 1) * B]
+                up_terms[at] = term[k * B : (k + 1) * B]
             return carry
 
         lax.fori_loop(0, H, up_term, 0, unroll=UNROLL)
@@ -245,73 +220,73 @@
         start(up_copies)
 
         def down_term(h, carry):
-            out = dot(hidden[h], far_blocks(cbuf, cols, down_order, h), (0, 0)).astype(BF)
+            term = dot(hidden[h], far_blocks(cbuf, cols, down_order, h), (0, 0)).astype(BF)
             for k in range(K):
                 at = grad_place(down_order[h * K + k], pos, True)
-                down_terms[at] = out[:, k * B : (k + 1) * B]
+                down_terms[at] = term[:, k * B : (k + 1) * B]
             return carry
 
         lax.fori_loop(0, H, down_term, 0, unroll=UNROLL)
         down_copies = grad_copies(down_terms, downs, sems, n + 3)
         start(down_copies)
+
+        def input_part(h, carry):
+            js = [up_order[h * K + k] for k in range(K)]
+            rhs = jnp.concatenate([ubuf[j] for j in js], axis=0)
+            add_far(acc, rows, js, dot(pre[h], rhs, (1, 1)))
+            return carry
+
+        lax.fori_loop(0, H, input_part, 0, unroll=UNROLL)
+        ring_up[...] = acc[(pos[0] + 4) & 7].astype(BF)
+        ring_down[...] = acc[(pos[0] + 5) & 7].astype(BF)
+        for i, r in enumerate(RING):
+            rest[i] = acc[(pos[0] + r) & 7].astype(BF)
+        acc[...] = jnp.zeros_like(acc)
+
+        def output_part(h, carry):
+            js = [down_order[h * K + k] for k in range(K)]
+            rhs = jnp.concatenate([dbuf[j] for j in js], axis=1)
+            add_far(acc, cols, js, dot(hidden[h], rhs, (1, 0)))
+            return carry
+
+        lax.fori_loop(0, H, output_part, 0, unroll=UNROLL)
+        out[...] = acc[...].astype(BF)
         finish(up_copies)
         finish(down_copies)
 
-    n = len(cot.places) + len(w.places) + len(x.places) + 6
-    out = call(
+    n = len(x.places) + len(up.places) + len(cot.places) + len(down.places) + 6
+    one = jax.ShapeDtypeStruct((B, 8 * B), BF)
+    hiddens = (H, B, B)
+    got = call(
         kernel,
-        [jax.ShapeDtypeStruct((H, B, B), BF)] + up_shapes + down_shapes,
-        (down_order, cols, up_order, rows, pos),
-        (*cot.arrays, *w.arrays, *x.arrays),
-        (hidden, slope),
+        [
+            *up_shapes,
+            *down_shapes,
+            one,
+            one,
+            jax.ShapeDtypeStruct((6, B, 8 * B), BF),
+            jax.ShapeDtypeStruct((8, B, 8 * B), BF),
+        ],
+        (up_order, rows, down_order, cols, pos),
+        sum(groups, ()),
+        (),
         [
             WIDE,
             TILES,
             WIDE,
+            TILES,
+            pltpu.VMEM(hiddens, BF),
+            pltpu.VMEM(hiddens, F32),
+            pltpu.VMEM(hiddens, BF),
             grad_scratch(False),
             grad_scratch(True),
+            WIDE_ACC,
             pltpu.SemaphoreType.DMA((n,)),
         ],
-        out_specs=(VMEM_SPEC,) + (ANY_SPEC,) * 6,
-        name="backward",
+        out_specs=(ANY_SPEC,) * 6 + (VMEM_SPEC,) * 4,
+        name="tile_pass",
     )
-    return out[0], out[1:4], out[4:]
-
-
-RING = (0, 1, 2, 3, 6, 7)
-
-
-def input_part(order, far, pos, act, w):
-    def kernel(order, far, pos, *refs):
-        nw = len(w.arrays)
-        act, up, down, rest, wbuf, acc, sems = refs[nw:]
-        copies = tile_copies(w.places, refs[:nw], pos, wbuf, sems, 0)
-        start(copies)
-        acc[...] = jnp.zeros_like(acc)
-        finish(copies)
-
-        def step(h, carry):
-            js = [order[h * K + k] for k in range(K)]
-            rhs = jnp.concatenate([wbuf[j] for j in js], axis=0)
-            add_far(acc, far, js, dot(act[h], rhs, (1, 1)))
-            return carry
-
-        lax.fori_loop(0, H, step, 0, unroll=UNROLL)
-        up[...] = acc[(pos[0] + 4) & 7].astype(BF)
-        down[...] = acc[(pos[0] + 5) & 7].astype(BF)
-        for n, r in enumerate(RING):
-            rest[n] = acc[(pos[0] + r) & 7].astype(BF)
-
-    one = jax.ShapeDtypeStruct((B, 8 * B), BF)
-    return call(
-        kernel,
-        [one, one, jax.ShapeDtypeStruct((6, B, 8 * B), BF)],
-        (order, far, pos),
-        w.arrays,
-        (act,),
-        [TILES, WIDE_ACC, pltpu.SemaphoreType.DMA((len(w.places),))],
-        name="input_part",
-    )
+    return got[:3], got[3:6], got[6:9], got[9]
 
 
 def core_swap(a):
@@ -384,42 +359,41 @@
     up = gather_up(up_tiles, up_order, down_order, pos)
     down = gather_down(down_tiles, up.arrays[0])
 
-    hidden, slope, partial_out = forward(up_order, rows, down_order, cols, pos, x, up, down)
+    (up0, up1, up_keep), (down12, down30, down_keep), ring_parts, partial_out = tile_pass(
+        up_order, rows, down_order, cols, pos, x, cot, up, down
+    )
     output = scatter_features(partial_out)
-    pre_grad, (up0, up1, up_keep), (down12, down30, down_keep) = backward(
-        down_order, cols, up_order, rows, pos, hidden, slope, cot, down, x
-    )
-    u1, u0 = core_swap(up1), core_swap(up0)
+    u1 = core_swap(up1)
     near = add(up_keep[1], u1[0]).astype(BF)
     u_y = y_swap(near)
     d12, d30 = core_swap(down12), core_swap(down30)
+    d12 = after(d12, near)
     t1, t2 = add(down_keep[0], d12[0]).astype(BF), add(down_keep[1], d12[1]).astype(BF)
     d_x1 = x_shift(t1, 1)
     t3 = add(down_keep[2], d30[0]).astype(BF)
     d_x3 = x_shift(t3, 3)
-    pre_grad_b = after(pre_grad, near, t1, t3)
-    part4, part5, rest = input_part(up_order, rows, pos, pre_grad_b, up)
+    u0 = core_swap(after(up0, d_x1))
+    part4, part5, rest = ring_parts
 
     part = {r: rest[n] for n, r in enumerate(RING)}
-    part4, part5, _ = lax.optimization_barrier((part4, part5, (d_x1, d_x3)))
     z1, w1 = z_up(part4), z_down(part5)
     d_x2 = x_shift(after(t2, d_x1), 2)
     total = (add(up_keep[0], u0[0]) + u_y.astype(F32)).astype(BF)
     u_x1, u_x3 = x_shift(total[1], 1), x_shift(total[3], 3)
-    z1, w1, _ = lax.optimization_barrier((z1, w1, total))
+    z1, w1, _ = lax.optimization_barrier((z1, w1, near))
     z2, w2 = add(part[3], z1).astype(BF), add(part[6], w1).astype(BF)
-    z2, w2, _ = lax.optimization_barrier((z2, w2, (output, d_x2)))
+    z2, w2, _ = lax.optimization_barrier((z2, w2, (d_x2, total)))
     z2, w2 = z_up(z2), z_down(w2)
     own = add(down_keep[3], d30[1]) + add(d_x1, d_x3) + d_x2.astype(F32)
     d_y = y_swap(own[1].astype(BF))
-    u_x2 = x_shift(after(total[2], u_x1), 2)
+    u_x2 = x_shift(total[2], 2)
     z3, w3 = add(part[2], z2).astype(BF), add(part[7], w2).astype(BF)
     z3, w3, _ = lax.optimization_barrier((z3, w3, (u_x1, u_x3)))
     z3, w3 = z_up(z3), z_down(w3)
     down_mine = (own[0] + d_y.astype(F32)).astype(BF)
     d_dp = dp_swap(down_mine)
     up_mine = (total[0].astype(F32) + add(u_x1, u_x3) + u_x2.astype(F32)).astype(BF)
-    z4 = z_up(after(add(part[1], z3).astype(BF), w3, d_y, u_x2))
+    z4 = z_up(after(add(part[1], z3).astype(BF), w3, u_x2, output))
     u_dp = dp_swap(up_mine)
     input_grad = (part[0].astype(F32) + add(z4, w3)).astype(BF)
     return (output, input_grad, add(up_mine, u_dp), add(down_mine, d_dp))

time: 171 us -> 189 us (1.11)
  waiting for transfers between devices: 57.6 us -> 86.8 us
  Pallas kernels: 39.3 us -> 28.2 us
  starting transfers between devices: 38.8 us -> 44.2 us
  other arithmetic: 16.3 us -> 12.2 us
  local copies, waits for them, and re-layouts: 4.23 us -> 2.18 us
    ppermute x12, waiting for transfers between devices: 13.2 us -> 34.1 us  [x_shift(): return lax.ppermute(a, 'fsdp', [(i, (i + 4 * d) % 16) for i in range(16)])]
    pallas_call x3 -> x1, Pallas kernels: 34.7 us -> 23.6 us  [call(): pl.pallas_call(kernel, out_shape=tuple(out_shape), in_specs=[SMEM_SPEC] *...]
    ppermute x3, waiting for transfers between devices: 2.77 us -> 12.9 us  [z_down(): return lax.ppermute(a, 'tensor', [(i, (i + 7) % 8) for i in range(8)])]
    ppermute x12, starting transfers between devices: 16.9 us -> 24.9 us  [x_shift(): return lax.ppermute(a, 'fsdp', [(i, (i + 4 * d) % 16) for i in range(16)])]
    ppermute x5, waiting for transfers between devices: 22.5 us -> 18.2 us  [y_swap(): return lax.ppermute(a, 'fsdp', [(i, i ^ 2) for i in range(16)])]
    ppermute x4, starting transfers between devices: 2.36 us -> 0.44 us  [z_up(): return lax.ppermute(a, 'tensor', [(i, (i + 1) % 8) for i in range(8)])]
  transfers between devices with their start and end apart: 40 -> 40, of which waited for: 18 -> 17; matrix products, arithmetic and copies ran while one was open for 9% -> 5% of each run, Pallas kernels for 16% -> 2%
where the time goes in v2:
time: 189 us; the launch traced here: 188 us
  waiting for transfers between devices  86.8 us (46%)
  starting transfers between devices  44.2 us (23%)
  Pallas kernels  28.2 us (15%)
  between operations  14.4 us (8%)
  other arithmetic  12.2 us (6%)
  local copies, waits for them, and re-layouts  2.18 us (1%)
    ppermute x12, waiting for transfers between devices, x_shift(): return lax.ppermute(a, 'fsdp', [(i, (i + 4 * d) % 16) for i in range(16)])  34.1 us
    ppermute x12, starting transfers between devices, x_shift(): return lax.ppermute(a, 'fsdp', [(i, (i + 4 * d) % 16) for i in range(16)])  24.9 us
    pallas_call x1, Pallas kernels, call(): pl.pallas_call(kernel, out_shape=tuple(out_shape), in_specs=[SMEM_SPEC] *...  23.6 us
    ppermute x5, waiting for transfers between devices, y_swap(): return lax.ppermute(a, 'fsdp', [(i, i ^ 2) for i in range(16)])  18.2 us
    ppermute x3, waiting for transfers between devices, z_down(): return lax.ppermute(a, 'tensor', [(i, (i + 7) % 8) for i in range(8)])  12.9 us
    all_gather x1, waiting for transfers between devices, body(): lax.all_gather(jnp.stack([activations, cotangent]), 'tensor', axis=0, til...  9.38 us
    ppermute x3, starting transfers between devices, z_down(): return lax.ppermute(a, 'tensor', [(i, (i + 7) % 8) for i in range(8)])  7.81 us
    ppermute x5, starting transfers between devices, y_swap(): return lax.ppermute(a, 'fsdp', [(i, i ^ 2) for i in range(16)])  5.53 us
  transfers between devices with their start and end apart: 40, of which 17 were waited for; matrix products, arithmetic and copies ran while one was open for 5% of the time, Pallas kernels for 2%

profile of v2, /device:TPU:8, one launch (start us, length us, event | category | flops | bytes accessed | tf_op | source)
XLA Modules:
  0.0 187.9 jit_solution(16806913865257435424)
XLA Ops:
  9.2 2.3 %collective-permute-start = (bf16[8,128,128]{2,1,0:T(8,128)(2,1)}, bf16[8,128,128]{2,1,0:T(8,128)(2,1)S(1)}, u32[]{:S(2)}, u32[]{:S(2)}) collective-permute-start(bf16[8,128,128]{2,1,0:T(8,128)(2,1)} %param.10), channel_id=1, source_target_pairs={{0,16},{8,24},{16,0},{24,8},{32,48},{40,56},{48,32},{56,40},{64,80... | collective-permute-start | bytes 786440 | tf_op jit(solution)/shard_map/ppermute | solution.py:297
  15.4 4.6 %plan.1 = (s32[128]{0:T(128)}, s32[128]{0:T(128)}) custom-call(s32[128]{0:T(128)} %bitcast.84, s32[128]{0:T(128)} %bitcast.85), custom_call_target="tpu_custom_call" | custom-call | tf_op jit(solution)/shard_map/plan/pallas_call | solution.py:55
  22.1 2.9 %collective-permute-done.9 = bf16[8,128,128]{2,1,0:T(8,128)(2,1)S(1)} collective-permute-done((bf16[8,128,128]{2,1,0:T(8,128)(2,1)}, bf16[8,128,128]{2,1,0:T(8,128)(2,1)S(1)}, u32[]{:S(2)}, u32[]{:S(2)}) %collective-permute-start.9) | collective-permute-done | bytes 262176 | tf_op jit(solution)/shard_map/ppermute | solution.py:301
  27.6 2.2 %collective-permute-start.3 = (bf16[2,8,128,128]{3,2,1,0:T(8,128)(2,1)S(1)}, bf16[2,8,128,128]{3,2,1,0:T(8,128)(2,1)S(1)}, u32[]{:S(2)}, u32[]{:S(2)}) collective-permute-start(bf16[2,8,128,128]{3,2,1,0:T(8,128)(2,1)S(1)} %pad_maximum_fusion.1.refs_1_), channel_id=1, source_target_pairs={{0,64},{8,72},{16,80},{24,88},{32,96},{40,104},{48,112},{56,120},{... | collective-permute-start | bytes 1572872 | tf_op jit(solution)/shard_map/ppermute | solution.py:301
  29.9 10.1 %collective-permute-done.12.refs_13_ = bf16[2,8,128,128]{3,2,1,0:T(8,128)(2,1)S(1)} collective-permute-done((bf16[2,8,128,128]{3,2,1,0:T(8,128)(2,1)S(1)}, bf16[2,8,128,128]{3,2,1,0:T(8,128)(2,1)S(1)}, u32[]{:S(2)}, u32[]{:S(2)}) %collective-permute-start.12) | collective-permute-done | bytes 524320 | tf_op jit(solution)/shard_map/ppermute | solution.py:297
  39.9 2.6 %collective-permute-start.2 = (bf16[2,8,128,128]{3,2,1,0:T(8,128)(2,1)S(1)}, bf16[2,8,128,128]{3,2,1,0:T(8,128)(2,1)S(1)}, u32[]{:S(2)}, u32[]{:S(2)}) collective-permute-start(bf16[2,8,128,128]{3,2,1,0:T(8,128)(2,1)S(1)} %pad_maximum_fusion.1.refs_1_), channel_id=1, source_target_pairs={{0,96},{8,104},{16,112},{24,120},{32,0},{40,8},{48,16},{56,24},{64... | collective-permute-start | bytes 1572872 | tf_op jit(solution)/shard_map/ppermute | solution.py:301
  42.6 8.1 %collective-permute-done.11.refs_12_ = bf16[2,8,128,128]{3,2,1,0:T(8,128)(2,1)S(1)} collective-permute-done((bf16[2,8,128,128]{3,2,1,0:T(8,128)(2,1)S(1)}, bf16[2,8,128,128]{3,2,1,0:T(8,128)(2,1)S(1)}, u32[]{:S(2)}, u32[]{:S(2)}) %collective-permute-start.11) | collective-permute-done | bytes 524320 | tf_op jit(solution)/shard_map/ppermute | solution.py:297
  51.3 3.3 %collective-permute-done.2.refs_3_ = bf16[2,8,128,128]{3,2,1,0:T(8,128)(2,1)S(1)} collective-permute-done((bf16[2,8,128,128]{3,2,1,0:T(8,128)(2,1)S(1)}, bf16[2,8,128,128]{3,2,1,0:T(8,128)(2,1)S(1)}, u32[]{:S(2)}, u32[]{:S(2)}) %collective-permute-start.2) | collective-permute-done | bytes 524320 | tf_op jit(solution)/shard_map/ppermute | solution.py:301
  54.6 2.0 %collective-permute-done.1.refs_2_ = bf16[2,8,128,128]{3,2,1,0:T(8,128)(2,1)S(1)} collective-permute-done((bf16[2,8,128,128]{3,2,1,0:T(8,128)(2,1)S(1)}, bf16[2,8,128,128]{3,2,1,0:T(8,128)(2,1)S(1)}, u32[]{:S(2)}, u32[]{:S(2)}) %collective-permute-start.1) | collective-permute-done | bytes 524320 | tf_op jit(solution)/shard_map/ppermute | solution.py:301
  58.7 9.4 %all-gather.3.cloned.1.call-done = bf16[16,128,1024]{2,1,0:T(8,128)(2,1)} async-done(((bf16[2,128,1024]{2,1,0:T(8,128)(2,1)}), bf16[16,128,1024]{2,1,0:T(8,128)(2,1)}) %all-gather.3.cloned.1.call-update) | async-done | bytes 4194320 | tf_op jit(solution)/shard_map/all_gather | solution.py:356
  68.1 23.6 %tile_pass.1 = (bf16[1,4,8,128,128]{4,3,2,1,0:T(8,128)(2,1)}, bf16[1,4,8,128,128]{4,3,2,1,0:T(8,128)(2,1)}, bf16[2,4,8,128,128]{4,3,2,1,0:T(8,128)(2,1)}, bf16[2...) custom-call(s32[128]{0:T(128)} %get-tuple-element.29.up_order, ...), custom_call_target="tpu_custom_call" | custom-call | flops 10000000 | bytes 100000 | tf_op jit(solution)/shard_map/tile_pass/pallas_call | solution.py:102
  92.5 2.4 %collective-permute-done.19 = bf16[1,4,8,128,128]{4,3,2,1,0:T(8,128)(2,1)} collective-permute-done((bf16[1,4,8,128,128]{4,3,2,1,0:T(8,128)(2,1)}, bf16[1,4,8,128,128]{4,3,2,1,0:T(8,128)(2,1)}, u32[]{:S(2)}, u32[]{:S(2)}) %collective-permute-start.19) | collective-permute-done | bytes 1048608 | tf_op jit(solution)/shard_map/ppermute | solution.py:293
  97.9 1.9 %fusion.4 = (bf16[2,8,128,128]{3,2,1,0:T(8,128)(2,1)S(1)}, bf16[2,8,128,128]{3,2,1,0:T(8,128)(2,1)S(1)}, bf16[2,8,128,128]{3,2,1,0:T(8,128)(2,1)S(1)}) fusion(bf16[2,2,8,128,128]{4,3,2,1,0:T(8,128)(2,1)} %collective-permute-done.20, bf16[4,2,8,128,128]{4,3,2,1,0:T(8,128)(2,1)S(1)} %copy-done.1, bf16[2,2,8,128,128]{4,3,2,1,0:T(8,128)(2,1)S(1)} %collective-permute-done.34), kind=kLoop, calls=%fused_computation.10 | loop fusion | flops 3145728 | bytes 4718592 | tf_op jit(solution)/shard_map/convert_element_type | solution.py:371
  101.9 13.2 %collective-permute-done.21 = bf16[2,8,128,128]{3,2,1,0:T(8,128)(2,1)S(1)} collective-permute-done((bf16[2,8,128,128]{3,2,1,0:T(8,128)(2,1)S(1)}, bf16[2,8,128,128]{3,2,1,0:T(8,128)(2,1)S(1)}, u32[]{:S(2)}, u32[]{:S(2)}) %collective-permute-start.21) | collective-permute-done | bytes 524320 | tf_op jit(solution)/shard_map/ppermute | solution.py:301
  118.8 12.9 %collective-permute-done.18 = bf16[128,1024]{1,0:T(8,128)(2,1)S(1)} collective-permute-done((bf16[128,1024]{1,0:T(8,128)(2,1)S(1)}, bf16[128,1024]{1,0:T(8,128)(2,1)S(1)}, u32[]{:S(2)}, u32[]{:S(2)}) %collective-permute-start.18) | collective-permute-done | bytes 262176 | tf_op jit(solution)/shard_map/ppermute | solution.py:313
  133.4 3.2 %collective-permute-start.26 = (bf16[128,1024]{1,0:T(8,128)(2,1)S(1)}, bf16[128,1024]{1,0:T(8,128)(2,1)S(1)}, u32[]{:S(2)}, u32[]{:S(2)}) collective-permute-start(bf16[128,1024]{1,0:T(8,128)(2,1)S(1)} %get-tuple-element.49), channel_id=1, source_target_pairs={{0,7},{1,0},{2,1},{3,2},{4,3},{5,4},{6,5},{7,6},{8,15},{9,8},{10,9... | collective-permute-start | bytes 786440 | tf_op jit(solution)/shard_map/ppermute | solution.py:313
  136.7 11.3 %collective-permute-start.28 = (bf16[8,128,128]{2,1,0:T(8,128)(2,1)S(1)}, bf16[8,128,128]{2,1,0:T(8,128)(2,1)S(1)}, u32[]{:S(2)}, u32[]{:S(2)}) collective-permute-start(bf16[8,128,128]{2,1,0:T(8,128)(2,1)S(1)} %get-tuple-element.62), channel_id=1, source_target_pairs={{0,96},{8,104},{16,112},{24,120},{32,0},{40,8},{48,16},{56,24},{64... | collective-permute-start | bytes 786440 | tf_op jit(solution)/shard_map/ppermute | solution.py:301
  150.4 2.4 %collective-permute-done.28 = bf16[8,128,128]{2,1,0:T(8,128)(2,1)S(1)} collective-permute-done((bf16[8,128,128]{2,1,0:T(8,128)(2,1)S(1)}, bf16[8,128,128]{2,1,0:T(8,128)(2,1)S(1)}, u32[]{:S(2)}, u32[]{:S(2)}) %collective-permute-start.28) | collective-permute-done | bytes 262176 | tf_op jit(solution)/shard_map/ppermute | solution.py:301
  152.9 9.0 %collective-permute-done.27 = bf16[8,128,128]{2,1,0:T(8,128)(2,1)S(1)} collective-permute-done((bf16[8,128,128]{2,1,0:T(8,128)(2,1)S(1)}, bf16[8,128,128]{2,1,0:T(8,128)(2,1)S(1)}, u32[]{:S(2)}, u32[]{:S(2)}) %collective-permute-start.27) | collective-permute-done | bytes 262176 | tf_op jit(solution)/shard_map/ppermute | solution.py:301
  162.0 2.2 %collective-permute-start.37 = (bf16[8,128,128]{2,1,0:T(8,128)(2,1)S(1)}, bf16[8,128,128]{2,1,0:T(8,128)(2,1)S(1)}, u32[]{:S(2)}, u32[]{:S(2)}) collective-permute-start(bf16[8,128,128]{2,1,0:T(8,128)(2,1)S(1)} %fusion.7), channel_id=1, source_target_pairs={{0,128},{128,0},{1,129},{129,1},{2,130},{130,2},{3,131},{131,3},{4... | collective-permute-start | bytes 786440 | tf_op jit(solution)/shard_map/ppermute | solution.py:305
  164.1 3.2 %collective-permute-start.30 = (bf16[128,1024]{1,0:T(8,128)(2,1)S(1)}, bf16[128,1024]{1,0:T(8,128)(2,1)S(1)}, u32[]{:S(2)}, u32[]{:S(2)}) collective-permute-start(bf16[128,1024]{1,0:T(8,128)(2,1)S(1)} %get-tuple-element.51), channel_id=1, source_target_pairs={{0,7},{1,0},{2,1},{3,2},{4,3},{5,4},{6,5},{7,6},{8,15},{9,8},{10,9... | collective-permute-start | bytes 786440 | tf_op jit(solution)/shard_map/ppermute | solution.py:313
  169.0 2.4 %collective-permute-done.29 = bf16[128,1024]{1,0:T(8,128)(2,1)S(1)} collective-permute-done((bf16[128,1024]{1,0:T(8,128)(2,1)S(1)}, bf16[128,1024]{1,0:T(8,128)(2,1)S(1)}, u32[]{:S(2)}, u32[]{:S(2)}) %collective-permute-start.29) | collective-permute-done | bytes 262176 | tf_op jit(solution)/shard_map/ppermute | solution.py:309
  172.5 3.0 %collective-permute-done.33 = bf16[8,128,128]{2,1,0:T(8,128)(2,1)S(1)} collective-permute-done((bf16[8,128,128]{2,1,0:T(8,128)(2,1)S(1)}, bf16[8,128,128]{2,1,0:T(8,128)(2,1)S(1)}, u32[]{:S(2)}, u32[]{:S(2)}) %collective-permute-start.33) | collective-permute-done | bytes 262176 | tf_op jit(solution)/shard_map/ppermute | solution.py:305
  176.3 3.0 %collective-permute-done.32 = bf16[128,1024]{1,0:T(8,128)(2,1)S(1)} collective-permute-done((bf16[128,1024]{1,0:T(8,128)(2,1)S(1)}, bf16[128,1024]{1,0:T(8,128)(2,1)S(1)}, u32[]{:S(2)}, u32[]{:S(2)}) %collective-permute-start.32) | collective-permute-done | bytes 262176 | tf_op jit(solution)/shard_map/ppermute | solution.py:309
  (123 shorter events, 32.3 us)
Async XLA Ops:
  7.2 60.9 %all-gather.3.cloned.1.call-start = ((), (), s32[]{:S(2)}) async-start(), calls=%async_computation.2 | async-start | bytes 4718592 | tf_op jit(solution)/shard_map/all_gather | solution.py:356
  9.2 162.4 %reduce-scatter.2.cloned.1.call-start = ((), (), s32[]{:S(2)}) async-start(), calls=%async_computation.1 | async-start | bytes 2359296 | tf_op jit(solution)/shard_map/reduce_scatter | solution.py:344
  12.8 12.2 %collective-permute-start.9 = (bf16[8,128,128]{2,1,0:T(8,128)(2,1)}, bf16[8,128,128]{2,1,0:T(8,128)(2,1)S(1)}, u32[]{:S(2)}, u32[]{:S(2)}) collective-permute-start(bf16[8,128,128]{2,1,0:T(8,128)(2,1)} %param.11), channel_id=1, source_target_pairs={{0,96},{8,104},{16,112},{24,120},{32,0},{40,8},{48,16},{56,24},{64... | collective-permute-start | bytes 786440 | tf_op jit(solution)/shard_map/ppermute | solution.py:301
  13.9 12.9 %collective-permute-start.8 = (bf16[8,128,128]{2,1,0:T(8,128)(2,1)}, bf16[8,128,128]{2,1,0:T(8,128)(2,1)S(1)}, u32[]{:S(2)}, u32[]{:S(2)}) collective-permute-start(bf16[8,128,128]{2,1,0:T(8,128)(2,1)} %param.11), channel_id=1, source_target_pairs={{0,32},{8,40},{16,48},{24,56},{32,64},{40,72},{48,80},{56,88},{64,... | collective-permute-start | bytes 786440 | tf_op jit(solution)/shard_map/ppermute | solution.py:301
  25.1 14.8 %collective-permute-start.12 = (bf16[2,8,128,128]{3,2,1,0:T(8,128)(2,1)S(1)}, bf16[2,8,128,128]{3,2,1,0:T(8,128)(2,1)S(1)}, u32[]{:S(2)}, u32[]{:S(2)}) collective-permute-start(bf16[2,8,128,128]{3,2,1,0:T(8,128)(2,1)S(1)} %pad_maximum_fusion.3.refs_11_), channel_id=1, source_target_pairs={{0,16},{8,24},{16,0},{24,8},{32,48},{40,56},{48,32},{56,40},{64,80... | collective-permute-start | bytes 1572872 | tf_op jit(solution)/shard_map/ppermute | solution.py:297
  26.9 15.7 %collective-permute-start.13 = (bf16[2,8,128,128]{3,2,1,0:T(8,128)(2,1)S(1)}, bf16[2,8,128,128]{3,2,1,0:T(8,128)(2,1)S(1)}, u32[]{:S(2)}, u32[]{:S(2)}) collective-permute-start(bf16[2,8,128,128]{3,2,1,0:T(8,128)(2,1)S(1)} %pad_maximum_fusion.2.refs_10_), channel_id=1, source_target_pairs={{0,8},{8,0},{16,24},{24,16},{32,40},{40,32},{48,56},{56,48},{64,72... | collective-permute-start | bytes 1572872 | tf_op jit(solution)/shard_map/ppermute | solution.py:293
  27.1 23.6 %collective-permute-start.11 = (bf16[2,8,128,128]{3,2,1,0:T(8,128)(2,1)S(1)}, bf16[2,8,128,128]{3,2,1,0:T(8,128)(2,1)S(1)}, u32[]{:S(2)}, u32[]{:S(2)}) collective-permute-start(bf16[2,8,128,128]{3,2,1,0:T(8,128)(2,1)S(1)} %pad_maximum_fusion.2.refs_10_), channel_id=1, source_target_pairs={{0,16},{8,24},{16,0},{24,8},{32,48},{40,56},{48,32},{56,40},{64,80... | collective-permute-start | bytes 1572872 | tf_op jit(solution)/shard_map/ppermute | solution.py:297
  27.6 23.2 %collective-permute-start.4 = (bf16[2,8,128,128]{3,2,1,0:T(8,128)(2,1)S(1)}, bf16[2,8,128,128]{3,2,1,0:T(8,128)(2,1)S(1)}, u32[]{:S(2)}, u32[]{:S(2)}) collective-permute-start(bf16[2,8,128,128]{3,2,1,0:T(8,128)(2,1)S(1)} %pad_maximum_fusion.1.refs_1_), channel_id=1, source_target_pairs={{0,8},{8,0},{16,24},{24,16},{32,40},{40,32},{48,56},{56,48},{64,72... | collective-permute-start | bytes 1572872 | tf_op jit(solution)/shard_map/ppermute | solution.py:293
  27.6 23.6 %collective-permute-start.3 = (bf16[2,8,128,128]{3,2,1,0:T(8,128)(2,1)S(1)}, bf16[2,8,128,128]{3,2,1,0:T(8,128)(2,1)S(1)}, u32[]{:S(2)}, u32[]{:S(2)}) collective-permute-start(bf16[2,8,128,128]{3,2,1,0:T(8,128)(2,1)S(1)} %pad_maximum_fusion.1.refs_1_), channel_id=1, source_target_pairs={{0,64},{8,72},{16,80},{24,88},{32,96},{40,104},{48,112},{56,120},{... | collective-permute-start | bytes 1572872 | tf_op jit(solution)/shard_map/ppermute | solution.py:301
  39.9 14.7 %collective-permute-start.2 = (bf16[2,8,128,128]{3,2,1,0:T(8,128)(2,1)S(1)}, bf16[2,8,128,128]{3,2,1,0:T(8,128)(2,1)S(1)}, u32[]{:S(2)}, u32[]{:S(2)}) collective-permute-start(bf16[2,8,128,128]{3,2,1,0:T(8,128)(2,1)S(1)} %pad_maximum_fusion.1.refs_1_), channel_id=1, source_target_pairs={{0,96},{8,104},{16,112},{24,120},{32,0},{40,8},{48,16},{56,24},{64... | collective-permute-start | bytes 1572872 | tf_op jit(solution)/shard_map/ppermute | solution.py:301
  42.6 14.0 %collective-permute-start.1 = (bf16[2,8,128,128]{3,2,1,0:T(8,128)(2,1)S(1)}, bf16[2,8,128,128]{3,2,1,0:T(8,128)(2,1)S(1)}, u32[]{:S(2)}, u32[]{:S(2)}) collective-permute-start(bf16[2,8,128,128]{3,2,1,0:T(8,128)(2,1)S(1)} %pad_maximum_fusion.1.refs_1_), channel_id=1, source_target_pairs={{0,32},{8,40},{16,48},{24,56},{32,64},{40,72},{48,80},{56,88},{64,... | collective-permute-start | bytes 1572872 | tf_op jit(solution)/shard_map/ppermute | solution.py:301
  99.8 15.2 %collective-permute-start.21 = (bf16[2,8,128,128]{3,2,1,0:T(8,128)(2,1)S(1)}, bf16[2,8,128,128]{3,2,1,0:T(8,128)(2,1)S(1)}, u32[]{:S(2)}, u32[]{:S(2)}) collective-permute-start(bf16[2,8,128,128]{3,2,1,0:T(8,128)(2,1)S(1)} %get-tuple-element.54), channel_id=1, source_target_pairs={{0,32},{8,40},{16,48},{24,56},{32,64},{40,72},{48,80},{56,88},{64,... | collective-permute-start | bytes 1572872 | tf_op jit(solution)/shard_map/ppermute | solution.py:301
  101.4 16.0 %collective-permute-start.17 = (bf16[128,1024]{1,0:T(8,128)(2,1)S(1)}, bf16[128,1024]{1,0:T(8,128)(2,1)S(1)}, u32[]{:S(2)}, u32[]{:S(2)}) collective-permute-start(bf16[128,1024]{1,0:T(8,128)(2,1)S(1)} %copy-done.21), channel_id=1, source_target_pairs={{0,1},{1,2},{2,3},{3,4},{4,5},{5,6},{6,7},{7,0},{8,9},{9,10},{10,1... | collective-permute-start | bytes 786440 | tf_op jit(solution)/shard_map/ppermute | solution.py:309
  101.4 31.2 %collective-permute-start.24 = (bf16[4,8,128,128]{3,2,1,0:T(8,128)(2,1)S(1)}, bf16[4,8,128,128]{3,2,1,0:T(8,128)(2,1)S(1)}, u32[]{:S(2)}, u32[]{:S(2)}) collective-permute-start(bf16[4,8,128,128]{3,2,1,0:T(8,128)(2,1)S(1)} %fusion.1), channel_id=1, source_target_pairs={{0,16},{8,24},{16,0},{24,8},{32,48},{40,56},{48,32},{56,40},{64,80... | collective-permute-start | bytes 3145736 | tf_op jit(solution)/shard_map/ppermute | solution.py:297
  115.1 17.5 %collective-permute-start.23 = (bf16[1,4,8,128,128]{4,3,2,1,0:T(8,128)(2,1)S(1)}, bf16[1,4,8,128,128]{4,3,2,1,0:T(8,128)(2,1)S(1)}, u32[]{:S(2)}, u32[]{:S(2)}) collective-permute-start(bf16[1,4,8,128,128]{4,3,2,1,0:T(8,128)(2,1)S(1)} %copy-done.19), channel_id=1, source_target_pairs={{0,8},{8,0},{16,24},{24,16},{32,40},{40,32},{48,56},{56,48},{64,72... | collective-permute-start | bytes 3145736 | tf_op jit(solution)/shard_map/ppermute | solution.py:293
  115.1 16.8 %collective-permute-start.35 = (bf16[2,8,128,128]{3,2,1,0:T(8,128)(2,1)S(1)}, bf16[2,8,128,128]{3,2,1,0:T(8,128)(2,1)S(1)}, u32[]{:S(2)}, u32[]{:S(2)}) collective-permute-start(bf16[2,8,128,128]{3,2,1,0:T(8,128)(2,1)S(1)} %get-tuple-element.56), channel_id=1, source_target_pairs={{0,96},{8,104},{16,112},{24,120},{32,0},{40,8},{48,16},{56,24},{64... | collective-permute-start | bytes 1572872 | tf_op jit(solution)/shard_map/ppermute | solution.py:301
  116.6 15.6 %collective-permute-start.22 = (bf16[2,8,128,128]{3,2,1,0:T(8,128)(2,1)S(1)}, bf16[2,8,128,128]{3,2,1,0:T(8,128)(2,1)S(1)}, u32[]{:S(2)}, u32[]{:S(2)}) collective-permute-start(bf16[2,8,128,128]{3,2,1,0:T(8,128)(2,1)S(1)} %get-tuple-element.45), channel_id=1, source_target_pairs={{0,64},{8,72},{16,80},{24,88},{32,96},{40,104},{48,112},{56,120},{... | collective-permute-start | bytes 1572872 | tf_op jit(solution)/shard_map/ppermute | solution.py:301
  117.4 14.3 %collective-permute-start.18 = (bf16[128,1024]{1,0:T(8,128)(2,1)S(1)}, bf16[128,1024]{1,0:T(8,128)(2,1)S(1)}, u32[]{:S(2)}, u32[]{:S(2)}) collective-permute-start(bf16[128,1024]{1,0:T(8,128)(2,1)S(1)} %copy-done.20), channel_id=1, source_target_pairs={{0,7},{1,0},{2,1},{3,2},{4,3},{5,4},{6,5},{7,6},{8,15},{9,8},{10,9... | collective-permute-start | bytes 786440 | tf_op jit(solution)/shard_map/ppermute | solution.py:313
  133.1 15.6 %collective-permute-start.25 = (bf16[128,1024]{1,0:T(8,128)(2,1)S(1)}, bf16[128,1024]{1,0:T(8,128)(2,1)S(1)}, u32[]{:S(2)}, u32[]{:S(2)}) collective-permute-start(bf16[128,1024]{1,0:T(8,128)(2,1)S(1)} %get-tuple-element.48), channel_id=1, source_target_pairs={{0,1},{1,2},{2,3},{3,4},{4,5},{5,6},{6,7},{7,0},{8,9},{9,10},{10,1... | collective-permute-start | bytes 786440 | tf_op jit(solution)/shard_map/ppermute | solution.py:309
  133.4 16.8 %collective-permute-start.26 = (bf16[128,1024]{1,0:T(8,128)(2,1)S(1)}, bf16[128,1024]{1,0:T(8,128)(2,1)S(1)}, u32[]{:S(2)}, u32[]{:S(2)}) collective-permute-start(bf16[128,1024]{1,0:T(8,128)(2,1)S(1)} %get-tuple-element.49), channel_id=1, source_target_pairs={{0,7},{1,0},{2,1},{3,2},{4,3},{5,4},{6,5},{7,6},{8,15},{9,8},{10,9... | collective-permute-start | bytes 786440 | tf_op jit(solution)/shard_map/ppermute | solution.py:313
  136.7 16.2 %collective-permute-start.28 = (bf16[8,128,128]{2,1,0:T(8,128)(2,1)S(1)}, bf16[8,128,128]{2,1,0:T(8,128)(2,1)S(1)}, u32[]{:S(2)}, u32[]{:S(2)}) collective-permute-start(bf16[8,128,128]{2,1,0:T(8,128)(2,1)S(1)} %get-tuple-element.62), channel_id=1, source_target_pairs={{0,96},{8,104},{16,112},{24,120},{32,0},{40,8},{48,16},{56,24},{64... | collective-permute-start | bytes 786440 | tf_op jit(solution)/shard_map/ppermute | solution.py:301
  148.0 13.9 %collective-permute-start.27 = (bf16[8,128,128]{2,1,0:T(8,128)(2,1)S(1)}, bf16[8,128,128]{2,1,0:T(8,128)(2,1)S(1)}, u32[]{:S(2)}, u32[]{:S(2)}) collective-permute-start(bf16[8,128,128]{2,1,0:T(8,128)(2,1)S(1)} %get-tuple-element.63), channel_id=1, source_target_pairs={{0,32},{8,40},{16,48},{24,56},{32,64},{40,72},{48,80},{56,88},{64,... | collective-permute-start | bytes 786440 | tf_op jit(solution)/shard_map/ppermute | solution.py:301
  148.0 13.9 %collective-permute-start.36 = (bf16[8,128,128]{2,1,0:T(8,128)(2,1)S(1)}, bf16[8,128,128]{2,1,0:T(8,128)(2,1)S(1)}, u32[]{:S(2)}, u32[]{:S(2)}) collective-permute-start(bf16[8,128,128]{2,1,0:T(8,128)(2,1)S(1)} %fusion.16), channel_id=1, source_target_pairs={{0,16},{8,24},{16,0},{24,8},{32,48},{40,56},{48,32},{56,40},{64,80... | collective-permute-start | bytes 786440 | tf_op jit(solution)/shard_map/ppermute | solution.py:297
  148.7 18.7 %collective-permute-start.31 = (bf16[8,128,128]{2,1,0:T(8,128)(2,1)S(1)}, bf16[8,128,128]{2,1,0:T(8,128)(2,1)S(1)}, u32[]{:S(2)}, u32[]{:S(2)}) collective-permute-start(bf16[8,128,128]{2,1,0:T(8,128)(2,1)S(1)} %get-tuple-element.61), channel_id=1, source_target_pairs={{0,64},{8,72},{16,80},{24,88},{32,96},{40,104},{48,112},{56,120},{... | collective-permute-start | bytes 786440 | tf_op jit(solution)/shard_map/ppermute | solution.py:301
  (38 other events, 454.7 us)
Sparse Core Ops, SparseCore 0:
  10.4 57.6 all-gather.2
  92.6 47.2 reduce-scatter.1

commit v3 on v2

--- a/solution.py
+++ b/solution.py
@@ -17,7 +17,7 @@
 K = 8
 NT = 128
 COST = 10_000_000
-UNROLL = 2
+UNROLL = 4
 VMEM_LIMIT = 56 * 1024 * 1024
 
 SMEM_SPEC = pl.BlockSpec(memory_space=pltpu.SMEM)
@@ -164,9 +164,6 @@
     ]
 
 
-RING = (0, 1, 2, 3, 6, 7)
-
-
 def tile_pass(up_order, rows, down_order, cols, pos, x, cot, up, down):
     up_shapes, down_shapes = grad_shapes(False), grad_shapes(True)
     groups = (x.arrays, up.arrays, cot.arrays, down.arrays)
@@ -176,7 +173,7 @@
         ins, refs = refs[: sum(counts)], refs[sum(counts) :]
         x_refs, u_refs = ins[: counts[0]], ins[counts[0] : sum(counts[:2])]
         c_refs, d_refs = ins[sum(counts[:2]) : sum(counts[:3])], ins[sum(counts[:3]) :]
-        ups, downs, (ring_up, ring_down, rest, out), scratch = refs[:3], refs[3:6], refs[6:10], refs[10:]
+        ups, downs, parts, scratch = refs[:3], refs[3:6], refs[6], refs[7:]
         xbuf, ubuf, cbuf, dbuf, hidden, slope, pre, up_terms, down_terms, acc, sems = scratch
         first = wide_copies(x.places, x_refs, pos, xbuf, sems, 0)
         first += tile_copies(up.places, u_refs, pos, ubuf, sems, len(first))
@@ -237,10 +234,7 @@
             return carry
 
         lax.fori_loop(0, H, input_part, 0, unroll=UNROLL)
-        ring_up[...] = acc[(pos[0] + 4) & 7].astype(BF)
-        ring_down[...] = acc[(pos[0] + 5) & 7].astype(BF)
-        for i, r in enumerate(RING):
-            rest[i] = acc[(pos[0] + r) & 7].astype(BF)
+        parts[:, 1] = acc[...].astype(BF)
         acc[...] = jnp.zeros_like(acc)
 
         def output_part(h, carry):
@@ -250,22 +244,18 @@
             return carry
 
         lax.fori_loop(0, H, output_part, 0, unroll=UNROLL)
-        out[...] = acc[...].astype(BF)
+        parts[:, 0] = acc[...].astype(BF)
         finish(up_copies)
         finish(down_copies)
 
     n = len(x.places) + len(up.places) + len(cot.places) + len(down.places) + 6
-    one = jax.ShapeDtypeStruct((B, 8 * B), BF)
     hiddens = (H, B, B)
     got = call(
         kernel,
         [
             *up_shapes,
             *down_shapes,
-            one,
-            one,
-            jax.ShapeDtypeStruct((6, B, 8 * B), BF),
-            jax.ShapeDtypeStruct((8, B, 8 * B), BF),
+            jax.ShapeDtypeStruct((8, 2, B, 8 * B), BF),
         ],
         (up_order, rows, down_order, cols, pos),
         sum(groups, ()),
@@ -283,10 +273,10 @@
             WIDE_ACC,
             pltpu.SemaphoreType.DMA((n,)),
         ],
-        out_specs=(ANY_SPEC,) * 6 + (VMEM_SPEC,) * 4,
+        out_specs=(ANY_SPEC,) * 6 + (VMEM_SPEC,),
         name="tile_pass",
     )
-    return got[:3], got[3:6], got[6:9], got[9]
+    return got[:3], got[3:6], got[6]
 
 
 def core_swap(a):
@@ -303,14 +293,6 @@
 
 def dp_swap(a):
     return lax.ppermute(a, "dp", [(0, 1), (1, 0)])
-
-
-def z_up(a):
-    return lax.ppermute(a, "tensor", [(i, (i + 1) % 8) for i in range(8)])
-
-
-def z_down(a):
-    return lax.ppermute(a, "tensor", [(i, (i + 7) % 8) for i in range(8)])
 
 
 def gather_up(tiles, *early):
@@ -359,43 +341,26 @@
     up = gather_up(up_tiles, up_order, down_order, pos)
     down = gather_down(down_tiles, up.arrays[0])
 
-    (up0, up1, up_keep), (down12, down30, down_keep), ring_parts, partial_out = tile_pass(
+    (up0, up1, up_keep), (down12, down30, down_keep), parts = tile_pass(
         up_order, rows, down_order, cols, pos, x, cot, up, down
     )
-    output = scatter_features(partial_out)
-    u1 = core_swap(up1)
+    output, input_grad = scatter_features(parts)
+    u1, d12, d30 = core_swap(up1), core_swap(down12), core_swap(down30)
     near = add(up_keep[1], u1[0]).astype(BF)
     u_y = y_swap(near)
-    d12, d30 = core_swap(down12), core_swap(down30)
     d12 = after(d12, near)
     t1, t2 = add(down_keep[0], d12[0]).astype(BF), add(down_keep[1], d12[1]).astype(BF)
-    d_x1 = x_shift(t1, 1)
     t3 = add(down_keep[2], d30[0]).astype(BF)
-    d_x3 = x_shift(t3, 3)
+    d_x1, d_x3, d_x2 = x_shift(t1, 1), x_shift(t3, 3), x_shift(t2, 2)
     u0 = core_swap(after(up0, d_x1))
-    part4, part5, rest = ring_parts
-
-    part = {r: rest[n] for n, r in enumerate(RING)}
-    z1, w1 = z_up(part4), z_down(part5)
-    d_x2 = x_shift(after(t2, d_x1), 2)
     total = (add(up_keep[0], u0[0]) + u_y.astype(F32)).astype(BF)
-    u_x1, u_x3 = x_shift(total[1], 1), x_shift(total[3], 3)
-    z1, w1, _ = lax.optimization_barrier((z1, w1, near))
-    z2, w2 = add(part[3], z1).astype(BF), add(part[6], w1).astype(BF)
-    z2, w2, _ = lax.optimization_barrier((z2, w2, (d_x2, total)))
-    z2, w2 = z_up(z2), z_down(w2)
+    u_x1, u_x3, u_x2 = x_shift(total[1], 1), x_shift(total[3], 3), x_shift(total[2], 2)
     own = add(down_keep[3], d30[1]) + add(d_x1, d_x3) + d_x2.astype(F32)
     d_y = y_swap(own[1].astype(BF))
-    u_x2 = x_shift(total[2], 2)
-    z3, w3 = add(part[2], z2).astype(BF), add(part[7], w2).astype(BF)
-    z3, w3, _ = lax.optimization_barrier((z3, w3, (u_x1, u_x3)))
-    z3, w3 = z_up(z3), z_down(w3)
     down_mine = (own[0] + d_y.astype(F32)).astype(BF)
     d_dp = dp_swap(down_mine)
     up_mine = (total[0].astype(F32) + add(u_x1, u_x3) + u_x2.astype(F32)).astype(BF)
-    z4 = z_up(after(add(part[1], z3).astype(BF), w3, u_x2, output))
     u_dp = dp_swap(up_mine)
-    input_grad = (part[0].astype(F32) + add(z4, w3)).astype(BF)
     return (output, input_grad, add(up_mine, u_dp), add(down_mine, d_dp))
 
 

time: 189 us -> 160 us (0.85)
  starting transfers between devices: 44.2 us -> 29.5 us
  waiting for transfers between devices: 86.8 us -> 77.7 us
  other arithmetic: 12.2 us -> 7.59 us
  Pallas kernels: 28.2 us -> 24.3 us
  local copies, waits for them, and re-layouts: 2.18 us -> 4.71 us
    ppermute x7 -> x0, waiting for transfers between devices: 18.3 us -> none  [the longest x3 12.9 us: z_down(): return lax.ppermute(a, 'tensor', [(i, (i + 7) % 8) for i in range(8)])]
    ppermute x7 -> x0, starting transfers between devices: 8.25 us -> none  [the longest x3 7.81 us: z_down(): return lax.ppermute(a, 'tensor', [(i, (i + 7) % 8) for i in range(8)])]
    ppermute x12, starting transfers between devices: 24.9 us -> 17.8 us  [x_shift(): return lax.ppermute(a, 'fsdp', [(i, (i + 4 * d) % 16) for i in range(16)])]
    pallas_call x1, Pallas kernels: 23.6 us -> 19.7 us  [call(): pl.pallas_call(kernel, out_shape=tuple(out_shape), in_specs=[SMEM_SPEC] *...]
    ppermute x12, waiting for transfers between devices: 34.1 us -> 37.6 us  [x_shift(): return lax.ppermute(a, 'fsdp', [(i, (i + 4 * d) % 16) for i in range(16)])]
    convert_element_type x5 -> x1, other arithmetic: 4.15 us -> 0.77 us  [body(): add(down_keep[1], d12[1]).astype(BF)]
    ppermute x2, waiting for transfers between devices: 2.96 us -> 5.57 us  [dp_swap(): return lax.ppermute(a, 'dp', [(0, 1), (1, 0)])]
    ppermute x5, waiting for transfers between devices: 18.2 us -> 20.8 us  [y_swap(): return lax.ppermute(a, 'fsdp', [(i, i ^ 2) for i in range(16)])]
  transfers between devices with their start and end apart: 40 -> 33, of which waited for: 17 -> 17; matrix products, arithmetic and copies ran while one was open for 5% -> 4% of each run, Pallas kernels for 2% -> 3%
where the time goes in v3:
time: 160 us; the launch traced here: 158 us
  waiting for transfers between devices  77.7 us (49%)
  starting transfers between devices  29.5 us (18%)
  Pallas kernels  24.3 us (15%)
  between operations  14.4 us (9%)
  other arithmetic  7.59 us (5%)
  local copies, waits for them, and re-layouts  4.71 us (3%)
    ppermute x12, waiting for transfers between devices, x_shift(): return lax.ppermute(a, 'fsdp', [(i, (i + 4 * d) % 16) for i in range(16)])  37.6 us
    ppermute x5, waiting for transfers between devices, y_swap(): return lax.ppermute(a, 'fsdp', [(i, i ^ 2) for i in range(16)])  20.8 us
    pallas_call x1, Pallas kernels, call(): pl.pallas_call(kernel, out_shape=tuple(out_shape), in_specs=[SMEM_SPEC] *...  19.7 us
    ppermute x12, starting transfers between devices, x_shift(): return lax.ppermute(a, 'fsdp', [(i, (i + 4 * d) % 16) for i in range(16)])  17.8 us
    all_gather x1, waiting for transfers between devices, body(): lax.all_gather(jnp.stack([activations, cotangent]), 'tensor', axis=0, til...  9.26 us
    ppermute x5, starting transfers between devices, y_swap(): return lax.ppermute(a, 'fsdp', [(i, i ^ 2) for i in range(16)])  5.58 us
    ppermute x2, waiting for transfers between devices, dp_swap(): return lax.ppermute(a, 'dp', [(0, 1), (1, 0)])  5.57 us
    pallas_call x1, Pallas kernels, plan(): pl.pallas_call(plan_kernel, out_shape=(shape, shape), in_specs=[SMEM_SPEC...  4.58 us
  transfers between devices with their start and end apart: 33, of which 17 were waited for; matrix products, arithmetic and copies ran while one was open for 4% of the time, Pallas kernels for 3%

profile of v3, /device:TPU:8, one launch (start us, length us, event | category | flops | bytes accessed | tf_op | source)
XLA Modules:
  0.0 158.1 jit_solution(17135330150438364652)
XLA Ops:
  7.2 1.9 %pad_maximum_fusion = bf16[2,128,1024]{2,1,0:T(8,128)(2,1)} fusion(bf16[1,128,1024]{2,1,0:T(8,128)(2,1)} %bitcast.58, bf16[1,128,1024]{2,1,0:T(8,128)(2,1)} %bitcast.59), kind=kLoop, calls=%fused_computation.16 | loop fusion | flops 262144 | bytes 1048576 | tf_op jit(solution)/shard_map/stack | solution.py:338
  9.2 2.3 %collective-permute-start = (bf16[8,128,128]{2,1,0:T(8,128)(2,1)}, bf16[8,128,128]{2,1,0:T(8,128)(2,1)S(1)}, u32[]{:S(2)}, u32[]{:S(2)}) collective-permute-start(bf16[8,128,128]{2,1,0:T(8,128)(2,1)} %param.10), channel_id=1, source_target_pairs={{0,16},{8,24},{16,0},{24,8},{32,48},{40,56},{48,32},{56,40},{64,80... | collective-permute-start | bytes 786440 | tf_op jit(solution)/shard_map/ppermute | solution.py:287
  15.4 4.6 %plan.1 = (s32[128]{0:T(128)}, s32[128]{0:T(128)}) custom-call(s32[128]{0:T(128)} %bitcast.68, s32[128]{0:T(128)} %bitcast.69), custom_call_target="tpu_custom_call" | custom-call | tf_op jit(solution)/shard_map/plan/pallas_call | solution.py:55
  22.1 2.9 %collective-permute-done.9 = bf16[8,128,128]{2,1,0:T(8,128)(2,1)S(1)} collective-permute-done((bf16[8,128,128]{2,1,0:T(8,128)(2,1)}, bf16[8,128,128]{2,1,0:T(8,128)(2,1)S(1)}, u32[]{:S(2)}, u32[]{:S(2)}) %collective-permute-start.9) | collective-permute-done | bytes 262176 | tf_op jit(solution)/shard_map/ppermute | solution.py:291
  27.6 2.2 %collective-permute-start.3 = (bf16[2,8,128,128]{3,2,1,0:T(8,128)(2,1)S(1)}, bf16[2,8,128,128]{3,2,1,0:T(8,128)(2,1)S(1)}, u32[]{:S(2)}, u32[]{:S(2)}) collective-permute-start(bf16[2,8,128,128]{3,2,1,0:T(8,128)(2,1)S(1)} %pad_maximum_fusion.1.refs_1_), channel_id=1, source_target_pairs={{0,64},{8,72},{16,80},{24,88},{32,96},{40,104},{48,112},{56,120},{... | collective-permute-start | bytes 1572872 | tf_op jit(solution)/shard_map/ppermute | solution.py:291
  29.9 10.1 %collective-permute-done.12.refs_13_ = bf16[2,8,128,128]{3,2,1,0:T(8,128)(2,1)S(1)} collective-permute-done((bf16[2,8,128,128]{3,2,1,0:T(8,128)(2,1)S(1)}, bf16[2,8,128,128]{3,2,1,0:T(8,128)(2,1)S(1)}, u32[]{:S(2)}, u32[]{:S(2)}) %collective-permute-start.12) | collective-permute-done | bytes 524320 | tf_op jit(solution)/shard_map/ppermute | solution.py:287
  39.9 2.6 %collective-permute-start.2 = (bf16[2,8,128,128]{3,2,1,0:T(8,128)(2,1)S(1)}, bf16[2,8,128,128]{3,2,1,0:T(8,128)(2,1)S(1)}, u32[]{:S(2)}, u32[]{:S(2)}) collective-permute-start(bf16[2,8,128,128]{3,2,1,0:T(8,128)(2,1)S(1)} %pad_maximum_fusion.1.refs_1_), channel_id=1, source_target_pairs={{0,96},{8,104},{16,112},{24,120},{32,0},{40,8},{48,16},{56,24},{64... | collective-permute-start | bytes 1572872 | tf_op jit(solution)/shard_map/ppermute | solution.py:291
  42.6 8.1 %collective-permute-done.11.refs_12_ = bf16[2,8,128,128]{3,2,1,0:T(8,128)(2,1)S(1)} collective-permute-done((bf16[2,8,128,128]{3,2,1,0:T(8,128)(2,1)S(1)}, bf16[2,8,128,128]{3,2,1,0:T(8,128)(2,1)S(1)}, u32[]{:S(2)}, u32[]{:S(2)}) %collective-permute-start.11) | collective-permute-done | bytes 524320 | tf_op jit(solution)/shard_map/ppermute | solution.py:287
  51.3 3.3 %collective-permute-done.2.refs_3_ = bf16[2,8,128,128]{3,2,1,0:T(8,128)(2,1)S(1)} collective-permute-done((bf16[2,8,128,128]{3,2,1,0:T(8,128)(2,1)S(1)}, bf16[2,8,128,128]{3,2,1,0:T(8,128)(2,1)S(1)}, u32[]{:S(2)}, u32[]{:S(2)}) %collective-permute-start.2) | collective-permute-done | bytes 524320 | tf_op jit(solution)/shard_map/ppermute | solution.py:291
  54.6 2.0 %collective-permute-done.1.refs_2_ = bf16[2,8,128,128]{3,2,1,0:T(8,128)(2,1)S(1)} collective-permute-done((bf16[2,8,128,128]{3,2,1,0:T(8,128)(2,1)S(1)}, bf16[2,8,128,128]{3,2,1,0:T(8,128)(2,1)S(1)}, u32[]{:S(2)}, u32[]{:S(2)}) %collective-permute-start.1) | collective-permute-done | bytes 524320 | tf_op jit(solution)/shard_map/ppermute | solution.py:291
  58.8 9.3 %all-gather.3.cloned.1.call-done = bf16[16,128,1024]{2,1,0:T(8,128)(2,1)} async-done(((bf16[2,128,1024]{2,1,0:T(8,128)(2,1)}), bf16[16,128,1024]{2,1,0:T(8,128)(2,1)}) %all-gather.3.cloned.1.call-update) | async-done | bytes 4194320 | tf_op jit(solution)/shard_map/all_gather | solution.py:338
  68.1 19.7 %tile_pass.1 = (bf16[1,4,8,128,128]{4,3,2,1,0:T(8,128)(2,1)}, bf16[1,4,8,128,128]{4,3,2,1,0:T(8,128)(2,1)}, bf16[2,4,8,128,128]{4,3,2,1,0:T(8,128)(2,1)}, bf16[2...) custom-call(s32[128]{0:T(128)} %get-tuple-element.18.up_order, ...), custom_call_target="tpu_custom_call" | custom-call | flops 10000000 | bytes 100000 | tf_op jit(solution)/shard_map/tile_pass/pallas_call | solution.py:102
  89.1 1.8 %collective-permute-done.18 = bf16[1,4,8,128,128]{4,3,2,1,0:T(8,128)(2,1)S(1)} collective-permute-done((bf16[1,4,8,128,128]{4,3,2,1,0:T(8,128)(2,1)}, bf16[1,4,8,128,128]{4,3,2,1,0:T(8,128)(2,1)S(1)}, u32[]{:S(2)}, u32[]{:S(2)}) %collective-permute-start.18) | collective-permute-done | bytes 1048608 | tf_op jit(solution)/shard_map/ppermute | solution.py:283
  91.2 2.6 %collective-permute-done.17 = bf16[2,2,8,128,128]{4,3,2,1,0:T(8,128)(2,1)S(1)} collective-permute-done((bf16[2,2,8,128,128]{4,3,2,1,0:T(8,128)(2,1)}, bf16[2,2,8,128,128]{4,3,2,1,0:T(8,128)(2,1)S(1)}, u32[]{:S(2)}, u32[]{:S(2)}) %collective-permute-start.17) | collective-permute-done | bytes 1048608 | tf_op jit(solution)/shard_map/ppermute | solution.py:283
  96.2 2.7 %collective-permute-start.28 = (bf16[2,8,128,128]{3,2,1,0:T(8,128)(2,1)S(1)}, bf16[2,8,128,128]{3,2,1,0:T(8,128)(2,1)S(1)}, u32[]{:S(2)}, u32[]{:S(2)}) collective-permute-start(bf16[2,8,128,128]{3,2,1,0:T(8,128)(2,1)S(1)} %get-tuple-element.32), channel_id=1, source_target_pairs={{0,64},{8,72},{16,80},{24,88},{32,96},{40,104},{48,112},{56,120},{... | collective-permute-start | bytes 1572872 | tf_op jit(solution)/shard_map/ppermute | solution.py:291
  100.9 9.0 %collective-permute-done.19 = bf16[2,8,128,128]{3,2,1,0:T(8,128)(2,1)S(1)} collective-permute-done((bf16[2,8,128,128]{3,2,1,0:T(8,128)(2,1)S(1)}, bf16[2,8,128,128]{3,2,1,0:T(8,128)(2,1)S(1)}, u32[]{:S(2)}, u32[]{:S(2)}) %collective-permute-start.19) | collective-permute-done | bytes 524320 | tf_op jit(solution)/shard_map/ppermute | solution.py:291
  109.9 12.1 %collective-permute-done.28 = bf16[2,8,128,128]{3,2,1,0:T(8,128)(2,1)S(1)} collective-permute-done((bf16[2,8,128,128]{3,2,1,0:T(8,128)(2,1)S(1)}, bf16[2,8,128,128]{3,2,1,0:T(8,128)(2,1)S(1)}, u32[]{:S(2)}, u32[]{:S(2)}) %collective-permute-start.28) | collective-permute-done | bytes 524320 | tf_op jit(solution)/shard_map/ppermute | solution.py:291
  123.1 1.7 %collective-permute-done.21 = bf16[4,8,128,128]{3,2,1,0:T(8,128)(2,1)S(1)} collective-permute-done((bf16[4,8,128,128]{3,2,1,0:T(8,128)(2,1)S(1)}, bf16[4,8,128,128]{3,2,1,0:T(8,128)(2,1)S(1)}, u32[]{:S(2)}, u32[]{:S(2)}) %collective-permute-start.21) | collective-permute-done | bytes 1048608 | tf_op jit(solution)/shard_map/ppermute | solution.py:287
  130.4 2.2 %collective-permute-start.30 = (bf16[8,128,128]{2,1,0:T(8,128)(2,1)S(1)}, bf16[8,128,128]{2,1,0:T(8,128)(2,1)S(1)}, u32[]{:S(2)}, u32[]{:S(2)}) collective-permute-start(bf16[8,128,128]{2,1,0:T(8,128)(2,1)S(1)} %fusion.7), channel_id=1, source_target_pairs={{0,128},{128,0},{1,129},{129,1},{2,130},{130,2},{3,131},{131,3},{4... | collective-permute-start | bytes 786440 | tf_op jit(solution)/shard_map/ppermute | solution.py:295
  132.6 1.7 %collective-permute-done.22 = bf16[8,128,128]{2,1,0:T(8,128)(2,1)S(1)} collective-permute-done((bf16[8,128,128]{2,1,0:T(8,128)(2,1)S(1)}, bf16[8,128,128]{2,1,0:T(8,128)(2,1)S(1)}, u32[]{:S(2)}, u32[]{:S(2)}) %collective-permute-start.22) | collective-permute-done | bytes 262176 | tf_op jit(solution)/shard_map/ppermute | solution.py:291
  134.3 5.2 %collective-permute-done.24 = bf16[8,128,128]{2,1,0:T(8,128)(2,1)S(1)} collective-permute-done((bf16[8,128,128]{2,1,0:T(8,128)(2,1)S(1)}, bf16[8,128,128]{2,1,0:T(8,128)(2,1)S(1)}, u32[]{:S(2)}, u32[]{:S(2)}) %collective-permute-start.24) | collective-permute-done | bytes 262176 | tf_op jit(solution)/shard_map/ppermute | solution.py:291
  139.9 2.3 %collective-permute-start.25 = (bf16[8,128,128]{2,1,0:T(8,128)(2,1)S(1)}, bf16[8,128,128]{2,1,0:T(8,128)(2,1)S(1)}, u32[]{:S(2)}, u32[]{:S(2)}) collective-permute-start(bf16[8,128,128]{2,1,0:T(8,128)(2,1)S(1)} %fusion.9), channel_id=1, source_target_pairs={{0,128},{128,0},{1,129},{129,1},{2,130},{130,2},{3,131},{131,3},{4... | collective-permute-start | bytes 786440 | tf_op jit(solution)/shard_map/ppermute | solution.py:295
  143.0 5.6 %collective-permute-done.25 = bf16[8,128,128]{2,1,0:T(8,128)(2,1)S(1)} collective-permute-done((bf16[8,128,128]{2,1,0:T(8,128)(2,1)S(1)}, bf16[8,128,128]{2,1,0:T(8,128)(2,1)S(1)}, u32[]{:S(2)}, u32[]{:S(2)}) %collective-permute-start.25) | collective-permute-done | bytes 262176 | tf_op jit(solution)/shard_map/ppermute | solution.py:295
  149.4 1.9 %slice_bitcast_fusion.5 = (bf16[128,1024]{1,0:T(8,128)(2,1)}, bf16[128,1024]{1,0:T(8,128)(2,1)}) fusion(bf16[1,2,128,1024]{3,2,1,0:T(8,128)(2,1)} %reduce-scatter.2.cloned.1.call-done), kind=kLoop, calls=%fused_computation.30 | loop fusion | bytes 1048576 | tf_op jit(solution)/shard_map/unstack | solution.py:347
  (102 shorter events, 26.1 us)
Async XLA Ops:
  7.2 60.9 %all-gather.3.cloned.1.call-start = ((), (), s32[]{:S(2)}) async-start(), calls=%async_computation.2 | async-start | bytes 4718592 | tf_op jit(solution)/shard_map/all_gather | solution.py:338
  9.2 140.3 %reduce-scatter.2.cloned.1.call-start = ((), (), s32[]{:S(2)}) async-start(), calls=%async_computation.1 | async-start | bytes 4718592 | tf_op jit(solution)/shard_map/reduce_scatter | solution.py:326
  9.2 10.8 %collective-permute-start = (bf16[8,128,128]{2,1,0:T(8,128)(2,1)}, bf16[8,128,128]{2,1,0:T(8,128)(2,1)S(1)}, u32[]{:S(2)}, u32[]{:S(2)}) collective-permute-start(bf16[8,128,128]{2,1,0:T(8,128)(2,1)} %param.10), channel_id=1, source_target_pairs={{0,16},{8,24},{16,0},{24,8},{32,48},{40,56},{48,32},{56,40},{64,80... | collective-permute-start | bytes 786440 | tf_op jit(solution)/shard_map/ppermute | solution.py:287
  11.5 10.6 %collective-permute-start.10 = (bf16[8,128,128]{2,1,0:T(8,128)(2,1)}, bf16[8,128,128]{2,1,0:T(8,128)(2,1)S(1)}, u32[]{:S(2)}, u32[]{:S(2)}) collective-permute-start(bf16[8,128,128]{2,1,0:T(8,128)(2,1)} %param.11), channel_id=1, source_target_pairs={{0,64},{8,72},{16,80},{24,88},{32,96},{40,104},{48,112},{56,120},{... | collective-permute-start | bytes 786440 | tf_op jit(solution)/shard_map/ppermute | solution.py:291
  12.8 12.2 %collective-permute-start.9 = (bf16[8,128,128]{2,1,0:T(8,128)(2,1)}, bf16[8,128,128]{2,1,0:T(8,128)(2,1)S(1)}, u32[]{:S(2)}, u32[]{:S(2)}) collective-permute-start(bf16[8,128,128]{2,1,0:T(8,128)(2,1)} %param.11), channel_id=1, source_target_pairs={{0,96},{8,104},{16,112},{24,120},{32,0},{40,8},{48,16},{56,24},{64... | collective-permute-start | bytes 786440 | tf_op jit(solution)/shard_map/ppermute | solution.py:291
  13.9 12.9 %collective-permute-start.8 = (bf16[8,128,128]{2,1,0:T(8,128)(2,1)}, bf16[8,128,128]{2,1,0:T(8,128)(2,1)S(1)}, u32[]{:S(2)}, u32[]{:S(2)}) collective-permute-start(bf16[8,128,128]{2,1,0:T(8,128)(2,1)} %param.11), channel_id=1, source_target_pairs={{0,32},{8,40},{16,48},{24,56},{32,64},{40,72},{48,80},{56,88},{64,... | collective-permute-start | bytes 786440 | tf_op jit(solution)/shard_map/ppermute | solution.py:291
  25.1 14.8 %collective-permute-start.12 = (bf16[2,8,128,128]{3,2,1,0:T(8,128)(2,1)S(1)}, bf16[2,8,128,128]{3,2,1,0:T(8,128)(2,1)S(1)}, u32[]{:S(2)}, u32[]{:S(2)}) collective-permute-start(bf16[2,8,128,128]{3,2,1,0:T(8,128)(2,1)S(1)} %pad_maximum_fusion.3.refs_11_), channel_id=1, source_target_pairs={{0,16},{8,24},{16,0},{24,8},{32,48},{40,56},{48,32},{56,40},{64,80... | collective-permute-start | bytes 1572872 | tf_op jit(solution)/shard_map/ppermute | solution.py:287
  26.9 15.7 %collective-permute-start.13 = (bf16[2,8,128,128]{3,2,1,0:T(8,128)(2,1)S(1)}, bf16[2,8,128,128]{3,2,1,0:T(8,128)(2,1)S(1)}, u32[]{:S(2)}, u32[]{:S(2)}) collective-permute-start(bf16[2,8,128,128]{3,2,1,0:T(8,128)(2,1)S(1)} %pad_maximum_fusion.2.refs_10_), channel_id=1, source_target_pairs={{0,8},{8,0},{16,24},{24,16},{32,40},{40,32},{48,56},{56,48},{64,72... | collective-permute-start | bytes 1572872 | tf_op jit(solution)/shard_map/ppermute | solution.py:283
  27.1 23.6 %collective-permute-start.11 = (bf16[2,8,128,128]{3,2,1,0:T(8,128)(2,1)S(1)}, bf16[2,8,128,128]{3,2,1,0:T(8,128)(2,1)S(1)}, u32[]{:S(2)}, u32[]{:S(2)}) collective-permute-start(bf16[2,8,128,128]{3,2,1,0:T(8,128)(2,1)S(1)} %pad_maximum_fusion.2.refs_10_), channel_id=1, source_target_pairs={{0,16},{8,24},{16,0},{24,8},{32,48},{40,56},{48,32},{56,40},{64,80... | collective-permute-start | bytes 1572872 | tf_op jit(solution)/shard_map/ppermute | solution.py:287
  27.6 23.2 %collective-permute-start.4 = (bf16[2,8,128,128]{3,2,1,0:T(8,128)(2,1)S(1)}, bf16[2,8,128,128]{3,2,1,0:T(8,128)(2,1)S(1)}, u32[]{:S(2)}, u32[]{:S(2)}) collective-permute-start(bf16[2,8,128,128]{3,2,1,0:T(8,128)(2,1)S(1)} %pad_maximum_fusion.1.refs_1_), channel_id=1, source_target_pairs={{0,8},{8,0},{16,24},{24,16},{32,40},{40,32},{48,56},{56,48},{64,72... | collective-permute-start | bytes 1572872 | tf_op jit(solution)/shard_map/ppermute | solution.py:283
  27.6 23.6 %collective-permute-start.3 = (bf16[2,8,128,128]{3,2,1,0:T(8,128)(2,1)S(1)}, bf16[2,8,128,128]{3,2,1,0:T(8,128)(2,1)S(1)}, u32[]{:S(2)}, u32[]{:S(2)}) collective-permute-start(bf16[2,8,128,128]{3,2,1,0:T(8,128)(2,1)S(1)} %pad_maximum_fusion.1.refs_1_), channel_id=1, source_target_pairs={{0,64},{8,72},{16,80},{24,88},{32,96},{40,104},{48,112},{56,120},{... | collective-permute-start | bytes 1572872 | tf_op jit(solution)/shard_map/ppermute | solution.py:291
  39.9 14.7 %collective-permute-start.2 = (bf16[2,8,128,128]{3,2,1,0:T(8,128)(2,1)S(1)}, bf16[2,8,128,128]{3,2,1,0:T(8,128)(2,1)S(1)}, u32[]{:S(2)}, u32[]{:S(2)}) collective-permute-start(bf16[2,8,128,128]{3,2,1,0:T(8,128)(2,1)S(1)} %pad_maximum_fusion.1.refs_1_), channel_id=1, source_target_pairs={{0,96},{8,104},{16,112},{24,120},{32,0},{40,8},{48,16},{56,24},{64... | collective-permute-start | bytes 1572872 | tf_op jit(solution)/shard_map/ppermute | solution.py:291
  42.6 14.0 %collective-permute-start.1 = (bf16[2,8,128,128]{3,2,1,0:T(8,128)(2,1)S(1)}, bf16[2,8,128,128]{3,2,1,0:T(8,128)(2,1)S(1)}, u32[]{:S(2)}, u32[]{:S(2)}) collective-permute-start(bf16[2,8,128,128]{3,2,1,0:T(8,128)(2,1)S(1)} %pad_maximum_fusion.1.refs_1_), channel_id=1, source_target_pairs={{0,32},{8,40},{16,48},{24,56},{32,64},{40,72},{48,80},{56,88},{64,... | collective-permute-start | bytes 1572872 | tf_op jit(solution)/shard_map/ppermute | solution.py:291
  94.6 15.3 %collective-permute-start.19 = (bf16[2,8,128,128]{3,2,1,0:T(8,128)(2,1)S(1)}, bf16[2,8,128,128]{3,2,1,0:T(8,128)(2,1)S(1)}, u32[]{:S(2)}, u32[]{:S(2)}) collective-permute-start(bf16[2,8,128,128]{3,2,1,0:T(8,128)(2,1)S(1)} %get-tuple-element.33), channel_id=1, source_target_pairs={{0,32},{8,40},{16,48},{24,56},{32,64},{40,72},{48,80},{56,88},{64,... | collective-permute-start | bytes 1572872 | tf_op jit(solution)/shard_map/ppermute | solution.py:291
  96.2 25.9 %collective-permute-start.28 = (bf16[2,8,128,128]{3,2,1,0:T(8,128)(2,1)S(1)}, bf16[2,8,128,128]{3,2,1,0:T(8,128)(2,1)S(1)}, u32[]{:S(2)}, u32[]{:S(2)}) collective-permute-start(bf16[2,8,128,128]{3,2,1,0:T(8,128)(2,1)S(1)} %get-tuple-element.32), channel_id=1, source_target_pairs={{0,64},{8,72},{16,80},{24,88},{32,96},{40,104},{48,112},{56,120},{... | collective-permute-start | bytes 1572872 | tf_op jit(solution)/shard_map/ppermute | solution.py:291
  98.9 23.2 %collective-permute-start.27 = (bf16[2,8,128,128]{3,2,1,0:T(8,128)(2,1)S(1)}, bf16[2,8,128,128]{3,2,1,0:T(8,128)(2,1)S(1)}, u32[]{:S(2)}, u32[]{:S(2)}) collective-permute-start(bf16[2,8,128,128]{3,2,1,0:T(8,128)(2,1)S(1)} %get-tuple-element.34), channel_id=1, source_target_pairs={{0,96},{8,104},{16,112},{24,120},{32,0},{40,8},{48,16},{56,24},{64... | collective-permute-start | bytes 1572872 | tf_op jit(solution)/shard_map/ppermute | solution.py:291
  100.3 24.5 %collective-permute-start.21 = (bf16[4,8,128,128]{3,2,1,0:T(8,128)(2,1)S(1)}, bf16[4,8,128,128]{3,2,1,0:T(8,128)(2,1)S(1)}, u32[]{:S(2)}, u32[]{:S(2)}) collective-permute-start(bf16[4,8,128,128]{3,2,1,0:T(8,128)(2,1)S(1)} %fusion.1), channel_id=1, source_target_pairs={{0,16},{8,24},{16,0},{24,8},{32,48},{40,56},{48,32},{56,40},{64,80... | collective-permute-start | bytes 3145736 | tf_op jit(solution)/shard_map/ppermute | solution.py:287
  109.9 14.9 %collective-permute-start.20 = (bf16[1,4,8,128,128]{4,3,2,1,0:T(8,128)(2,1)S(1)}, bf16[1,4,8,128,128]{4,3,2,1,0:T(8,128)(2,1)S(1)}, u32[]{:S(2)}, u32[]{:S(2)}) collective-permute-start(bf16[1,4,8,128,128]{4,3,2,1,0:T(8,128)(2,1)S(1)} %copy-done.18), channel_id=1, source_target_pairs={{0,8},{8,0},{16,24},{24,16},{32,40},{40,32},{48,56},{56,48},{64,72... | collective-permute-start | bytes 3145736 | tf_op jit(solution)/shard_map/ppermute | solution.py:283
  122.5 7.8 %collective-permute-start.29 = (bf16[8,128,128]{2,1,0:T(8,128)(2,1)S(1)}, bf16[8,128,128]{2,1,0:T(8,128)(2,1)S(1)}, u32[]{:S(2)}, u32[]{:S(2)}) collective-permute-start(bf16[8,128,128]{2,1,0:T(8,128)(2,1)S(1)} %fusion.10), channel_id=1, source_target_pairs={{0,16},{8,24},{16,0},{24,8},{32,48},{40,56},{48,32},{56,40},{64,80... | collective-permute-start | bytes 786440 | tf_op jit(solution)/shard_map/ppermute | solution.py:287
  125.4 8.8 %collective-permute-start.22 = (bf16[8,128,128]{2,1,0:T(8,128)(2,1)S(1)}, bf16[8,128,128]{2,1,0:T(8,128)(2,1)S(1)}, u32[]{:S(2)}, u32[]{:S(2)}) collective-permute-start(bf16[8,128,128]{2,1,0:T(8,128)(2,1)S(1)} %get-tuple-element.35), channel_id=1, source_target_pairs={{0,32},{8,40},{16,48},{24,56},{32,64},{40,72},{48,80},{56,88},{64,... | collective-permute-start | bytes 786440 | tf_op jit(solution)/shard_map/ppermute | solution.py:291
  126.2 13.3 %collective-permute-start.24 = (bf16[8,128,128]{2,1,0:T(8,128)(2,1)S(1)}, bf16[8,128,128]{2,1,0:T(8,128)(2,1)S(1)}, u32[]{:S(2)}, u32[]{:S(2)}) collective-permute-start(bf16[8,128,128]{2,1,0:T(8,128)(2,1)S(1)} %get-tuple-element.36), channel_id=1, source_target_pairs={{0,64},{8,72},{16,80},{24,88},{32,96},{40,104},{48,112},{56,120},{... | collective-permute-start | bytes 786440 | tf_op jit(solution)/shard_map/ppermute | solution.py:291
  127.8 11.9 %collective-permute-start.23 = (bf16[8,128,128]{2,1,0:T(8,128)(2,1)S(1)}, bf16[8,128,128]{2,1,0:T(8,128)(2,1)S(1)}, u32[]{:S(2)}, u32[]{:S(2)}) collective-permute-start(bf16[8,128,128]{2,1,0:T(8,128)(2,1)S(1)} %get-tuple-element.37), channel_id=1, source_target_pairs={{0,96},{8,104},{16,112},{24,120},{32,0},{40,8},{48,16},{56,24},{64... | collective-permute-start | bytes 786440 | tf_op jit(solution)/shard_map/ppermute | solution.py:291
  130.4 11.8 %collective-permute-start.30 = (bf16[8,128,128]{2,1,0:T(8,128)(2,1)S(1)}, bf16[8,128,128]{2,1,0:T(8,128)(2,1)S(1)}, u32[]{:S(2)}, u32[]{:S(2)}) collective-permute-start(bf16[8,128,128]{2,1,0:T(8,128)(2,1)S(1)} %fusion.7), channel_id=1, source_target_pairs={{0,128},{128,0},{1,129},{129,1},{2,130},{130,2},{3,131},{131,3},{4... | collective-permute-start | bytes 786440 | tf_op jit(solution)/shard_map/ppermute | solution.py:295
  139.9 8.7 %collective-permute-start.25 = (bf16[8,128,128]{2,1,0:T(8,128)(2,1)S(1)}, bf16[8,128,128]{2,1,0:T(8,128)(2,1)S(1)}, u32[]{:S(2)}, u32[]{:S(2)}) collective-permute-start(bf16[8,128,128]{2,1,0:T(8,128)(2,1)S(1)} %fusion.9), channel_id=1, source_target_pairs={{0,128},{128,0},{1,129},{129,1},{2,130},{130,2},{3,131},{131,3},{4... | collective-permute-start | bytes 786440 | tf_op jit(solution)/shard_map/ppermute | solution.py:295
  (29 other events, 334.0 us)
Sparse Core Ops, SparseCore 0:
  10.4 57.6 all-gather.2
  88.0 53.8 reduce-scatter.1

commit v4 on v3

--- a/solution.py
+++ b/solution.py
@@ -348,19 +348,19 @@
     u1, d12, d30 = core_swap(up1), core_swap(down12), core_swap(down30)
     near = add(up_keep[1], u1[0]).astype(BF)
     u_y = y_swap(near)
-    d12 = after(d12, near)
+    u0 = core_swap(after(up0, near))
+    d12, d30, _ = lax.optimization_barrier((d12, d30, u0))
     t1, t2 = add(down_keep[0], d12[0]).astype(BF), add(down_keep[1], d12[1]).astype(BF)
     t3 = add(down_keep[2], d30[0]).astype(BF)
     d_x1, d_x3, d_x2 = x_shift(t1, 1), x_shift(t3, 3), x_shift(t2, 2)
-    u0 = core_swap(after(up0, d_x1))
     total = (add(up_keep[0], u0[0]) + u_y.astype(F32)).astype(BF)
     u_x1, u_x3, u_x2 = x_shift(total[1], 1), x_shift(total[3], 3), x_shift(total[2], 2)
     own = add(down_keep[3], d30[1]) + add(d_x1, d_x3) + d_x2.astype(F32)
-    d_y = y_swap(own[1].astype(BF))
+    d_y = y_swap(after(own[1].astype(BF), total))
     down_mine = (own[0] + d_y.astype(F32)).astype(BF)
     d_dp = dp_swap(down_mine)
     up_mine = (total[0].astype(F32) + add(u_x1, u_x3) + u_x2.astype(F32)).astype(BF)
-    u_dp = dp_swap(up_mine)
+    u_dp = after(dp_swap(up_mine), output, input_grad)
     return (output, input_grad, add(up_mine, u_dp), add(down_mine, d_dp))
 
 

time: 160 us -> 159 us (level)
  waiting for transfers between devices: 77.7 us -> 74.3 us
  starting transfers between devices: 29.5 us -> 31.6 us
    ppermute x12, waiting for transfers between devices: 37.6 us -> 21.6 us  [x_shift(): return lax.ppermute(a, 'fsdp', [(i, (i + 4 * d) % 16) for i in range(16)])]
    ppermute x5, waiting for transfers between devices: 20.8 us -> 34.8 us  [y_swap(): return lax.ppermute(a, 'fsdp', [(i, i ^ 2) for i in range(16)])]
    ppermute x2, waiting for transfers between devices: 5.57 us -> 3.56 us  [dp_swap(): return lax.ppermute(a, 'dp', [(0, 1), (1, 0)])]
    ppermute x12, starting transfers between devices: 17.8 us -> 19.4 us  [x_shift(): return lax.ppermute(a, 'fsdp', [(i, (i + 4 * d) % 16) for i in range(16)])]
  transfers between devices with their start and end apart: 33 -> 33, of which waited for: 17 -> 15; matrix products, arithmetic and copies ran while one was open for 4% -> 4% of each run, Pallas kernels for 3% -> 3%
where the time goes in v4:
time: 159 us; the launch traced here: 157 us
  waiting for transfers between devices  74.3 us (47%)
  starting transfers between devices  31.6 us (20%)
  Pallas kernels  24.3 us (15%)
  between operations  14.4 us (9%)
  other arithmetic  7.62 us (5%)
  local copies, waits for them, and re-layouts  4.69 us (3%)
    ppermute x5, waiting for transfers between devices, y_swap(): return lax.ppermute(a, 'fsdp', [(i, i ^ 2) for i in range(16)])  34.8 us
    ppermute x12, waiting for transfers between devices, x_shift(): return lax.ppermute(a, 'fsdp', [(i, (i + 4 * d) % 16) for i in range(16)])  21.6 us
    pallas_call x1, Pallas kernels, call(): pl.pallas_call(kernel, out_shape=tuple(out_shape), in_specs=[SMEM_SPEC] *...  19.7 us
    ppermute x12, starting transfers between devices, x_shift(): return lax.ppermute(a, 'fsdp', [(i, (i + 4 * d) % 16) for i in range(16)])  19.4 us
    all_gather x1, waiting for transfers between devices, body(): lax.all_gather(jnp.stack([activations, cotangent]), 'tensor', axis=0, til...  9.26 us
    ppermute x5, starting transfers between devices, y_swap(): return lax.ppermute(a, 'fsdp', [(i, i ^ 2) for i in range(16)])  5.57 us
    ppermute x12, waiting for transfers between devices, core_swap(): return lax.ppermute(a, 'fsdp', [(i, i ^ 1) for i in range(16)])  4.95 us
    ppermute x2, starting transfers between devices, dp_swap(): return lax.ppermute(a, 'dp', [(0, 1), (1, 0)])  4.71 us
  transfers between devices with their start and end apart: 33, of which 15 were waited for; matrix products, arithmetic and copies ran while one was open for 4% of the time, Pallas kernels for 3%

profile of v4, /device:TPU:8, one launch (start us, length us, event | category | flops | bytes accessed | tf_op | source)
XLA Modules:
  0.0 156.8 jit_solution(16412055400607207063)
XLA Ops:
  7.2 1.9 %pad_maximum_fusion = bf16[2,128,1024]{2,1,0:T(8,128)(2,1)} fusion(bf16[1,128,1024]{2,1,0:T(8,128)(2,1)} %bitcast.58, bf16[1,128,1024]{2,1,0:T(8,128)(2,1)} %bitcast.59), kind=kLoop, calls=%fused_computation.16 | loop fusion | flops 262144 | bytes 1048576 | tf_op jit(solution)/shard_map/stack | solution.py:338
  9.2 2.3 %collective-permute-start = (bf16[8,128,128]{2,1,0:T(8,128)(2,1)}, bf16[8,128,128]{2,1,0:T(8,128)(2,1)S(1)}, u32[]{:S(2)}, u32[]{:S(2)}) collective-permute-start(bf16[8,128,128]{2,1,0:T(8,128)(2,1)} %param.10), channel_id=1, source_target_pairs={{0,16},{8,24},{16,0},{24,8},{32,48},{40,56},{48,32},{56,40},{64,80... | collective-permute-start | bytes 786440 | tf_op jit(solution)/shard_map/ppermute | solution.py:287
  15.4 4.6 %plan.1 = (s32[128]{0:T(128)}, s32[128]{0:T(128)}) custom-call(s32[128]{0:T(128)} %bitcast.68, s32[128]{0:T(128)} %bitcast.69), custom_call_target="tpu_custom_call" | custom-call | tf_op jit(solution)/shard_map/plan/pallas_call | solution.py:55
  22.1 2.9 %collective-permute-done.9 = bf16[8,128,128]{2,1,0:T(8,128)(2,1)S(1)} collective-permute-done((bf16[8,128,128]{2,1,0:T(8,128)(2,1)}, bf16[8,128,128]{2,1,0:T(8,128)(2,1)S(1)}, u32[]{:S(2)}, u32[]{:S(2)}) %collective-permute-start.9) | collective-permute-done | bytes 262176 | tf_op jit(solution)/shard_map/ppermute | solution.py:291
  27.6 2.2 %collective-permute-start.3 = (bf16[2,8,128,128]{3,2,1,0:T(8,128)(2,1)S(1)}, bf16[2,8,128,128]{3,2,1,0:T(8,128)(2,1)S(1)}, u32[]{:S(2)}, u32[]{:S(2)}) collective-permute-start(bf16[2,8,128,128]{3,2,1,0:T(8,128)(2,1)S(1)} %pad_maximum_fusion.1.refs_1_), channel_id=1, source_target_pairs={{0,64},{8,72},{16,80},{24,88},{32,96},{40,104},{48,112},{56,120},{... | collective-permute-start | bytes 1572872 | tf_op jit(solution)/shard_map/ppermute | solution.py:291
  29.9 10.1 %collective-permute-done.12.refs_13_ = bf16[2,8,128,128]{3,2,1,0:T(8,128)(2,1)S(1)} collective-permute-done((bf16[2,8,128,128]{3,2,1,0:T(8,128)(2,1)S(1)}, bf16[2,8,128,128]{3,2,1,0:T(8,128)(2,1)S(1)}, u32[]{:S(2)}, u32[]{:S(2)}) %collective-permute-start.12) | collective-permute-done | bytes 524320 | tf_op jit(solution)/shard_map/ppermute | solution.py:287
  39.9 2.6 %collective-permute-start.2 = (bf16[2,8,128,128]{3,2,1,0:T(8,128)(2,1)S(1)}, bf16[2,8,128,128]{3,2,1,0:T(8,128)(2,1)S(1)}, u32[]{:S(2)}, u32[]{:S(2)}) collective-permute-start(bf16[2,8,128,128]{3,2,1,0:T(8,128)(2,1)S(1)} %pad_maximum_fusion.1.refs_1_), channel_id=1, source_target_pairs={{0,96},{8,104},{16,112},{24,120},{32,0},{40,8},{48,16},{56,24},{64... | collective-permute-start | bytes 1572872 | tf_op jit(solution)/shard_map/ppermute | solution.py:291
  42.6 8.1 %collective-permute-done.11.refs_12_ = bf16[2,8,128,128]{3,2,1,0:T(8,128)(2,1)S(1)} collective-permute-done((bf16[2,8,128,128]{3,2,1,0:T(8,128)(2,1)S(1)}, bf16[2,8,128,128]{3,2,1,0:T(8,128)(2,1)S(1)}, u32[]{:S(2)}, u32[]{:S(2)}) %collective-permute-start.11) | collective-permute-done | bytes 524320 | tf_op jit(solution)/shard_map/ppermute | solution.py:287
  51.3 3.3 %collective-permute-done.2.refs_3_ = bf16[2,8,128,128]{3,2,1,0:T(8,128)(2,1)S(1)} collective-permute-done((bf16[2,8,128,128]{3,2,1,0:T(8,128)(2,1)S(1)}, bf16[2,8,128,128]{3,2,1,0:T(8,128)(2,1)S(1)}, u32[]{:S(2)}, u32[]{:S(2)}) %collective-permute-start.2) | collective-permute-done | bytes 524320 | tf_op jit(solution)/shard_map/ppermute | solution.py:291
  54.6 2.0 %collective-permute-done.1.refs_2_ = bf16[2,8,128,128]{3,2,1,0:T(8,128)(2,1)S(1)} collective-permute-done((bf16[2,8,128,128]{3,2,1,0:T(8,128)(2,1)S(1)}, bf16[2,8,128,128]{3,2,1,0:T(8,128)(2,1)S(1)}, u32[]{:S(2)}, u32[]{:S(2)}) %collective-permute-start.1) | collective-permute-done | bytes 524320 | tf_op jit(solution)/shard_map/ppermute | solution.py:291
  58.8 9.3 %all-gather.3.cloned.1.call-done = bf16[16,128,1024]{2,1,0:T(8,128)(2,1)} async-done(((bf16[2,128,1024]{2,1,0:T(8,128)(2,1)}), bf16[16,128,1024]{2,1,0:T(8,128)(2,1)}) %all-gather.3.cloned.1.call-update) | async-done | bytes 4194320 | tf_op jit(solution)/shard_map/all_gather | solution.py:338
  68.1 19.7 %tile_pass.1 = (bf16[1,4,8,128,128]{4,3,2,1,0:T(8,128)(2,1)}, bf16[1,4,8,128,128]{4,3,2,1,0:T(8,128)(2,1)}, bf16[2,4,8,128,128]{4,3,2,1,0:T(8,128)(2,1)}, bf16[2...) custom-call(s32[128]{0:T(128)} %get-tuple-element.21.up_order, ...), custom_call_target="tpu_custom_call" | custom-call | flops 10000000 | bytes 100000 | tf_op jit(solution)/shard_map/tile_pass/pallas_call | solution.py:102
  89.1 1.8 %collective-permute-done.17 = bf16[1,4,8,128,128]{4,3,2,1,0:T(8,128)(2,1)S(1)} collective-permute-done((bf16[1,4,8,128,128]{4,3,2,1,0:T(8,128)(2,1)}, bf16[1,4,8,128,128]{4,3,2,1,0:T(8,128)(2,1)S(1)}, u32[]{:S(2)}, u32[]{:S(2)}) %collective-permute-start.17) | collective-permute-done | bytes 1048608 | tf_op jit(solution)/shard_map/ppermute | solution.py:283
  92.0 1.9 %collective-permute-done.24 = bf16[2,2,8,128,128]{4,3,2,1,0:T(8,128)(2,1)S(1)} collective-permute-done((bf16[2,2,8,128,128]{4,3,2,1,0:T(8,128)(2,1)}, bf16[2,2,8,128,128]{4,3,2,1,0:T(8,128)(2,1)S(1)}, u32[]{:S(2)}, u32[]{:S(2)}) %collective-permute-start.24) | collective-permute-done | bytes 1048608 | tf_op jit(solution)/shard_map/ppermute | solution.py:283
  97.5 2.7 %collective-permute-start.28 = (bf16[2,8,128,128]{3,2,1,0:T(8,128)(2,1)S(1)}, bf16[2,8,128,128]{3,2,1,0:T(8,128)(2,1)S(1)}, u32[]{:S(2)}, u32[]{:S(2)}) collective-permute-start(bf16[2,8,128,128]{3,2,1,0:T(8,128)(2,1)S(1)} %get-tuple-element.39), channel_id=1, source_target_pairs={{0,64},{8,72},{16,80},{24,88},{32,96},{40,104},{48,112},{56,120},{... | collective-permute-start | bytes 1572872 | tf_op jit(solution)/shard_map/ppermute | solution.py:291
  101.6 15.3 %collective-permute-done.19 = bf16[4,8,128,128]{3,2,1,0:T(8,128)(2,1)S(1)} collective-permute-done((bf16[4,8,128,128]{3,2,1,0:T(8,128)(2,1)S(1)}, bf16[4,8,128,128]{3,2,1,0:T(8,128)(2,1)S(1)}, u32[]{:S(2)}, u32[]{:S(2)}) %collective-permute-start.19) | collective-permute-done | bytes 1048608 | tf_op jit(solution)/shard_map/ppermute | solution.py:287
  117.5 5.9 %collective-permute-done.28 = bf16[2,8,128,128]{3,2,1,0:T(8,128)(2,1)S(1)} collective-permute-done((bf16[2,8,128,128]{3,2,1,0:T(8,128)(2,1)S(1)}, bf16[2,8,128,128]{3,2,1,0:T(8,128)(2,1)S(1)}, u32[]{:S(2)}, u32[]{:S(2)}) %collective-permute-start.28) | collective-permute-done | bytes 524320 | tf_op jit(solution)/shard_map/ppermute | solution.py:291
  124.5 1.7 %collective-permute-start.20 = (bf16[8,128,128]{2,1,0:T(8,128)(2,1)S(1)}, bf16[8,128,128]{2,1,0:T(8,128)(2,1)S(1)}, u32[]{:S(2)}, u32[]{:S(2)}) collective-permute-start(bf16[8,128,128]{2,1,0:T(8,128)(2,1)S(1)} %get-tuple-element.41), channel_id=1, source_target_pairs={{0,32},{8,40},{16,48},{24,56},{32,64},{40,72},{48,80},{56,88},{64,... | collective-permute-start | bytes 786440 | tf_op jit(solution)/shard_map/ppermute | solution.py:291
  126.2 2.4 %collective-permute-start.22 = (bf16[8,128,128]{2,1,0:T(8,128)(2,1)S(1)}, bf16[8,128,128]{2,1,0:T(8,128)(2,1)S(1)}, u32[]{:S(2)}, u32[]{:S(2)}) collective-permute-start(bf16[8,128,128]{2,1,0:T(8,128)(2,1)S(1)} %get-tuple-element.42), channel_id=1, source_target_pairs={{0,64},{8,72},{16,80},{24,88},{32,96},{40,104},{48,112},{56,120},{... | collective-permute-start | bytes 786440 | tf_op jit(solution)/shard_map/ppermute | solution.py:291
  131.5 2.2 %collective-permute-start.30 = (bf16[8,128,128]{2,1,0:T(8,128)(2,1)S(1)}, bf16[8,128,128]{2,1,0:T(8,128)(2,1)S(1)}, u32[]{:S(2)}, u32[]{:S(2)}) collective-permute-start(bf16[8,128,128]{2,1,0:T(8,128)(2,1)S(1)} %fusion.7), channel_id=1, source_target_pairs={{0,128},{128,0},{1,129},{129,1},{2,130},{130,2},{3,131},{131,3},{4... | collective-permute-start | bytes 786440 | tf_op jit(solution)/shard_map/ppermute | solution.py:295
  133.7 6.5 %collective-permute-done.22 = bf16[8,128,128]{2,1,0:T(8,128)(2,1)S(1)} collective-permute-done((bf16[8,128,128]{2,1,0:T(8,128)(2,1)S(1)}, bf16[8,128,128]{2,1,0:T(8,128)(2,1)S(1)}, u32[]{:S(2)}, u32[]{:S(2)}) %collective-permute-start.22) | collective-permute-done | bytes 262176 | tf_op jit(solution)/shard_map/ppermute | solution.py:291
  140.4 2.5 %collective-permute-start.23 = (bf16[8,128,128]{2,1,0:T(8,128)(2,1)S(1)}, bf16[8,128,128]{2,1,0:T(8,128)(2,1)S(1)}, u32[]{:S(2)}, u32[]{:S(2)}) collective-permute-start(bf16[8,128,128]{2,1,0:T(8,128)(2,1)S(1)} %fusion.9), channel_id=1, source_target_pairs={{0,128},{128,0},{1,129},{129,1},{2,130},{130,2},{3,131},{131,3},{4... | collective-permute-start | bytes 786440 | tf_op jit(solution)/shard_map/ppermute | solution.py:295
  143.7 1.9 %slice_bitcast_fusion.5 = (bf16[128,1024]{1,0:T(8,128)(2,1)}, bf16[128,1024]{1,0:T(8,128)(2,1)}) fusion(bf16[1,2,128,1024]{3,2,1,0:T(8,128)(2,1)} %reduce-scatter.2.cloned.1.call-done), kind=kLoop, calls=%fused_computation.30 | loop fusion | bytes 1048576 | tf_op jit(solution)/shard_map/unstack | solution.py:347
  145.6 3.6 %collective-permute-done.23 = bf16[8,128,128]{2,1,0:T(8,128)(2,1)S(1)} collective-permute-done((bf16[8,128,128]{2,1,0:T(8,128)(2,1)S(1)}, bf16[8,128,128]{2,1,0:T(8,128)(2,1)S(1)}, u32[]{:S(2)}, u32[]{:S(2)}) %collective-permute-start.23) | collective-permute-done | bytes 262176 | tf_op jit(solution)/shard_map/ppermute | solution.py:295
  (102 shorter events, 25.3 us)
Async XLA Ops:
  7.2 60.9 %all-gather.3.cloned.1.call-start = ((), (), s32[]{:S(2)}) async-start(), calls=%async_computation.2 | async-start | bytes 4718592 | tf_op jit(solution)/shard_map/all_gather | solution.py:338
  9.2 134.6 %reduce-scatter.2.cloned.1.call-start = ((), (), s32[]{:S(2)}) async-start(), calls=%async_computation.1 | async-start | bytes 4718592 | tf_op jit(solution)/shard_map/reduce_scatter | solution.py:326
  9.2 10.8 %collective-permute-start = (bf16[8,128,128]{2,1,0:T(8,128)(2,1)}, bf16[8,128,128]{2,1,0:T(8,128)(2,1)S(1)}, u32[]{:S(2)}, u32[]{:S(2)}) collective-permute-start(bf16[8,128,128]{2,1,0:T(8,128)(2,1)} %param.10), channel_id=1, source_target_pairs={{0,16},{8,24},{16,0},{24,8},{32,48},{40,56},{48,32},{56,40},{64,80... | collective-permute-start | bytes 786440 | tf_op jit(solution)/shard_map/ppermute | solution.py:287
  11.5 10.6 %collective-permute-start.10 = (bf16[8,128,128]{2,1,0:T(8,128)(2,1)}, bf16[8,128,128]{2,1,0:T(8,128)(2,1)S(1)}, u32[]{:S(2)}, u32[]{:S(2)}) collective-permute-start(bf16[8,128,128]{2,1,0:T(8,128)(2,1)} %param.11), channel_id=1, source_target_pairs={{0,64},{8,72},{16,80},{24,88},{32,96},{40,104},{48,112},{56,120},{... | collective-permute-start | bytes 786440 | tf_op jit(solution)/shard_map/ppermute | solution.py:291
  12.8 12.2 %collective-permute-start.9 = (bf16[8,128,128]{2,1,0:T(8,128)(2,1)}, bf16[8,128,128]{2,1,0:T(8,128)(2,1)S(1)}, u32[]{:S(2)}, u32[]{:S(2)}) collective-permute-start(bf16[8,128,128]{2,1,0:T(8,128)(2,1)} %param.11), channel_id=1, source_target_pairs={{0,96},{8,104},{16,112},{24,120},{32,0},{40,8},{48,16},{56,24},{64... | collective-permute-start | bytes 786440 | tf_op jit(solution)/shard_map/ppermute | solution.py:291
  13.9 12.9 %collective-permute-start.8 = (bf16[8,128,128]{2,1,0:T(8,128)(2,1)}, bf16[8,128,128]{2,1,0:T(8,128)(2,1)S(1)}, u32[]{:S(2)}, u32[]{:S(2)}) collective-permute-start(bf16[8,128,128]{2,1,0:T(8,128)(2,1)} %param.11), channel_id=1, source_target_pairs={{0,32},{8,40},{16,48},{24,56},{32,64},{40,72},{48,80},{56,88},{64,... | collective-permute-start | bytes 786440 | tf_op jit(solution)/shard_map/ppermute | solution.py:291
  25.1 14.8 %collective-permute-start.12 = (bf16[2,8,128,128]{3,2,1,0:T(8,128)(2,1)S(1)}, bf16[2,8,128,128]{3,2,1,0:T(8,128)(2,1)S(1)}, u32[]{:S(2)}, u32[]{:S(2)}) collective-permute-start(bf16[2,8,128,128]{3,2,1,0:T(8,128)(2,1)S(1)} %pad_maximum_fusion.3.refs_11_), channel_id=1, source_target_pairs={{0,16},{8,24},{16,0},{24,8},{32,48},{40,56},{48,32},{56,40},{64,80... | collective-permute-start | bytes 1572872 | tf_op jit(solution)/shard_map/ppermute | solution.py:287
  26.9 15.7 %collective-permute-start.13 = (bf16[2,8,128,128]{3,2,1,0:T(8,128)(2,1)S(1)}, bf16[2,8,128,128]{3,2,1,0:T(8,128)(2,1)S(1)}, u32[]{:S(2)}, u32[]{:S(2)}) collective-permute-start(bf16[2,8,128,128]{3,2,1,0:T(8,128)(2,1)S(1)} %pad_maximum_fusion.2.refs_10_), channel_id=1, source_target_pairs={{0,8},{8,0},{16,24},{24,16},{32,40},{40,32},{48,56},{56,48},{64,72... | collective-permute-start | bytes 1572872 | tf_op jit(solution)/shard_map/ppermute | solution.py:283
  27.1 23.6 %collective-permute-start.11 = (bf16[2,8,128,128]{3,2,1,0:T(8,128)(2,1)S(1)}, bf16[2,8,128,128]{3,2,1,0:T(8,128)(2,1)S(1)}, u32[]{:S(2)}, u32[]{:S(2)}) collective-permute-start(bf16[2,8,128,128]{3,2,1,0:T(8,128)(2,1)S(1)} %pad_maximum_fusion.2.refs_10_), channel_id=1, source_target_pairs={{0,16},{8,24},{16,0},{24,8},{32,48},{40,56},{48,32},{56,40},{64,80... | collective-permute-start | bytes 1572872 | tf_op jit(solution)/shard_map/ppermute | solution.py:287
  27.6 23.2 %collective-permute-start.4 = (bf16[2,8,128,128]{3,2,1,0:T(8,128)(2,1)S(1)}, bf16[2,8,128,128]{3,2,1,0:T(8,128)(2,1)S(1)}, u32[]{:S(2)}, u32[]{:S(2)}) collective-permute-start(bf16[2,8,128,128]{3,2,1,0:T(8,128)(2,1)S(1)} %pad_maximum_fusion.1.refs_1_), channel_id=1, source_target_pairs={{0,8},{8,0},{16,24},{24,16},{32,40},{40,32},{48,56},{56,48},{64,72... | collective-permute-start | bytes 1572872 | tf_op jit(solution)/shard_map/ppermute | solution.py:283
  27.6 23.6 %collective-permute-start.3 = (bf16[2,8,128,128]{3,2,1,0:T(8,128)(2,1)S(1)}, bf16[2,8,128,128]{3,2,1,0:T(8,128)(2,1)S(1)}, u32[]{:S(2)}, u32[]{:S(2)}) collective-permute-start(bf16[2,8,128,128]{3,2,1,0:T(8,128)(2,1)S(1)} %pad_maximum_fusion.1.refs_1_), channel_id=1, source_target_pairs={{0,64},{8,72},{16,80},{24,88},{32,96},{40,104},{48,112},{56,120},{... | collective-permute-start | bytes 1572872 | tf_op jit(solution)/shard_map/ppermute | solution.py:291
  39.9 14.7 %collective-permute-start.2 = (bf16[2,8,128,128]{3,2,1,0:T(8,128)(2,1)S(1)}, bf16[2,8,128,128]{3,2,1,0:T(8,128)(2,1)S(1)}, u32[]{:S(2)}, u32[]{:S(2)}) collective-permute-start(bf16[2,8,128,128]{3,2,1,0:T(8,128)(2,1)S(1)} %pad_maximum_fusion.1.refs_1_), channel_id=1, source_target_pairs={{0,96},{8,104},{16,112},{24,120},{32,0},{40,8},{48,16},{56,24},{64... | collective-permute-start | bytes 1572872 | tf_op jit(solution)/shard_map/ppermute | solution.py:291
  42.6 14.0 %collective-permute-start.1 = (bf16[2,8,128,128]{3,2,1,0:T(8,128)(2,1)S(1)}, bf16[2,8,128,128]{3,2,1,0:T(8,128)(2,1)S(1)}, u32[]{:S(2)}, u32[]{:S(2)}) collective-permute-start(bf16[2,8,128,128]{3,2,1,0:T(8,128)(2,1)S(1)} %pad_maximum_fusion.1.refs_1_), channel_id=1, source_target_pairs={{0,32},{8,40},{16,48},{24,56},{32,64},{40,72},{48,80},{56,88},{64,... | collective-permute-start | bytes 1572872 | tf_op jit(solution)/shard_map/ppermute | solution.py:291
  50.7 5.9 %collective-permute-start.15 = (bf16[2,8,128,128]{3,2,1,0:T(8,128)(2,1)S(1)}, bf16[2,8,128,128]{3,2,1,0:T(8,128)(2,1)S(1)}, u32[]{:S(2)}, u32[]{:S(2)}) collective-permute-start(bf16[2,8,128,128]{3,2,1,0:T(8,128)(2,1)S(1)} %collective-permute-done.11.refs_12_), channel_id=1, source_target_pairs={{0,8},{8,0},{16,24},{24,16},{32,40},{40,32},{48,56},{56,48},{64,72... | collective-permute-start | bytes 1572872 | tf_op jit(solution)/shard_map/ppermute | solution.py:283
  91.5 25.4 %collective-permute-start.19 = (bf16[4,8,128,128]{3,2,1,0:T(8,128)(2,1)S(1)}, bf16[4,8,128,128]{3,2,1,0:T(8,128)(2,1)S(1)}, u32[]{:S(2)}, u32[]{:S(2)}) collective-permute-start(bf16[4,8,128,128]{3,2,1,0:T(8,128)(2,1)S(1)} %fusion.1), channel_id=1, source_target_pairs={{0,16},{8,24},{16,0},{24,8},{32,48},{40,56},{48,32},{56,40},{64,80... | collective-permute-start | bytes 3145736 | tf_op jit(solution)/shard_map/ppermute | solution.py:287
  95.9 21.5 %collective-permute-start.26 = (bf16[2,8,128,128]{3,2,1,0:T(8,128)(2,1)S(1)}, bf16[2,8,128,128]{3,2,1,0:T(8,128)(2,1)S(1)}, u32[]{:S(2)}, u32[]{:S(2)}) collective-permute-start(bf16[2,8,128,128]{3,2,1,0:T(8,128)(2,1)S(1)} %get-tuple-element.38), channel_id=1, source_target_pairs={{0,32},{8,40},{16,48},{24,56},{32,64},{40,72},{48,80},{56,88},{64,... | collective-permute-start | bytes 1572872 | tf_op jit(solution)/shard_map/ppermute | solution.py:291
  97.5 25.9 %collective-permute-start.28 = (bf16[2,8,128,128]{3,2,1,0:T(8,128)(2,1)S(1)}, bf16[2,8,128,128]{3,2,1,0:T(8,128)(2,1)S(1)}, u32[]{:S(2)}, u32[]{:S(2)}) collective-permute-start(bf16[2,8,128,128]{3,2,1,0:T(8,128)(2,1)S(1)} %get-tuple-element.39), channel_id=1, source_target_pairs={{0,64},{8,72},{16,80},{24,88},{32,96},{40,104},{48,112},{56,120},{... | collective-permute-start | bytes 1572872 | tf_op jit(solution)/shard_map/ppermute | solution.py:291
  100.2 23.2 %collective-permute-start.27 = (bf16[2,8,128,128]{3,2,1,0:T(8,128)(2,1)S(1)}, bf16[2,8,128,128]{3,2,1,0:T(8,128)(2,1)S(1)}, u32[]{:S(2)}, u32[]{:S(2)}) collective-permute-start(bf16[2,8,128,128]{3,2,1,0:T(8,128)(2,1)S(1)} %get-tuple-element.40), channel_id=1, source_target_pairs={{0,96},{8,104},{16,112},{24,120},{32,0},{40,8},{48,16},{56,24},{64... | collective-permute-start | bytes 1572872 | tf_op jit(solution)/shard_map/ppermute | solution.py:291
  123.8 7.6 %collective-permute-start.29 = (bf16[8,128,128]{2,1,0:T(8,128)(2,1)S(1)}, bf16[8,128,128]{2,1,0:T(8,128)(2,1)S(1)}, u32[]{:S(2)}, u32[]{:S(2)}) collective-permute-start(bf16[8,128,128]{2,1,0:T(8,128)(2,1)S(1)} %fusion.10), channel_id=1, source_target_pairs={{0,16},{8,24},{16,0},{24,8},{32,48},{40,56},{48,32},{56,40},{64,80... | collective-permute-start | bytes 786440 | tf_op jit(solution)/shard_map/ppermute | solution.py:287
  124.5 9.2 %collective-permute-start.20 = (bf16[8,128,128]{2,1,0:T(8,128)(2,1)S(1)}, bf16[8,128,128]{2,1,0:T(8,128)(2,1)S(1)}, u32[]{:S(2)}, u32[]{:S(2)}) collective-permute-start(bf16[8,128,128]{2,1,0:T(8,128)(2,1)S(1)} %get-tuple-element.41), channel_id=1, source_target_pairs={{0,32},{8,40},{16,48},{24,56},{32,64},{40,72},{48,80},{56,88},{64,... | collective-permute-start | bytes 786440 | tf_op jit(solution)/shard_map/ppermute | solution.py:291
  126.2 14.0 %collective-permute-start.22 = (bf16[8,128,128]{2,1,0:T(8,128)(2,1)S(1)}, bf16[8,128,128]{2,1,0:T(8,128)(2,1)S(1)}, u32[]{:S(2)}, u32[]{:S(2)}) collective-permute-start(bf16[8,128,128]{2,1,0:T(8,128)(2,1)S(1)} %get-tuple-element.42), channel_id=1, source_target_pairs={{0,64},{8,72},{16,80},{24,88},{32,96},{40,104},{48,112},{56,120},{... | collective-permute-start | bytes 786440 | tf_op jit(solution)/shard_map/ppermute | solution.py:291
  128.6 11.6 %collective-permute-start.21 = (bf16[8,128,128]{2,1,0:T(8,128)(2,1)S(1)}, bf16[8,128,128]{2,1,0:T(8,128)(2,1)S(1)}, u32[]{:S(2)}, u32[]{:S(2)}) collective-permute-start(bf16[8,128,128]{2,1,0:T(8,128)(2,1)S(1)} %get-tuple-element.43), channel_id=1, source_target_pairs={{0,96},{8,104},{16,112},{24,120},{32,0},{40,8},{48,16},{56,24},{64... | collective-permute-start | bytes 786440 | tf_op jit(solution)/shard_map/ppermute | solution.py:291
  131.5 11.4 %collective-permute-start.30 = (bf16[8,128,128]{2,1,0:T(8,128)(2,1)S(1)}, bf16[8,128,128]{2,1,0:T(8,128)(2,1)S(1)}, u32[]{:S(2)}, u32[]{:S(2)}) collective-permute-start(bf16[8,128,128]{2,1,0:T(8,128)(2,1)S(1)} %fusion.7), channel_id=1, source_target_pairs={{0,128},{128,0},{1,129},{129,1},{2,130},{130,2},{3,131},{131,3},{4... | collective-permute-start | bytes 786440 | tf_op jit(solution)/shard_map/ppermute | solution.py:295
  140.4 8.8 %collective-permute-start.23 = (bf16[8,128,128]{2,1,0:T(8,128)(2,1)S(1)}, bf16[8,128,128]{2,1,0:T(8,128)(2,1)S(1)}, u32[]{:S(2)}, u32[]{:S(2)}) collective-permute-start(bf16[8,128,128]{2,1,0:T(8,128)(2,1)S(1)} %fusion.9), channel_id=1, source_target_pairs={{0,128},{128,0},{1,129},{129,1},{2,130},{130,2},{3,131},{131,3},{4... | collective-permute-start | bytes 786440 | tf_op jit(solution)/shard_map/ppermute | solution.py:295
  (29 other events, 320.6 us)
Sparse Core Ops, SparseCore 0:
  10.4 57.6 all-gather.2
  88.0 53.8 reduce-scatter.1

commit v5 on v4

--- a/solution.py
+++ b/solution.py
@@ -295,6 +295,27 @@
     return lax.ppermute(a, "dp", [(0, 1), (1, 0)])
 
 
+def z_up(a):
+    return lax.ppermute(a, "tensor", [(i, (i + 1) % 8) for i in range(8)])
+
+
+def z_down(a):
+    return lax.ppermute(a, "tensor", [(i, (i + 7) % 8) for i in range(8)])
+
+
+def ring_gather(a, *before_last):
+    arrays, places = [a], [(0, None, (0,), None)]
+    up = down = a
+    for k in (1, 2, 3, 4):
+        up = z_up(up if k < 4 else after(up, *before_last))
+        down = z_down(down) if k < 4 else None
+        for part, shift in ((up, -k), (down, k)):
+            if part is not None:
+                places.append((len(arrays), None, (shift,), None))
+                arrays.append(part)
+    return Wide(tuple(arrays), places)
+
+
 def gather_up(tiles, *early):
     both = after(jnp.stack([tiles, y_swap(tiles)]), *early)
     mine = [both] + [x_shift(both, d) for d in (1, 3, 2)]
@@ -335,11 +356,11 @@
     pos = jnp.stack([lax.axis_index("tensor"), f >> 2, (f >> 1) & 1, f & 1]).astype(jnp.int32)
     rows, cols = up_rows[:, 0], down_cols[:, 0]
     up_order, down_order = plan(up_cols[:, 0], down_rows[:, 0])
-    pair = lax.all_gather(jnp.stack([activations, cotangent]), "tensor", axis=0, tiled=False)
-    x = Wide((pair,), [(0, (z, 0), z, None) for z in range(8)])
-    cot = Wide((pair,), [(0, (z, 1), z, None) for z in range(8)])
+    wide = lax.all_gather(cotangent, "tensor", axis=0, tiled=False)
+    cot = Wide((wide,), [(0, z, z, None) for z in range(8)])
     up = gather_up(up_tiles, up_order, down_order, pos)
     down = gather_down(down_tiles, up.arrays[0])
+    x = ring_gather(activations, *up.arrays[1:3], *down.arrays[2:4])
 
     (up0, up1, up_keep), (down12, down30, down_keep), parts = tile_pass(
         up_order, rows, down_order, cols, pos, x, cot, up, down

time: 159 us -> 172 us (1.082)
  starting transfers between devices: 31.6 us -> 44.2 us
  waiting for transfers between devices: 74.3 us -> 76.4 us
  other arithmetic: 7.62 us -> 5.72 us
    ppermute x0 -> x7, waiting for transfers between devices: none -> 31.9 us  [the longest x4 21.2 us: z_up(): return lax.ppermute(a, 'tensor', [(i, (i + 1) % 8) for i in range(8)])]
    ppermute x5, waiting for transfers between devices: 34.8 us -> 20.2 us  [y_swap(): return lax.ppermute(a, 'fsdp', [(i, i ^ 2) for i in range(16)])]
    ppermute x0 -> x7, starting transfers between devices: none -> 11.7 us  [the longest x3 11.5 us: z_down(): return lax.ppermute(a, 'tensor', [(i, (i + 7) % 8) for i in range(8)])]
    all_gather x1, waiting for transfers between devices: 9.26 us -> 0.01 us  [body(): wide = lax.all_gather(cotangent, 'tensor', axis=0, tiled=False)]
    ppermute x12, waiting for transfers between devices: 21.6 us -> 16 us  [x_shift(): return lax.ppermute(a, 'fsdp', [(i, (i + 4 * d) % 16) for i in range(16)])]
    another operation x1 -> x0, other arithmetic: 1.9 us -> none  [body(): jnp.stack([activations, cotangent])]
  transfers between devices with their start and end apart: 33 -> 40, of which waited for: 15 -> 17; matrix products, arithmetic and copies ran while one was open for 4% -> 4% of each run, Pallas kernels for 3% -> 3%
where the time goes in v5:
time: 172 us; the launch traced here: 170 us
  waiting for transfers between devices  76.4 us (44%)
  starting transfers between devices  44.2 us (26%)
  Pallas kernels  24.3 us (14%)
  between operations  14.5 us (8%)
  other arithmetic  5.72 us (3%)
  local copies, waits for them, and re-layouts  5.17 us (3%)
    ppermute x4, waiting for transfers between devices, z_up(): return lax.ppermute(a, 'tensor', [(i, (i + 1) % 8) for i in range(8)])  21.2 us
    ppermute x12, starting transfers between devices, x_shift(): return lax.ppermute(a, 'fsdp', [(i, (i + 4 * d) % 16) for i in range(16)])  20.6 us
    ppermute x5, waiting for transfers between devices, y_swap(): return lax.ppermute(a, 'fsdp', [(i, i ^ 2) for i in range(16)])  20.2 us
    pallas_call x1, Pallas kernels, call(): pl.pallas_call(kernel, out_shape=tuple(out_shape), in_specs=[SMEM_SPEC] *...  19.7 us
    ppermute x12, waiting for transfers between devices, x_shift(): return lax.ppermute(a, 'fsdp', [(i, (i + 4 * d) % 16) for i in range(16)])  16 us
    ppermute x3, starting transfers between devices, z_down(): return lax.ppermute(a, 'tensor', [(i, (i + 7) % 8) for i in range(8)])  11.5 us
    ppermute x3, waiting for transfers between devices, z_down(): return lax.ppermute(a, 'tensor', [(i, (i + 7) % 8) for i in range(8)])  10.7 us
    ppermute x2, starting transfers between devices, dp_swap(): return lax.ppermute(a, 'dp', [(0, 1), (1, 0)])  4.96 us
  transfers between devices with their start and end apart: 40, of which 17 were waited for; matrix products, arithmetic and copies ran while one was open for 4% of the time, Pallas kernels for 3%

profile of v5, /device:TPU:8, one launch (start us, length us, event | category | flops | bytes accessed | tf_op | source)
XLA Modules:
  0.0 170.3 jit_solution(8367189670355625273)
XLA Ops:
  8.0 2.3 %collective-permute-start.6 = (bf16[8,128,128]{2,1,0:T(8,128)(2,1)}, bf16[8,128,128]{2,1,0:T(8,128)(2,1)S(1)}, u32[]{:S(2)}, u32[]{:S(2)}) collective-permute-start(bf16[8,128,128]{2,1,0:T(8,128)(2,1)} %param.10), channel_id=1, source_target_pairs={{0,16},{8,24},{16,0},{24,8},{32,48},{40,56},{48,32},{56,40},{64,80... | collective-permute-start | bytes 786440 | tf_op jit(solution)/shard_map/ppermute | solution.py:287
  11.9 2.7 %collective-permute-start.12 = (bf16[8,128,128]{2,1,0:T(8,128)(2,1)}, bf16[8,128,128]{2,1,0:T(8,128)(2,1)S(1)}, u32[]{:S(2)}, u32[]{:S(2)}) collective-permute-start(bf16[8,128,128]{2,1,0:T(8,128)(2,1)} %param.11), channel_id=1, source_target_pairs={{0,64},{8,72},{16,80},{24,88},{32,96},{40,104},{48,112},{56,120},{... | collective-permute-start | bytes 786440 | tf_op jit(solution)/shard_map/ppermute | solution.py:291
  16.3 5.9 %collective-permute-start.1 = (bf16[128,1024]{1,0:T(8,128)(2,1)}, bf16[128,1024]{1,0:T(8,128)(2,1)}, u32[]{:S(2)}, u32[]{:S(2)}) collective-permute-start(bf16[128,1024]{1,0:T(8,128)(2,1)} %refs_0_.1), channel_id=1, source_target_pairs={{0,7},{1,0},{2,1},{3,2},{4,3},{5,4},{6,5},{7,6},{8,15},{9,8},{10,9... | collective-permute-start | bytes 786440 | tf_op jit(solution)/shard_map/ppermute | solution.py:303
  22.8 4.6 %plan.1 = (s32[128]{0:T(128)}, s32[128]{0:T(128)}) custom-call(s32[128]{0:T(128)} %bitcast.63, s32[128]{0:T(128)} %bitcast.64), custom_call_target="tpu_custom_call" | custom-call | tf_op jit(solution)/shard_map/plan/pallas_call | solution.py:55
  29.1 2.3 %collective-permute-done.1.refs_2_ = bf16[128,1024]{1,0:T(8,128)(2,1)} collective-permute-done((bf16[128,1024]{1,0:T(8,128)(2,1)}, bf16[128,1024]{1,0:T(8,128)(2,1)}, u32[]{:S(2)}, u32[]{:S(2)}) %collective-permute-start.1) | collective-permute-done | bytes 262176 | tf_op jit(solution)/shard_map/ppermute | solution.py:303
  31.5 3.7 %collective-permute-start.3 = (bf16[128,1024]{1,0:T(8,128)(2,1)}, bf16[128,1024]{1,0:T(8,128)(2,1)S(1)}, u32[]{:S(2)}, u32[]{:S(2)}) collective-permute-start(bf16[128,1024]{1,0:T(8,128)(2,1)} %collective-permute-done.1.refs_2_), channel_id=1, source_target_pairs={{0,7},{1,0},{2,1},{3,2},{4,3},{5,4},{6,5},{7,6},{8,15},{9,8},{10,9... | collective-permute-start | bytes 786440 | tf_op jit(solution)/shard_map/ppermute | solution.py:303
  35.4 2.9 %collective-permute-start.8 = (bf16[2,8,128,128]{3,2,1,0:T(8,128)(2,1)S(1)}, bf16[2,8,128,128]{3,2,1,0:T(8,128)(2,1)S(1)}, u32[]{:S(2)}, u32[]{:S(2)}) collective-permute-start(bf16[2,8,128,128]{3,2,1,0:T(8,128)(2,1)S(1)} %pad_maximum_fusion.refs_8_), channel_id=1, source_target_pairs={{0,96},{8,104},{16,112},{24,120},{32,0},{40,8},{48,16},{56,24},{64... | collective-permute-start | bytes 1572872 | tf_op jit(solution)/shard_map/ppermute | solution.py:291
  38.3 3.1 %collective-permute-done.2.refs_3_ = bf16[128,1024]{1,0:T(8,128)(2,1)S(1)} collective-permute-done((bf16[128,1024]{1,0:T(8,128)(2,1)S(1)}, bf16[128,1024]{1,0:T(8,128)(2,1)S(1)}, u32[]{:S(2)}, u32[]{:S(2)}) %collective-permute-start.2) | collective-permute-done | bytes 262176 | tf_op jit(solution)/shard_map/ppermute | solution.py:299
  44.8 13.9 %collective-permute-done.4.refs_5_ = bf16[128,1024]{1,0:T(8,128)(2,1)S(1)} collective-permute-done((bf16[128,1024]{1,0:T(8,128)(2,1)S(1)}, bf16[128,1024]{1,0:T(8,128)(2,1)S(1)}, u32[]{:S(2)}, u32[]{:S(2)}) %collective-permute-start.4) | collective-permute-done | bytes 262176 | tf_op jit(solution)/shard_map/ppermute | solution.py:299
  59.3 2.6 %collective-permute-start.15 = (bf16[2,8,128,128]{3,2,1,0:T(8,128)(2,1)S(1)}, bf16[2,8,128,128]{3,2,1,0:T(8,128)(2,1)S(1)}, u32[]{:S(2)}, u32[]{:S(2)}) collective-permute-start(bf16[2,8,128,128]{3,2,1,0:T(8,128)(2,1)S(1)} %pad_maximum_fusion.refs_8_), channel_id=1, source_target_pairs={{0,64},{8,72},{16,80},{24,88},{32,96},{40,104},{48,112},{56,120},{... | collective-permute-start | bytes 1572872 | tf_op jit(solution)/shard_map/ppermute | solution.py:291
  62.0 1.9 %collective-permute-start.5 = (bf16[128,1024]{1,0:T(8,128)(2,1)S(1)}, bf16[128,1024]{1,0:T(8,128)(2,1)S(1)}, u32[]{:S(2)}, u32[]{:S(2)}) collective-permute-start(bf16[128,1024]{1,0:T(8,128)(2,1)S(1)} %collective-permute-done.3.refs_4_), channel_id=1, source_target_pairs={{0,7},{1,0},{2,1},{3,2},{4,3},{5,4},{6,5},{7,6},{8,15},{9,8},{10,9... | collective-permute-start | bytes 786440 | tf_op jit(solution)/shard_map/ppermute | solution.py:303
  63.9 6.4 %collective-permute-done.5.refs_6_ = bf16[128,1024]{1,0:T(8,128)(2,1)S(1)} collective-permute-done((bf16[128,1024]{1,0:T(8,128)(2,1)S(1)}, bf16[128,1024]{1,0:T(8,128)(2,1)S(1)}, u32[]{:S(2)}, u32[]{:S(2)}) %collective-permute-start.5) | collective-permute-done | bytes 262176 | tf_op jit(solution)/shard_map/ppermute | solution.py:303
  71.7 3.4 %collective-permute-done.15.refs_11_ = bf16[2,8,128,128]{3,2,1,0:T(8,128)(2,1)S(1)} collective-permute-done((bf16[2,8,128,128]{3,2,1,0:T(8,128)(2,1)S(1)}, bf16[2,8,128,128]{3,2,1,0:T(8,128)(2,1)S(1)}, u32[]{:S(2)}, u32[]{:S(2)}) %collective-permute-start.15) | collective-permute-done | bytes 524320 | tf_op jit(solution)/shard_map/ppermute | solution.py:291
  75.1 4.1 %collective-permute-done.14.refs_7_ = bf16[128,1024]{1,0:T(8,128)(2,1)S(1)} collective-permute-done((bf16[128,1024]{1,0:T(8,128)(2,1)S(1)}, bf16[128,1024]{1,0:T(8,128)(2,1)S(1)}, u32[]{:S(2)}, u32[]{:S(2)}) %collective-permute-start.14) | collective-permute-done | bytes 262176 | tf_op jit(solution)/shard_map/ppermute | solution.py:299
  81.4 19.7 %tile_pass.1 = (bf16[1,4,8,128,128]{4,3,2,1,0:T(8,128)(2,1)}, bf16[1,4,8,128,128]{4,3,2,1,0:T(8,128)(2,1)}, bf16[2,4,8,128,128]{4,3,2,1,0:T(8,128)(2,1)}, bf16[2...) custom-call(s32[128]{0:T(128)} %get-tuple-element.22.up_order, ...), custom_call_target="tpu_custom_call" | custom-call | flops 10000000 | bytes 100000 | tf_op jit(solution)/shard_map/tile_pass/pallas_call | solution.py:102
  110.2 2.1 %collective-permute-start.35 = (bf16[2,8,128,128]{3,2,1,0:T(8,128)(2,1)S(1)}, bf16[2,8,128,128]{3,2,1,0:T(8,128)(2,1)S(1)}, u32[]{:S(2)}, u32[]{:S(2)}) collective-permute-start(bf16[2,8,128,128]{3,2,1,0:T(8,128)(2,1)S(1)} %get-tuple-element.41), channel_id=1, source_target_pairs={{0,64},{8,72},{16,80},{24,88},{32,96},{40,104},{48,112},{56,120},{... | collective-permute-start | bytes 1572872 | tf_op jit(solution)/shard_map/ppermute | solution.py:291
  113.0 17.2 %collective-permute-done.26 = bf16[4,8,128,128]{3,2,1,0:T(8,128)(2,1)S(1)} collective-permute-done((bf16[4,8,128,128]{3,2,1,0:T(8,128)(2,1)S(1)}, bf16[4,8,128,128]{3,2,1,0:T(8,128)(2,1)S(1)}, u32[]{:S(2)}, u32[]{:S(2)}) %collective-permute-start.26) | collective-permute-done | bytes 1048608 | tf_op jit(solution)/shard_map/ppermute | solution.py:287
  130.7 5.4 %collective-permute-done.33 = bf16[2,8,128,128]{3,2,1,0:T(8,128)(2,1)S(1)} collective-permute-done((bf16[2,8,128,128]{3,2,1,0:T(8,128)(2,1)S(1)}, bf16[2,8,128,128]{3,2,1,0:T(8,128)(2,1)S(1)}, u32[]{:S(2)}, u32[]{:S(2)}) %collective-permute-start.33) | collective-permute-done | bytes 524320 | tf_op jit(solution)/shard_map/ppermute | solution.py:291
  138.5 3.6 %collective-permute-start.29 = (bf16[8,128,128]{2,1,0:T(8,128)(2,1)S(1)}, bf16[8,128,128]{2,1,0:T(8,128)(2,1)S(1)}, u32[]{:S(2)}, u32[]{:S(2)}) collective-permute-start(bf16[8,128,128]{2,1,0:T(8,128)(2,1)S(1)} %get-tuple-element.44), channel_id=1, source_target_pairs={{0,64},{8,72},{16,80},{24,88},{32,96},{40,104},{48,112},{56,120},{... | collective-permute-start | bytes 786440 | tf_op jit(solution)/shard_map/ppermute | solution.py:291
  142.1 2.8 %collective-permute-done.36 = bf16[8,128,128]{2,1,0:T(8,128)(2,1)S(1)} collective-permute-done((bf16[8,128,128]{2,1,0:T(8,128)(2,1)S(1)}, bf16[8,128,128]{2,1,0:T(8,128)(2,1)S(1)}, u32[]{:S(2)}, u32[]{:S(2)}) %collective-permute-start.36) | collective-permute-done | bytes 262176 | tf_op jit(solution)/shard_map/ppermute | solution.py:287
  144.9 2.3 %collective-permute-start.37 = (bf16[8,128,128]{2,1,0:T(8,128)(2,1)S(1)}, bf16[8,128,128]{2,1,0:T(8,128)(2,1)S(1)}, u32[]{:S(2)}, u32[]{:S(2)}) collective-permute-start(bf16[8,128,128]{2,1,0:T(8,128)(2,1)S(1)} %fusion.7), channel_id=1, source_target_pairs={{0,128},{128,0},{1,129},{129,1},{2,130},{130,2},{3,131},{131,3},{4... | collective-permute-start | bytes 786440 | tf_op jit(solution)/shard_map/ppermute | solution.py:295
  147.2 6.5 %collective-permute-done.29 = bf16[8,128,128]{2,1,0:T(8,128)(2,1)S(1)} collective-permute-done((bf16[8,128,128]{2,1,0:T(8,128)(2,1)S(1)}, bf16[8,128,128]{2,1,0:T(8,128)(2,1)S(1)}, u32[]{:S(2)}, u32[]{:S(2)}) %collective-permute-start.29) | collective-permute-done | bytes 262176 | tf_op jit(solution)/shard_map/ppermute | solution.py:291
  153.9 2.7 %collective-permute-start.30 = (bf16[8,128,128]{2,1,0:T(8,128)(2,1)S(1)}, bf16[8,128,128]{2,1,0:T(8,128)(2,1)S(1)}, u32[]{:S(2)}, u32[]{:S(2)}) collective-permute-start(bf16[8,128,128]{2,1,0:T(8,128)(2,1)S(1)} %fusion.9), channel_id=1, source_target_pairs={{0,128},{128,0},{1,129},{129,1},{2,130},{130,2},{3,131},{131,3},{4... | collective-permute-start | bytes 786440 | tf_op jit(solution)/shard_map/ppermute | solution.py:295
  159.3 3.4 %collective-permute-done.30 = bf16[8,128,128]{2,1,0:T(8,128)(2,1)S(1)} collective-permute-done((bf16[8,128,128]{2,1,0:T(8,128)(2,1)S(1)}, bf16[8,128,128]{2,1,0:T(8,128)(2,1)S(1)}, u32[]{:S(2)}, u32[]{:S(2)}) %collective-permute-start.30) | collective-permute-done | bytes 262176 | tf_op jit(solution)/shard_map/ppermute | solution.py:295
  (127 shorter events, 30.4 us)
Async XLA Ops:
  7.2 74.1 %all-gather.3.cloned.1.call-start = ((), (), s32[]{:S(2)}) async-start(), calls=%async_computation.2 | async-start | bytes 2359296 | tf_op jit(solution)/shard_map/all_gather | solution.py:359
  7.9 149.5 %reduce-scatter.2.cloned.1.call-start = ((), (), s32[]{:S(2)}) async-start(), calls=%async_computation.1 | async-start | bytes 4718592 | tf_op jit(solution)/shard_map/reduce_scatter | solution.py:347
  10.2 17.1 %collective-permute-start = (bf16[128,1024]{1,0:T(8,128)(2,1)}, bf16[128,1024]{1,0:T(8,128)(2,1)S(1)}, u32[]{:S(2)}, u32[]{:S(2)}) collective-permute-start(bf16[128,1024]{1,0:T(8,128)(2,1)} %refs_0_.1), channel_id=1, source_target_pairs={{0,1},{1,2},{2,3},{3,4},{4,5},{5,6},{6,7},{7,0},{8,9},{9,10},{10,1... | collective-permute-start | bytes 786440 | tf_op jit(solution)/shard_map/ppermute | solution.py:299
  10.4 18.1 %collective-permute-start.9 = (bf16[8,128,128]{2,1,0:T(8,128)(2,1)}, bf16[8,128,128]{2,1,0:T(8,128)(2,1)S(1)}, u32[]{:S(2)}, u32[]{:S(2)}) collective-permute-start(bf16[8,128,128]{2,1,0:T(8,128)(2,1)} %param.11), channel_id=1, source_target_pairs={{0,32},{8,40},{16,48},{24,56},{32,64},{40,72},{48,80},{56,88},{64,... | collective-permute-start | bytes 786440 | tf_op jit(solution)/shard_map/ppermute | solution.py:291
  11.9 16.6 %collective-permute-start.12 = (bf16[8,128,128]{2,1,0:T(8,128)(2,1)}, bf16[8,128,128]{2,1,0:T(8,128)(2,1)S(1)}, u32[]{:S(2)}, u32[]{:S(2)}) collective-permute-start(bf16[8,128,128]{2,1,0:T(8,128)(2,1)} %param.11), channel_id=1, source_target_pairs={{0,64},{8,72},{16,80},{24,88},{32,96},{40,104},{48,112},{56,120},{... | collective-permute-start | bytes 786440 | tf_op jit(solution)/shard_map/ppermute | solution.py:291
  14.6 13.9 %collective-permute-start.11 = (bf16[8,128,128]{2,1,0:T(8,128)(2,1)}, bf16[8,128,128]{2,1,0:T(8,128)(2,1)S(1)}, u32[]{:S(2)}, u32[]{:S(2)}) collective-permute-start(bf16[8,128,128]{2,1,0:T(8,128)(2,1)} %param.11), channel_id=1, source_target_pairs={{0,96},{8,104},{16,112},{24,120},{32,0},{40,8},{48,16},{56,24},{64... | collective-permute-start | bytes 786440 | tf_op jit(solution)/shard_map/ppermute | solution.py:291
  16.3 15.2 %collective-permute-start.1 = (bf16[128,1024]{1,0:T(8,128)(2,1)}, bf16[128,1024]{1,0:T(8,128)(2,1)}, u32[]{:S(2)}, u32[]{:S(2)}) collective-permute-start(bf16[128,1024]{1,0:T(8,128)(2,1)} %refs_0_.1), channel_id=1, source_target_pairs={{0,7},{1,0},{2,1},{3,2},{4,3},{5,4},{6,5},{7,6},{8,15},{9,8},{10,9... | collective-permute-start | bytes 786440 | tf_op jit(solution)/shard_map/ppermute | solution.py:303
  27.4 14.0 %collective-permute-start.2 = (bf16[128,1024]{1,0:T(8,128)(2,1)S(1)}, bf16[128,1024]{1,0:T(8,128)(2,1)S(1)}, u32[]{:S(2)}, u32[]{:S(2)}) collective-permute-start(bf16[128,1024]{1,0:T(8,128)(2,1)S(1)} %collective-permute-done.refs_1_), channel_id=1, source_target_pairs={{0,1},{1,2},{2,3},{3,4},{4,5},{5,6},{6,7},{7,0},{8,9},{9,10},{10,1... | collective-permute-start | bytes 786440 | tf_op jit(solution)/shard_map/ppermute | solution.py:299
  28.6 30.1 %collective-permute-start.13 = (bf16[2,8,128,128]{3,2,1,0:T(8,128)(2,1)S(1)}, bf16[2,8,128,128]{3,2,1,0:T(8,128)(2,1)S(1)}, u32[]{:S(2)}, u32[]{:S(2)}) collective-permute-start(bf16[2,8,128,128]{3,2,1,0:T(8,128)(2,1)S(1)} %pad_maximum_fusion.2.refs_18_), channel_id=1, source_target_pairs={{0,16},{8,24},{16,0},{24,8},{32,48},{40,56},{48,32},{56,40},{64,80... | collective-permute-start | bytes 1572872 | tf_op jit(solution)/shard_map/ppermute | solution.py:287
  31.5 13.3 %collective-permute-start.3 = (bf16[128,1024]{1,0:T(8,128)(2,1)}, bf16[128,1024]{1,0:T(8,128)(2,1)S(1)}, u32[]{:S(2)}, u32[]{:S(2)}) collective-permute-start(bf16[128,1024]{1,0:T(8,128)(2,1)} %collective-permute-done.1.refs_2_), channel_id=1, source_target_pairs={{0,7},{1,0},{2,1},{3,2},{4,3},{5,4},{6,5},{7,6},{8,15},{9,8},{10,9... | collective-permute-start | bytes 786440 | tf_op jit(solution)/shard_map/ppermute | solution.py:303
  35.2 24.0 %collective-permute-start.10 = (bf16[2,8,128,128]{3,2,1,0:T(8,128)(2,1)S(1)}, bf16[2,8,128,128]{3,2,1,0:T(8,128)(2,1)S(1)}, u32[]{:S(2)}, u32[]{:S(2)}) collective-permute-start(bf16[2,8,128,128]{3,2,1,0:T(8,128)(2,1)S(1)} %pad_maximum_fusion.1.refs_17_), channel_id=1, source_target_pairs={{0,16},{8,24},{16,0},{24,8},{32,48},{40,56},{48,32},{56,40},{64,80... | collective-permute-start | bytes 1572872 | tf_op jit(solution)/shard_map/ppermute | solution.py:287
  35.4 24.0 %collective-permute-start.8 = (bf16[2,8,128,128]{3,2,1,0:T(8,128)(2,1)S(1)}, bf16[2,8,128,128]{3,2,1,0:T(8,128)(2,1)S(1)}, u32[]{:S(2)}, u32[]{:S(2)}) collective-permute-start(bf16[2,8,128,128]{3,2,1,0:T(8,128)(2,1)S(1)} %pad_maximum_fusion.refs_8_), channel_id=1, source_target_pairs={{0,96},{8,104},{16,112},{24,120},{32,0},{40,8},{48,16},{56,24},{64... | collective-permute-start | bytes 1572872 | tf_op jit(solution)/shard_map/ppermute | solution.py:291
  41.4 20.6 %collective-permute-start.7 = (bf16[2,8,128,128]{3,2,1,0:T(8,128)(2,1)S(1)}, bf16[2,8,128,128]{3,2,1,0:T(8,128)(2,1)S(1)}, u32[]{:S(2)}, u32[]{:S(2)}) collective-permute-start(bf16[2,8,128,128]{3,2,1,0:T(8,128)(2,1)S(1)} %pad_maximum_fusion.refs_8_), channel_id=1, source_target_pairs={{0,32},{8,40},{16,48},{24,56},{32,64},{40,72},{48,80},{56,88},{64,... | collective-permute-start | bytes 1572872 | tf_op jit(solution)/shard_map/ppermute | solution.py:291
  44.8 13.9 %collective-permute-start.4 = (bf16[128,1024]{1,0:T(8,128)(2,1)S(1)}, bf16[128,1024]{1,0:T(8,128)(2,1)S(1)}, u32[]{:S(2)}, u32[]{:S(2)}) collective-permute-start(bf16[128,1024]{1,0:T(8,128)(2,1)S(1)} %collective-permute-done.2.refs_3_), channel_id=1, source_target_pairs={{0,1},{1,2},{2,3},{3,4},{4,5},{5,6},{6,7},{7,0},{8,9},{9,10},{10,1... | collective-permute-start | bytes 786440 | tf_op jit(solution)/shard_map/ppermute | solution.py:299
  58.7 12.4 %collective-permute-start.21 = (bf16[2,8,128,128]{3,2,1,0:T(8,128)(2,1)S(1)}, bf16[2,8,128,128]{3,2,1,0:T(8,128)(2,1)S(1)}, u32[]{:S(2)}, u32[]{:S(2)}) collective-permute-start(bf16[2,8,128,128]{3,2,1,0:T(8,128)(2,1)S(1)} %pad_maximum_fusion.2.refs_18_), channel_id=1, source_target_pairs={{0,8},{8,0},{16,24},{24,16},{32,40},{40,32},{48,56},{56,48},{64,72... | collective-permute-start | bytes 1572872 | tf_op jit(solution)/shard_map/ppermute | solution.py:283
  58.7 12.3 %collective-permute-start.20 = (bf16[2,8,128,128]{3,2,1,0:T(8,128)(2,1)S(1)}, bf16[2,8,128,128]{3,2,1,0:T(8,128)(2,1)S(1)}, u32[]{:S(2)}, u32[]{:S(2)}) collective-permute-start(bf16[2,8,128,128]{3,2,1,0:T(8,128)(2,1)S(1)} %pad_maximum_fusion.1.refs_17_), channel_id=1, source_target_pairs={{0,8},{8,0},{16,24},{24,16},{32,40},{40,32},{48,56},{56,48},{64,72... | collective-permute-start | bytes 1572872 | tf_op jit(solution)/shard_map/ppermute | solution.py:283
  59.2 12.4 %collective-permute-start.16 = (bf16[2,8,128,128]{3,2,1,0:T(8,128)(2,1)S(1)}, bf16[2,8,128,128]{3,2,1,0:T(8,128)(2,1)S(1)}, u32[]{:S(2)}, u32[]{:S(2)}) collective-permute-start(bf16[2,8,128,128]{3,2,1,0:T(8,128)(2,1)S(1)} %pad_maximum_fusion.refs_8_), channel_id=1, source_target_pairs={{0,8},{8,0},{16,24},{24,16},{32,40},{40,32},{48,56},{56,48},{64,72... | collective-permute-start | bytes 1572872 | tf_op jit(solution)/shard_map/ppermute | solution.py:283
  59.3 15.8 %collective-permute-start.15 = (bf16[2,8,128,128]{3,2,1,0:T(8,128)(2,1)S(1)}, bf16[2,8,128,128]{3,2,1,0:T(8,128)(2,1)S(1)}, u32[]{:S(2)}, u32[]{:S(2)}) collective-permute-start(bf16[2,8,128,128]{3,2,1,0:T(8,128)(2,1)S(1)} %pad_maximum_fusion.refs_8_), channel_id=1, source_target_pairs={{0,64},{8,72},{16,80},{24,88},{32,96},{40,104},{48,112},{56,120},{... | collective-permute-start | bytes 1572872 | tf_op jit(solution)/shard_map/ppermute | solution.py:291
  105.0 25.2 %collective-permute-start.26 = (bf16[4,8,128,128]{3,2,1,0:T(8,128)(2,1)S(1)}, bf16[4,8,128,128]{3,2,1,0:T(8,128)(2,1)S(1)}, u32[]{:S(2)}, u32[]{:S(2)}) collective-permute-start(bf16[4,8,128,128]{3,2,1,0:T(8,128)(2,1)S(1)} %fusion.1), channel_id=1, source_target_pairs={{0,16},{8,24},{16,0},{24,8},{32,48},{40,56},{48,32},{56,40},{64,80... | collective-permute-start | bytes 3145736 | tf_op jit(solution)/shard_map/ppermute | solution.py:287
  109.2 26.9 %collective-permute-start.33 = (bf16[2,8,128,128]{3,2,1,0:T(8,128)(2,1)S(1)}, bf16[2,8,128,128]{3,2,1,0:T(8,128)(2,1)S(1)}, u32[]{:S(2)}, u32[]{:S(2)}) collective-permute-start(bf16[2,8,128,128]{3,2,1,0:T(8,128)(2,1)S(1)} %get-tuple-element.40), channel_id=1, source_target_pairs={{0,32},{8,40},{16,48},{24,56},{32,64},{40,72},{48,80},{56,88},{64,... | collective-permute-start | bytes 1572872 | tf_op jit(solution)/shard_map/ppermute | solution.py:291
  110.2 25.9 %collective-permute-start.35 = (bf16[2,8,128,128]{3,2,1,0:T(8,128)(2,1)S(1)}, bf16[2,8,128,128]{3,2,1,0:T(8,128)(2,1)S(1)}, u32[]{:S(2)}, u32[]{:S(2)}) collective-permute-start(bf16[2,8,128,128]{3,2,1,0:T(8,128)(2,1)S(1)} %get-tuple-element.41), channel_id=1, source_target_pairs={{0,64},{8,72},{16,80},{24,88},{32,96},{40,104},{48,112},{56,120},{... | collective-permute-start | bytes 1572872 | tf_op jit(solution)/shard_map/ppermute | solution.py:291
  112.3 24.5 %collective-permute-start.34 = (bf16[2,8,128,128]{3,2,1,0:T(8,128)(2,1)S(1)}, bf16[2,8,128,128]{3,2,1,0:T(8,128)(2,1)S(1)}, u32[]{:S(2)}, u32[]{:S(2)}) collective-permute-start(bf16[2,8,128,128]{3,2,1,0:T(8,128)(2,1)S(1)} %get-tuple-element.42), channel_id=1, source_target_pairs={{0,96},{8,104},{16,112},{24,120},{32,0},{40,8},{48,16},{56,24},{64... | collective-permute-start | bytes 1572872 | tf_op jit(solution)/shard_map/ppermute | solution.py:291
  138.5 15.2 %collective-permute-start.29 = (bf16[8,128,128]{2,1,0:T(8,128)(2,1)S(1)}, bf16[8,128,128]{2,1,0:T(8,128)(2,1)S(1)}, u32[]{:S(2)}, u32[]{:S(2)}) collective-permute-start(bf16[8,128,128]{2,1,0:T(8,128)(2,1)S(1)} %get-tuple-element.44), channel_id=1, source_target_pairs={{0,64},{8,72},{16,80},{24,88},{32,96},{40,104},{48,112},{56,120},{... | collective-permute-start | bytes 786440 | tf_op jit(solution)/shard_map/ppermute | solution.py:291
  142.1 11.6 %collective-permute-start.28 = (bf16[8,128,128]{2,1,0:T(8,128)(2,1)S(1)}, bf16[8,128,128]{2,1,0:T(8,128)(2,1)S(1)}, u32[]{:S(2)}, u32[]{:S(2)}) collective-permute-start(bf16[8,128,128]{2,1,0:T(8,128)(2,1)S(1)} %get-tuple-element.45), channel_id=1, source_target_pairs={{0,96},{8,104},{16,112},{24,120},{32,0},{40,8},{48,16},{56,24},{64... | collective-permute-start | bytes 786440 | tf_op jit(solution)/shard_map/ppermute | solution.py:291
  (42 other events, 570.4 us)
Sparse Core Ops, SparseCore 0:
  9.8 50.0 all-gather.2
  101.2 52.7 reduce-scatter.1

commit v6 on v4

--- a/solution.py
+++ b/solution.py
@@ -356,7 +356,7 @@
     total = (add(up_keep[0], u0[0]) + u_y.astype(F32)).astype(BF)
     u_x1, u_x3, u_x2 = x_shift(total[1], 1), x_shift(total[3], 3), x_shift(total[2], 2)
     own = add(down_keep[3], d30[1]) + add(d_x1, d_x3) + d_x2.astype(F32)
-    d_y = y_swap(after(own[1].astype(BF), total))
+    d_y = y_swap(after(own[1].astype(BF), total, u_x1, u_x3))
     down_mine = (own[0] + d_y.astype(F32)).astype(BF)
     d_dp = dp_swap(down_mine)
     up_mine = (total[0].astype(F32) + add(u_x1, u_x3) + u_x2.astype(F32)).astype(BF)

time: 159 us -> 160 us (level); the launches traced: 157 us -> 160 us
  waiting for transfers between devices: 74.3 us -> 77.4 us
    ppermute x12, waiting for transfers between devices: 21.6 us -> 16.9 us  [x_shift(): return lax.ppermute(a, 'fsdp', [(i, (i + 4 * d) % 16) for i in range(16)])]
    ppermute x2, waiting for transfers between devices: 3.56 us -> 7.76 us  [dp_swap(): return lax.ppermute(a, 'dp', [(0, 1), (1, 0)])]
    ppermute x5, waiting for transfers between devices: 34.8 us -> 38.6 us  [y_swap(): return lax.ppermute(a, 'fsdp', [(i, i ^ 2) for i in range(16)])]
  transfers between devices with their start and end apart: 33 -> 33, of which waited for: 15 -> 16; matrix products, arithmetic and copies ran while one was open for 4% -> 4% of each run, Pallas kernels for 3% -> 3%
where the time goes in v6:
time: 160 us
  waiting for transfers between devices  77.4 us (48%)
  starting transfers between devices  31.5 us (20%)
  Pallas kernels  24.3 us (15%)
  between operations  14.4 us (9%)
  other arithmetic  7.61 us (5%)
  local copies, waits for them, and re-layouts  4.71 us (3%)
    ppermute x5, waiting for transfers between devices, y_swap(): return lax.ppermute(a, 'fsdp', [(i, i ^ 2) for i in range(16)])  38.6 us
    ppermute x12, starting transfers between devices, x_shift(): return lax.ppermute(a, 'fsdp', [(i, (i + 4 * d) % 16) for i in range(16)])  19.9 us
    pallas_call x1, Pallas kernels, call(): pl.pallas_call(kernel, out_shape=tuple(out_shape), in_specs=[SMEM_SPEC] *...  19.7 us
    ppermute x12, waiting for transfers between devices, x_shift(): return lax.ppermute(a, 'fsdp', [(i, (i + 4 * d) % 16) for i in range(16)])  16.9 us
    all_gather x1, waiting for transfers between devices, body(): lax.all_gather(jnp.stack([activations, cotangent]), 'tensor', axis=0, til...  9.26 us
    ppermute x2, waiting for transfers between devices, dp_swap(): return lax.ppermute(a, 'dp', [(0, 1), (1, 0)])  7.76 us
    ppermute x5, starting transfers between devices, y_swap(): return lax.ppermute(a, 'fsdp', [(i, i ^ 2) for i in range(16)])  5.5 us
    ppermute x12, waiting for transfers between devices, core_swap(): return lax.ppermute(a, 'fsdp', [(i, i ^ 1) for i in range(16)])  4.94 us
  transfers between devices with their start and end apart: 33, of which 16 were waited for; matrix products, arithmetic and copies ran while one was open for 4% of the time, Pallas kernels for 3%

profile of v6, /device:TPU:8, one launch (start us, length us, event | category | flops | bytes accessed | tf_op | source)
XLA Modules:
  0.0 159.8 jit_solution(12342444060386288320)
XLA Ops:
  7.2 1.9 %pad_maximum_fusion = bf16[2,128,1024]{2,1,0:T(8,128)(2,1)} fusion(bf16[1,128,1024]{2,1,0:T(8,128)(2,1)} %bitcast.58, bf16[1,128,1024]{2,1,0:T(8,128)(2,1)} %bitcast.59), kind=kLoop, calls=%fused_computation.16 | loop fusion | flops 262144 | bytes 1048576 | tf_op jit(solution)/shard_map/stack | solution.py:338
  9.2 2.3 %collective-permute-start = (bf16[8,128,128]{2,1,0:T(8,128)(2,1)}, bf16[8,128,128]{2,1,0:T(8,128)(2,1)S(1)}, u32[]{:S(2)}, u32[]{:S(2)}) collective-permute-start(bf16[8,128,128]{2,1,0:T(8,128)(2,1)} %param.10), channel_id=1, source_target_pairs={{0,16},{8,24},{16,0},{24,8},{32,48},{40,56},{48,32},{56,40},{64,80... | collective-permute-start | bytes 786440 | tf_op jit(solution)/shard_map/ppermute | solution.py:287
  15.4 4.6 %plan.1 = (s32[128]{0:T(128)}, s32[128]{0:T(128)}) custom-call(s32[128]{0:T(128)} %bitcast.68, s32[128]{0:T(128)} %bitcast.69), custom_call_target="tpu_custom_call" | custom-call | tf_op jit(solution)/shard_map/plan/pallas_call | solution.py:55
  22.1 2.9 %collective-permute-done.9 = bf16[8,128,128]{2,1,0:T(8,128)(2,1)S(1)} collective-permute-done((bf16[8,128,128]{2,1,0:T(8,128)(2,1)}, bf16[8,128,128]{2,1,0:T(8,128)(2,1)S(1)}, u32[]{:S(2)}, u32[]{:S(2)}) %collective-permute-start.9) | collective-permute-done | bytes 262176 | tf_op jit(solution)/shard_map/ppermute | solution.py:291
  27.6 2.2 %collective-permute-start.3 = (bf16[2,8,128,128]{3,2,1,0:T(8,128)(2,1)S(1)}, bf16[2,8,128,128]{3,2,1,0:T(8,128)(2,1)S(1)}, u32[]{:S(2)}, u32[]{:S(2)}) collective-permute-start(bf16[2,8,128,128]{3,2,1,0:T(8,128)(2,1)S(1)} %pad_maximum_fusion.1.refs_1_), channel_id=1, source_target_pairs={{0,64},{8,72},{16,80},{24,88},{32,96},{40,104},{48,112},{56,120},{... | collective-permute-start | bytes 1572872 | tf_op jit(solution)/shard_map/ppermute | solution.py:291
  29.9 10.1 %collective-permute-done.12.refs_13_ = bf16[2,8,128,128]{3,2,1,0:T(8,128)(2,1)S(1)} collective-permute-done((bf16[2,8,128,128]{3,2,1,0:T(8,128)(2,1)S(1)}, bf16[2,8,128,128]{3,2,1,0:T(8,128)(2,1)S(1)}, u32[]{:S(2)}, u32[]{:S(2)}) %collective-permute-start.12) | collective-permute-done | bytes 524320 | tf_op jit(solution)/shard_map/ppermute | solution.py:287
  39.9 2.6 %collective-permute-start.2 = (bf16[2,8,128,128]{3,2,1,0:T(8,128)(2,1)S(1)}, bf16[2,8,128,128]{3,2,1,0:T(8,128)(2,1)S(1)}, u32[]{:S(2)}, u32[]{:S(2)}) collective-permute-start(bf16[2,8,128,128]{3,2,1,0:T(8,128)(2,1)S(1)} %pad_maximum_fusion.1.refs_1_), channel_id=1, source_target_pairs={{0,96},{8,104},{16,112},{24,120},{32,0},{40,8},{48,16},{56,24},{64... | collective-permute-start | bytes 1572872 | tf_op jit(solution)/shard_map/ppermute | solution.py:291
  42.6 8.1 %collective-permute-done.11.refs_12_ = bf16[2,8,128,128]{3,2,1,0:T(8,128)(2,1)S(1)} collective-permute-done((bf16[2,8,128,128]{3,2,1,0:T(8,128)(2,1)S(1)}, bf16[2,8,128,128]{3,2,1,0:T(8,128)(2,1)S(1)}, u32[]{:S(2)}, u32[]{:S(2)}) %collective-permute-start.11) | collective-permute-done | bytes 524320 | tf_op jit(solution)/shard_map/ppermute | solution.py:287
  51.3 3.3 %collective-permute-done.2.refs_3_ = bf16[2,8,128,128]{3,2,1,0:T(8,128)(2,1)S(1)} collective-permute-done((bf16[2,8,128,128]{3,2,1,0:T(8,128)(2,1)S(1)}, bf16[2,8,128,128]{3,2,1,0:T(8,128)(2,1)S(1)}, u32[]{:S(2)}, u32[]{:S(2)}) %collective-permute-start.2) | collective-permute-done | bytes 524320 | tf_op jit(solution)/shard_map/ppermute | solution.py:291
  54.6 2.0 %collective-permute-done.1.refs_2_ = bf16[2,8,128,128]{3,2,1,0:T(8,128)(2,1)S(1)} collective-permute-done((bf16[2,8,128,128]{3,2,1,0:T(8,128)(2,1)S(1)}, bf16[2,8,128,128]{3,2,1,0:T(8,128)(2,1)S(1)}, u32[]{:S(2)}, u32[]{:S(2)}) %collective-permute-start.1) | collective-permute-done | bytes 524320 | tf_op jit(solution)/shard_map/ppermute | solution.py:291
  58.8 9.3 %all-gather.3.cloned.1.call-done = bf16[16,128,1024]{2,1,0:T(8,128)(2,1)} async-done(((bf16[2,128,1024]{2,1,0:T(8,128)(2,1)}), bf16[16,128,1024]{2,1,0:T(8,128)(2,1)}) %all-gather.3.cloned.1.call-update) | async-done | bytes 4194320 | tf_op jit(solution)/shard_map/all_gather | solution.py:338
  68.1 19.7 %tile_pass.1 = (bf16[1,4,8,128,128]{4,3,2,1,0:T(8,128)(2,1)}, bf16[1,4,8,128,128]{4,3,2,1,0:T(8,128)(2,1)}, bf16[2,4,8,128,128]{4,3,2,1,0:T(8,128)(2,1)}, bf16[2...) custom-call(s32[128]{0:T(128)} %get-tuple-element.21.up_order, ...), custom_call_target="tpu_custom_call" | custom-call | flops 10000000 | bytes 100000 | tf_op jit(solution)/shard_map/tile_pass/pallas_call | solution.py:102
  89.1 1.8 %collective-permute-done.17 = bf16[1,4,8,128,128]{4,3,2,1,0:T(8,128)(2,1)S(1)} collective-permute-done((bf16[1,4,8,128,128]{4,3,2,1,0:T(8,128)(2,1)}, bf16[1,4,8,128,128]{4,3,2,1,0:T(8,128)(2,1)S(1)}, u32[]{:S(2)}, u32[]{:S(2)}) %collective-permute-start.17) | collective-permute-done | bytes 1048608 | tf_op jit(solution)/shard_map/ppermute | solution.py:283
  92.0 1.8 %collective-permute-done.24 = bf16[2,2,8,128,128]{4,3,2,1,0:T(8,128)(2,1)S(1)} collective-permute-done((bf16[2,2,8,128,128]{4,3,2,1,0:T(8,128)(2,1)}, bf16[2,2,8,128,128]{4,3,2,1,0:T(8,128)(2,1)S(1)}, u32[]{:S(2)}, u32[]{:S(2)}) %collective-permute-start.24) | collective-permute-done | bytes 1048608 | tf_op jit(solution)/shard_map/ppermute | solution.py:283
  97.5 2.7 %collective-permute-start.28 = (bf16[2,8,128,128]{3,2,1,0:T(8,128)(2,1)S(1)}, bf16[2,8,128,128]{3,2,1,0:T(8,128)(2,1)S(1)}, u32[]{:S(2)}, u32[]{:S(2)}) collective-permute-start(bf16[2,8,128,128]{3,2,1,0:T(8,128)(2,1)S(1)} %get-tuple-element.39), channel_id=1, source_target_pairs={{0,64},{8,72},{16,80},{24,88},{32,96},{40,104},{48,112},{56,120},{... | collective-permute-start | bytes 1572872 | tf_op jit(solution)/shard_map/ppermute | solution.py:291
  101.6 15.3 %collective-permute-done.19 = bf16[4,8,128,128]{3,2,1,0:T(8,128)(2,1)S(1)} collective-permute-done((bf16[4,8,128,128]{3,2,1,0:T(8,128)(2,1)S(1)}, bf16[4,8,128,128]{3,2,1,0:T(8,128)(2,1)S(1)}, u32[]{:S(2)}, u32[]{:S(2)}) %collective-permute-start.19) | collective-permute-done | bytes 1048608 | tf_op jit(solution)/shard_map/ppermute | solution.py:287
  120.8 3.3 %collective-permute-done.28 = bf16[2,8,128,128]{3,2,1,0:T(8,128)(2,1)S(1)} collective-permute-done((bf16[2,8,128,128]{3,2,1,0:T(8,128)(2,1)S(1)}, bf16[2,8,128,128]{3,2,1,0:T(8,128)(2,1)S(1)}, u32[]{:S(2)}, u32[]{:S(2)}) %collective-permute-start.28) | collective-permute-done | bytes 524320 | tf_op jit(solution)/shard_map/ppermute | solution.py:291
  124.6 4.3 %collective-permute-done.20 = bf16[8,128,128]{2,1,0:T(8,128)(2,1)S(1)} collective-permute-done((bf16[8,128,128]{2,1,0:T(8,128)(2,1)S(1)}, bf16[8,128,128]{2,1,0:T(8,128)(2,1)S(1)}, u32[]{:S(2)}, u32[]{:S(2)}) %collective-permute-start.20) | collective-permute-done | bytes 262176 | tf_op jit(solution)/shard_map/ppermute | solution.py:291
  129.5 2.7 %collective-permute-start.22 = (bf16[8,128,128]{2,1,0:T(8,128)(2,1)S(1)}, bf16[8,128,128]{2,1,0:T(8,128)(2,1)S(1)}, u32[]{:S(2)}, u32[]{:S(2)}) collective-permute-start(bf16[8,128,128]{2,1,0:T(8,128)(2,1)S(1)} %get-tuple-element.42), channel_id=1, source_target_pairs={{0,64},{8,72},{16,80},{24,88},{32,96},{40,104},{48,112},{56,120},{... | collective-permute-start | bytes 786440 | tf_op jit(solution)/shard_map/ppermute | solution.py:291
  132.2 5.1 %collective-permute-done.29 = bf16[8,128,128]{2,1,0:T(8,128)(2,1)S(1)} collective-permute-done((bf16[8,128,128]{2,1,0:T(8,128)(2,1)S(1)}, bf16[8,128,128]{2,1,0:T(8,128)(2,1)S(1)}, u32[]{:S(2)}, u32[]{:S(2)}) %collective-permute-start.29) | collective-permute-done | bytes 262176 | tf_op jit(solution)/shard_map/ppermute | solution.py:287
  137.3 2.2 %collective-permute-start.30 = (bf16[8,128,128]{2,1,0:T(8,128)(2,1)S(1)}, bf16[8,128,128]{2,1,0:T(8,128)(2,1)S(1)}, u32[]{:S(2)}, u32[]{:S(2)}) collective-permute-start(bf16[8,128,128]{2,1,0:T(8,128)(2,1)S(1)} %fusion.7), channel_id=1, source_target_pairs={{0,128},{128,0},{1,129},{129,1},{2,130},{130,2},{3,131},{131,3},{4... | collective-permute-start | bytes 786440 | tf_op jit(solution)/shard_map/ppermute | solution.py:295
  139.7 2.0 %collective-permute-start.23 = (bf16[8,128,128]{2,1,0:T(8,128)(2,1)S(1)}, bf16[8,128,128]{2,1,0:T(8,128)(2,1)S(1)}, u32[]{:S(2)}, u32[]{:S(2)}) collective-permute-start(bf16[8,128,128]{2,1,0:T(8,128)(2,1)S(1)} %fusion.9), channel_id=1, source_target_pairs={{0,128},{128,0},{1,129},{129,1},{2,130},{130,2},{3,131},{131,3},{4... | collective-permute-start | bytes 786440 | tf_op jit(solution)/shard_map/ppermute | solution.py:295
  141.7 6.5 %collective-permute-done.30 = bf16[8,128,128]{2,1,0:T(8,128)(2,1)S(1)} collective-permute-done((bf16[8,128,128]{2,1,0:T(8,128)(2,1)S(1)}, bf16[8,128,128]{2,1,0:T(8,128)(2,1)S(1)}, u32[]{:S(2)}, u32[]{:S(2)}) %collective-permute-start.30) | collective-permute-done | bytes 262176 | tf_op jit(solution)/shard_map/ppermute | solution.py:295
  149.0 1.9 %slice_bitcast_fusion.5 = (bf16[128,1024]{1,0:T(8,128)(2,1)}, bf16[128,1024]{1,0:T(8,128)(2,1)}) fusion(bf16[1,2,128,1024]{3,2,1,0:T(8,128)(2,1)} %reduce-scatter.2.cloned.1.call-done), kind=kLoop, calls=%fused_computation.30 | loop fusion | bytes 1048576 | tf_op jit(solution)/shard_map/unstack | solution.py:347
  (102 shorter events, 27.0 us)
Async XLA Ops:
  7.2 60.9 %all-gather.3.cloned.1.call-start = ((), (), s32[]{:S(2)}) async-start(), calls=%async_computation.2 | async-start | bytes 4718592 | tf_op jit(solution)/shard_map/all_gather | solution.py:338
  9.2 139.9 %reduce-scatter.2.cloned.1.call-start = ((), (), s32[]{:S(2)}) async-start(), calls=%async_computation.1 | async-start | bytes 4718592 | tf_op jit(solution)/shard_map/reduce_scatter | solution.py:326
  9.2 10.8 %collective-permute-start = (bf16[8,128,128]{2,1,0:T(8,128)(2,1)}, bf16[8,128,128]{2,1,0:T(8,128)(2,1)S(1)}, u32[]{:S(2)}, u32[]{:S(2)}) collective-permute-start(bf16[8,128,128]{2,1,0:T(8,128)(2,1)} %param.10), channel_id=1, source_target_pairs={{0,16},{8,24},{16,0},{24,8},{32,48},{40,56},{48,32},{56,40},{64,80... | collective-permute-start | bytes 786440 | tf_op jit(solution)/shard_map/ppermute | solution.py:287
  11.5 10.6 %collective-permute-start.10 = (bf16[8,128,128]{2,1,0:T(8,128)(2,1)}, bf16[8,128,128]{2,1,0:T(8,128)(2,1)S(1)}, u32[]{:S(2)}, u32[]{:S(2)}) collective-permute-start(bf16[8,128,128]{2,1,0:T(8,128)(2,1)} %param.11), channel_id=1, source_target_pairs={{0,64},{8,72},{16,80},{24,88},{32,96},{40,104},{48,112},{56,120},{... | collective-permute-start | bytes 786440 | tf_op jit(solution)/shard_map/ppermute | solution.py:291
  12.8 12.2 %collective-permute-start.9 = (bf16[8,128,128]{2,1,0:T(8,128)(2,1)}, bf16[8,128,128]{2,1,0:T(8,128)(2,1)S(1)}, u32[]{:S(2)}, u32[]{:S(2)}) collective-permute-start(bf16[8,128,128]{2,1,0:T(8,128)(2,1)} %param.11), channel_id=1, source_target_pairs={{0,96},{8,104},{16,112},{24,120},{32,0},{40,8},{48,16},{56,24},{64... | collective-permute-start | bytes 786440 | tf_op jit(solution)/shard_map/ppermute | solution.py:291
  13.9 12.9 %collective-permute-start.8 = (bf16[8,128,128]{2,1,0:T(8,128)(2,1)}, bf16[8,128,128]{2,1,0:T(8,128)(2,1)S(1)}, u32[]{:S(2)}, u32[]{:S(2)}) collective-permute-start(bf16[8,128,128]{2,1,0:T(8,128)(2,1)} %param.11), channel_id=1, source_target_pairs={{0,32},{8,40},{16,48},{24,56},{32,64},{40,72},{48,80},{56,88},{64,... | collective-permute-start | bytes 786440 | tf_op jit(solution)/shard_map/ppermute | solution.py:291
  25.1 14.8 %collective-permute-start.12 = (bf16[2,8,128,128]{3,2,1,0:T(8,128)(2,1)S(1)}, bf16[2,8,128,128]{3,2,1,0:T(8,128)(2,1)S(1)}, u32[]{:S(2)}, u32[]{:S(2)}) collective-permute-start(bf16[2,8,128,128]{3,2,1,0:T(8,128)(2,1)S(1)} %pad_maximum_fusion.3.refs_11_), channel_id=1, source_target_pairs={{0,16},{8,24},{16,0},{24,8},{32,48},{40,56},{48,32},{56,40},{64,80... | collective-permute-start | bytes 1572872 | tf_op jit(solution)/shard_map/ppermute | solution.py:287
  26.9 15.7 %collective-permute-start.13 = (bf16[2,8,128,128]{3,2,1,0:T(8,128)(2,1)S(1)}, bf16[2,8,128,128]{3,2,1,0:T(8,128)(2,1)S(1)}, u32[]{:S(2)}, u32[]{:S(2)}) collective-permute-start(bf16[2,8,128,128]{3,2,1,0:T(8,128)(2,1)S(1)} %pad_maximum_fusion.2.refs_10_), channel_id=1, source_target_pairs={{0,8},{8,0},{16,24},{24,16},{32,40},{40,32},{48,56},{56,48},{64,72... | collective-permute-start | bytes 1572872 | tf_op jit(solution)/shard_map/ppermute | solution.py:283
  27.1 23.6 %collective-permute-start.11 = (bf16[2,8,128,128]{3,2,1,0:T(8,128)(2,1)S(1)}, bf16[2,8,128,128]{3,2,1,0:T(8,128)(2,1)S(1)}, u32[]{:S(2)}, u32[]{:S(2)}) collective-permute-start(bf16[2,8,128,128]{3,2,1,0:T(8,128)(2,1)S(1)} %pad_maximum_fusion.2.refs_10_), channel_id=1, source_target_pairs={{0,16},{8,24},{16,0},{24,8},{32,48},{40,56},{48,32},{56,40},{64,80... | collective-permute-start | bytes 1572872 | tf_op jit(solution)/shard_map/ppermute | solution.py:287
  27.6 23.2 %collective-permute-start.4 = (bf16[2,8,128,128]{3,2,1,0:T(8,128)(2,1)S(1)}, bf16[2,8,128,128]{3,2,1,0:T(8,128)(2,1)S(1)}, u32[]{:S(2)}, u32[]{:S(2)}) collective-permute-start(bf16[2,8,128,128]{3,2,1,0:T(8,128)(2,1)S(1)} %pad_maximum_fusion.1.refs_1_), channel_id=1, source_target_pairs={{0,8},{8,0},{16,24},{24,16},{32,40},{40,32},{48,56},{56,48},{64,72... | collective-permute-start | bytes 1572872 | tf_op jit(solution)/shard_map/ppermute | solution.py:283
  27.6 23.6 %collective-permute-start.3 = (bf16[2,8,128,128]{3,2,1,0:T(8,128)(2,1)S(1)}, bf16[2,8,128,128]{3,2,1,0:T(8,128)(2,1)S(1)}, u32[]{:S(2)}, u32[]{:S(2)}) collective-permute-start(bf16[2,8,128,128]{3,2,1,0:T(8,128)(2,1)S(1)} %pad_maximum_fusion.1.refs_1_), channel_id=1, source_target_pairs={{0,64},{8,72},{16,80},{24,88},{32,96},{40,104},{48,112},{56,120},{... | collective-permute-start | bytes 1572872 | tf_op jit(solution)/shard_map/ppermute | solution.py:291
  39.9 14.7 %collective-permute-start.2 = (bf16[2,8,128,128]{3,2,1,0:T(8,128)(2,1)S(1)}, bf16[2,8,128,128]{3,2,1,0:T(8,128)(2,1)S(1)}, u32[]{:S(2)}, u32[]{:S(2)}) collective-permute-start(bf16[2,8,128,128]{3,2,1,0:T(8,128)(2,1)S(1)} %pad_maximum_fusion.1.refs_1_), channel_id=1, source_target_pairs={{0,96},{8,104},{16,112},{24,120},{32,0},{40,8},{48,16},{56,24},{64... | collective-permute-start | bytes 1572872 | tf_op jit(solution)/shard_map/ppermute | solution.py:291
  42.6 14.0 %collective-permute-start.1 = (bf16[2,8,128,128]{3,2,1,0:T(8,128)(2,1)S(1)}, bf16[2,8,128,128]{3,2,1,0:T(8,128)(2,1)S(1)}, u32[]{:S(2)}, u32[]{:S(2)}) collective-permute-start(bf16[2,8,128,128]{3,2,1,0:T(8,128)(2,1)S(1)} %pad_maximum_fusion.1.refs_1_), channel_id=1, source_target_pairs={{0,32},{8,40},{16,48},{24,56},{32,64},{40,72},{48,80},{56,88},{64,... | collective-permute-start | bytes 1572872 | tf_op jit(solution)/shard_map/ppermute | solution.py:291
  50.7 5.9 %collective-permute-start.15 = (bf16[2,8,128,128]{3,2,1,0:T(8,128)(2,1)S(1)}, bf16[2,8,128,128]{3,2,1,0:T(8,128)(2,1)S(1)}, u32[]{:S(2)}, u32[]{:S(2)}) collective-permute-start(bf16[2,8,128,128]{3,2,1,0:T(8,128)(2,1)S(1)} %collective-permute-done.11.refs_12_), channel_id=1, source_target_pairs={{0,8},{8,0},{16,24},{24,16},{32,40},{40,32},{48,56},{56,48},{64,72... | collective-permute-start | bytes 1572872 | tf_op jit(solution)/shard_map/ppermute | solution.py:283
  91.5 25.4 %collective-permute-start.19 = (bf16[4,8,128,128]{3,2,1,0:T(8,128)(2,1)S(1)}, bf16[4,8,128,128]{3,2,1,0:T(8,128)(2,1)S(1)}, u32[]{:S(2)}, u32[]{:S(2)}) collective-permute-start(bf16[4,8,128,128]{3,2,1,0:T(8,128)(2,1)S(1)} %fusion.1), channel_id=1, source_target_pairs={{0,16},{8,24},{16,0},{24,8},{32,48},{40,56},{48,32},{56,40},{64,80... | collective-permute-start | bytes 3145736 | tf_op jit(solution)/shard_map/ppermute | solution.py:287
  95.9 24.9 %collective-permute-start.26 = (bf16[2,8,128,128]{3,2,1,0:T(8,128)(2,1)S(1)}, bf16[2,8,128,128]{3,2,1,0:T(8,128)(2,1)S(1)}, u32[]{:S(2)}, u32[]{:S(2)}) collective-permute-start(bf16[2,8,128,128]{3,2,1,0:T(8,128)(2,1)S(1)} %get-tuple-element.38), channel_id=1, source_target_pairs={{0,32},{8,40},{16,48},{24,56},{32,64},{40,72},{48,80},{56,88},{64,... | collective-permute-start | bytes 1572872 | tf_op jit(solution)/shard_map/ppermute | solution.py:291
  97.5 26.7 %collective-permute-start.28 = (bf16[2,8,128,128]{3,2,1,0:T(8,128)(2,1)S(1)}, bf16[2,8,128,128]{3,2,1,0:T(8,128)(2,1)S(1)}, u32[]{:S(2)}, u32[]{:S(2)}) collective-permute-start(bf16[2,8,128,128]{3,2,1,0:T(8,128)(2,1)S(1)} %get-tuple-element.39), channel_id=1, source_target_pairs={{0,64},{8,72},{16,80},{24,88},{32,96},{40,104},{48,112},{56,120},{... | collective-permute-start | bytes 1572872 | tf_op jit(solution)/shard_map/ppermute | solution.py:291
  100.2 24.0 %collective-permute-start.27 = (bf16[2,8,128,128]{3,2,1,0:T(8,128)(2,1)S(1)}, bf16[2,8,128,128]{3,2,1,0:T(8,128)(2,1)S(1)}, u32[]{:S(2)}, u32[]{:S(2)}) collective-permute-start(bf16[2,8,128,128]{3,2,1,0:T(8,128)(2,1)S(1)} %get-tuple-element.40), channel_id=1, source_target_pairs={{0,96},{8,104},{16,112},{24,120},{32,0},{40,8},{48,16},{56,24},{64... | collective-permute-start | bytes 1572872 | tf_op jit(solution)/shard_map/ppermute | solution.py:291
  117.5 11.4 %collective-permute-start.20 = (bf16[8,128,128]{2,1,0:T(8,128)(2,1)S(1)}, bf16[8,128,128]{2,1,0:T(8,128)(2,1)S(1)}, u32[]{:S(2)}, u32[]{:S(2)}) collective-permute-start(bf16[8,128,128]{2,1,0:T(8,128)(2,1)S(1)} %get-tuple-element.41), channel_id=1, source_target_pairs={{0,32},{8,40},{16,48},{24,56},{32,64},{40,72},{48,80},{56,88},{64,... | collective-permute-start | bytes 786440 | tf_op jit(solution)/shard_map/ppermute | solution.py:291
  119.1 9.9 %collective-permute-start.21 = (bf16[8,128,128]{2,1,0:T(8,128)(2,1)S(1)}, bf16[8,128,128]{2,1,0:T(8,128)(2,1)S(1)}, u32[]{:S(2)}, u32[]{:S(2)}) collective-permute-start(bf16[8,128,128]{2,1,0:T(8,128)(2,1)S(1)} %get-tuple-element.43), channel_id=1, source_target_pairs={{0,96},{8,104},{16,112},{24,120},{32,0},{40,8},{48,16},{56,24},{64... | collective-permute-start | bytes 786440 | tf_op jit(solution)/shard_map/ppermute | solution.py:291
  128.9 8.3 %collective-permute-start.29 = (bf16[8,128,128]{2,1,0:T(8,128)(2,1)S(1)}, bf16[8,128,128]{2,1,0:T(8,128)(2,1)S(1)}, u32[]{:S(2)}, u32[]{:S(2)}) collective-permute-start(bf16[8,128,128]{2,1,0:T(8,128)(2,1)S(1)} %fusion.10), channel_id=1, source_target_pairs={{0,16},{8,24},{16,0},{24,8},{32,48},{40,56},{48,32},{56,40},{64,80... | collective-permute-start | bytes 786440 | tf_op jit(solution)/shard_map/ppermute | solution.py:287
  129.5 10.1 %collective-permute-start.22 = (bf16[8,128,128]{2,1,0:T(8,128)(2,1)S(1)}, bf16[8,128,128]{2,1,0:T(8,128)(2,1)S(1)}, u32[]{:S(2)}, u32[]{:S(2)}) collective-permute-start(bf16[8,128,128]{2,1,0:T(8,128)(2,1)S(1)} %get-tuple-element.42), channel_id=1, source_target_pairs={{0,64},{8,72},{16,80},{24,88},{32,96},{40,104},{48,112},{56,120},{... | collective-permute-start | bytes 786440 | tf_op jit(solution)/shard_map/ppermute | solution.py:291
  137.3 10.8 %collective-permute-start.30 = (bf16[8,128,128]{2,1,0:T(8,128)(2,1)S(1)}, bf16[8,128,128]{2,1,0:T(8,128)(2,1)S(1)}, u32[]{:S(2)}, u32[]{:S(2)}) collective-permute-start(bf16[8,128,128]{2,1,0:T(8,128)(2,1)S(1)} %fusion.7), channel_id=1, source_target_pairs={{0,128},{128,0},{1,129},{129,1},{2,130},{130,2},{3,131},{131,3},{4... | collective-permute-start | bytes 786440 | tf_op jit(solution)/shard_map/ppermute | solution.py:295
  139.7 12.5 %collective-permute-start.23 = (bf16[8,128,128]{2,1,0:T(8,128)(2,1)S(1)}, bf16[8,128,128]{2,1,0:T(8,128)(2,1)S(1)}, u32[]{:S(2)}, u32[]{:S(2)}) collective-permute-start(bf16[8,128,128]{2,1,0:T(8,128)(2,1)S(1)} %fusion.9), channel_id=1, source_target_pairs={{0,128},{128,0},{1,129},{129,1},{2,130},{130,2},{3,131},{131,3},{4... | collective-permute-start | bytes 786440 | tf_op jit(solution)/shard_map/ppermute | solution.py:295
  (29 other events, 320.6 us)
Sparse Core Ops, SparseCore 0:
  10.4 57.6 all-gather.2
  88.0 53.8 reduce-scatter.1
